TPU v7x, 512 devices: a whole 4x4x16 slice. The times are simulated.
512 devices in a mesh: lon: 32 (over y, x, core), lat: 16 (over z).
Axes of the slice: x: 4, y: 4, z: 16, core: 2. Of those that a mesh axis runs over, the one named last changes fastest.
Arguments:
- ensemble: float32 [3, 512, 256, 256], P(None, 'lon', 'lat'), may hold values from -6 to 6
- bathymetry: int32 [512, 256], P('lon', 'lat'), may hold values from 0 to 15
- obs_cell: int32 [32, 16, 128], P('lon', 'lat'), may hold values from 0 to 767, as said below
- obs_value: float32 [32, 16, 128], P('lon', 'lat'), may hold values from -6 to 6
- obs_weight: float32 [32, 16, 128], P('lon', 'lat'), may hold values from 0.02 to 0.2
Outputs:
- analysis: float32 [3, 512, 256, 256], P(None, 'lon', 'lat')
- transform: float32 [256, 256], replicated
Inputs may be any that keep to these rules, and one draw needn't show every extreme that they name: `obs_cell`: entries index a tile's fields field-major, then longitude, then latitude; every tile observes its first cell (entry 0) and its last cell (entry 767).
All inputs are finite; a program needn't handle non-finite values.
Results may differ from a plain program's by a relative error of at most 0.00022.
Values sent between devices are 32-bit elements; how exact they have to be, the bound alone decides.
No kernel may reach another device: no remote copies, remote signals or barrier semaphores. Data moves between devices by JAX's collectives and lax.ppermute only.
A program may use at most 64 MiB of HBM per device.

v0:
```python
import jax
import jax.numpy as jnp
from jax import lax
from jax.sharding import PartitionSpec as P

STEPS = 2
NS_ITERS = 6
LEVELS = 16


time_step = 0.6
gravity = 1.0
rotation = 0.3


def padded(block, sides, width):
    for axis, dim in sides:
        count = lax.axis_size(axis)
        forward = [(i, i + 1) for i in range(count - 1)]
        forward.append((count - 1, 0))
        backward = [(target, source) for source, target in forward]
        low = lax.ppermute(
            lax.slice_in_dim(block, block.shape[dim] - width, None, axis=dim), axis, forward
        )
        high = lax.ppermute(lax.slice_in_dim(block, 0, width, axis=dim), axis, backward)
        block = jnp.concatenate([low, block, high], axis=dim)
    return block


def advance(fields, depths, coriolis, inside):
    height = fields[0]
    east_flow = fields[1]
    north_flow = fields[2]
    spread_in = 0.5 * (east_flow[2:, 1:-1] - east_flow[:-2, 1:-1]) + 0.5 * (
        north_flow[1:-1, 2:] - north_flow[1:-1, :-2]
    )
    new_height = (height[1:-1, 1:-1] - time_step * depths[1:-1, 1:-1, None] * spread_in) * inside[
        1:-1
    ][None, :, None]
    slope_east = 0.5 * (new_height[2:, 1:-1] - new_height[:-2, 1:-1])
    slope_north = 0.5 * (new_height[1:-1, 2:] - new_height[1:-1, :-2])
    turning = coriolis[2:-2][None, :, None]
    keeper = inside[2:-2][None, :, None]
    new_east = (
        east_flow[2:-2, 2:-2]
        + time_step * (turning * north_flow[2:-2, 2:-2] - gravity * slope_east)
    ) * keeper
    new_north = (
        north_flow[2:-2, 2:-2]
        + time_step * (-turning * east_flow[2:-2, 2:-2] - gravity * slope_north)
    ) * keeper
    return jnp.stack([new_height[1:-1, 1:-1], new_east, new_north])


def transform_of(gram, projected):
    members = gram.shape[0]
    highest = lax.Precision.HIGHEST
    identity = jnp.eye(members, dtype=jnp.float32)
    system = (members - 1.0) * identity + gram
    scaler = jnp.sqrt(jnp.sum(system * system))
    root = system / scaler
    inverse = identity
    for _ in range(NS_ITERS):
        factor = 1.5 * identity - 0.5 * jnp.dot(inverse, root, precision=highest)
        root = jnp.dot(root, factor, precision=highest)
        inverse = jnp.dot(factor, inverse, precision=highest)
    spread = jnp.sqrt((members - 1.0) / scaler) * inverse
    offset = (
        jnp.dot(inverse, jnp.dot(inverse, projected, precision=highest), precision=highest) / scaler
    )
    return spread + offset[:, None]


def products(anomaly_obs, innovation):
    highest = lax.Precision.HIGHEST
    gram_part = jnp.dot(
        anomaly_obs.T, anomaly_obs, precision=highest, preferred_element_type=jnp.float32
    )
    proj_part = jnp.dot(
        innovation, anomaly_obs, precision=highest, preferred_element_type=jnp.float32
    )
    return (gram_part, proj_part)


def local(ensemble, bathymetry, obs_cell, obs_value, obs_weight):
    highest = lax.Precision.HIGHEST
    tile_lon = ensemble.shape[1]
    tile_lat = ensemble.shape[2]
    members = ensemble.shape[3]
    total_lat = tile_lat * lax.axis_size("lat")
    reach = 2 * STEPS
    depths = (bathymetry.astype(jnp.float32) + 1.0) / LEVELS
    depth_ext = padded(depths, (("lon", 0), ("lat", 1)), reach)
    rows = (
        lax.axis_index("lat") * tile_lat - reach + jnp.arange(tile_lat + 2 * reach, dtype=jnp.int32)
    )
    inside = ((rows >= 0) & (rows < total_lat)).astype(jnp.float32)
    coriolis = rotation * (2.0 * (rows.astype(jnp.float32) + 0.5) / total_lat - 1.0)
    depth_ext = depth_ext * inside[None, :]
    state = ensemble
    for _ in range(STEPS):
        extended = padded(state, (("lon", 1), ("lat", 2)), 2)
        cut = reach - 2
        lon_end = depth_ext.shape[0] - cut
        lat_end = depth_ext.shape[1] - cut
        local_depth = depth_ext[cut:lon_end, cut:lat_end]
        local_turn = coriolis[cut:lat_end]
        local_inside = inside[cut:lat_end]
        extended = extended * local_inside[None, None, :, None]
        state = advance(extended, local_depth, local_turn, local_inside)
    average = jnp.mean(state, axis=-1, keepdims=True)
    anomalies = state - average
    cells = obs_cell.reshape(-1)
    predicted = jnp.take(state.reshape(3 * tile_lon * tile_lat, members), cells, axis=0)
    ymean = jnp.mean(predicted, axis=-1)
    weight = obs_weight.reshape(-1)
    anomaly_obs = (predicted - ymean[:, None]) * weight[:, None]
    innovation = (obs_value.reshape(-1) - ymean) * weight
    gram_part, proj_part = products(anomaly_obs, innovation)
    gram, projected = lax.psum((gram_part, proj_part), ("lon", "lat"))
    transform = transform_of(gram, projected)
    moved = jnp.dot(
        anomalies.reshape(-1, members),
        transform,
        precision=highest,
        preferred_element_type=jnp.float32,
    )
    analysis = average + moved.reshape(state.shape)
    return (analysis, transform)


def solution(mesh):
    return jax.shard_map(
        local,
        mesh=mesh,
        in_specs=(
            P(None, "lon", "lat", None),
            P("lon", "lat"),
            P("lon", "lat", None),
            P("lon", "lat", None),
            P("lon", "lat", None),
        ),
        out_specs=(P(None, "lon", "lat", None), P()),
        check_vma=False,
    )
```

profile of v0, /device:TPU:1, one launch (start us, length us, event | category | flops | bytes accessed | tf_op | source)
XLA Modules:
  0.0 660.3 jit_solution(1069049348528086783)
XLA Ops:
  7.2 0.7 add_multiply_fusion
  7.9 4.5 collective-permute-start.4
  12.4 6.2 collective-permute-start.5
  18.6 1.0 fusion.70
  19.6 1.9 collective-permute-start
  21.5 7.0 %collective-permute-start.1 = (f32[3,2,16,256]{3,2,1,0:T(8,128)S(1)}, f32[3,2,16,256]{3,2,1,0:T(8,128)S(1)}, u32[]{:S(2)}, u32[]{:S(2)}) collective-permute-start(f32[3,2,16,256]{3,2,1,0:T(8,128)S(1)} %get-tuple-element.20), channel_id=1, source_target_pairs={{16,0},{32,16},{48,32},{64,48},{80,64},{96,80},{112,96},{128,112},... | collective-permute-start | bytes 294920 | tf_op jit(solution)/shard_map/ppermute | solution.py:25
  28.9 1.9 collective-permute-start.6
  30.8 5.8 collective-permute-start.7
  36.6 1.2 constant_dynamic-update-slice_fusion.1
  37.9 1.9 collective-permute-start.2
  39.8 4.6 collective-permute-start.3
  44.7 1.5 collective-permute-done.3
  47.2 2.8 collective-permute-start.8
  50.0 7.5 %collective-permute-start.9 = (f32[3,2,16,256]{3,2,1,0:T(8,128)S(1)}, f32[3,2,16,256]{3,2,1,0:T(8,128)S(1)}, u32[]{:S(2)}, u32[]{:S(2)}) collective-permute-start(f32[3,2,16,256]{3,2,1,0:T(8,128)S(1)} %get-tuple-element.19), channel_id=1, source_target_pairs={{16,0},{32,16},{48,32},{64,48},{80,64},{96,80},{112,96},{128,112},... | collective-permute-start | bytes 294920 | tf_op jit(solution)/shard_map/ppermute | solution.py:25
  57.6 0.9 collective-permute-done.9
  58.5 1.9 collective-permute-start.10
  60.5 5.3 collective-permute-start.11
  66.1 1.5 collective-permute-done.11
  68.7 0.8 gather_fusion
  69.7 1.2 fusion.44
  71.2 111.3 %psum.15 = f32[256]{0:T(256)S(1)} all-reduce(f32[256]{0:T(256)S(1)} %bitcast.90), channel_id=1, replica_groups=mesh['lon'=32,'lat'=16] {'lon','lat'}, use_global_device_ids=true, to_apply=%region_4.5 | all-reduce | flops 256 | bytes 2048 | tf_op jit(solution)/shard_map/psum | solution.py:120
  182.5 458.5 %all-reduce.2.cloned.1.call-done = f32[256,256]{1,0:T(8,128)} async-done(((f32[256,256]{1,0:T(8,128)}), f32[256,256]{1,0:T(8,128)}) %all-reduce.2.cloned.1.call-update) | async-done | bytes 262160 | tf_op jit(solution)/shard_map/psum | solution.py:120
  641.1 1.7 multiply_reduce_fusion
  643.4 1.3 fusion.5
  645.0 0.4 fusion.53
  645.4 0.4 fusion.4
  646.6 0.4 fusion.3
  647.8 0.4 fusion.2
  648.9 0.4 fusion.1
  649.3 0.4 fusion.81
  650.1 0.4 fusion
  651.7 1.7 convolution_add_fusion
  (65 shorter events, 7.7 us)
Async XLA Ops:
  7.2 633.9 %all-reduce.2.cloned.1.call-start = ((), (), s32[]{:S(2)}) async-start(), calls=%async_computation | async-start | bytes 524288 | tf_op jit(solution)/shard_map/psum | solution.py:120
  7.9 20.9 %collective-permute-start.4 = (f32[4,16]{1,0:T(4,128)S(1)}, f32[4,16]{1,0:T(4,128)S(1)}, u32[]{:S(2)}, u32[]{:S(2)}) collective-permute-start(f32[4,16]{1,0:T(4,128)S(1)} %get-tuple-element.26), channel_id=1, source_target_pairs={{0,16},{16,32},{32,48},{48,64},{64,80},{80,96},{96,112},{112,128},... | collective-permute-start | bytes 776 | tf_op jit(solution)/shard_map/ppermute | solution.py:22
  12.4 16.4 %collective-permute-start.5 = (f32[4,16]{1,0:T(4,128)S(1)}, f32[4,16]{1,0:T(4,128)S(1)}, u32[]{:S(2)}, u32[]{:S(2)}) collective-permute-start(f32[4,16]{1,0:T(4,128)S(1)} %get-tuple-element.27), channel_id=1, source_target_pairs={{16,0},{32,16},{48,32},{64,48},{80,64},{96,80},{112,96},{128,112},... | collective-permute-start | bytes 776 | tf_op jit(solution)/shard_map/ppermute | solution.py:25
  19.6 17.0 %collective-permute-start = (f32[3,2,16,256]{3,2,1,0:T(8,128)S(1)}, f32[3,2,16,256]{3,2,1,0:T(8,128)S(1)}, u32[]{:S(2)}, u32[]{:S(2)}) collective-permute-start(f32[3,2,16,256]{3,2,1,0:T(8,128)S(1)} %get-tuple-element.21), channel_id=1, source_target_pairs={{0,16},{16,32},{32,48},{48,64},{64,80},{80,96},{96,112},{112,128},... | collective-permute-start | bytes 294920 | tf_op jit(solution)/shard_map/ppermute | solution.py:22
  21.5 16.3 %collective-permute-start.1 = (f32[3,2,16,256]{3,2,1,0:T(8,128)S(1)}, f32[3,2,16,256]{3,2,1,0:T(8,128)S(1)}, u32[]{:S(2)}, u32[]{:S(2)}) collective-permute-start(f32[3,2,16,256]{3,2,1,0:T(8,128)S(1)} %get-tuple-element.20), channel_id=1, source_target_pairs={{16,0},{32,16},{48,32},{64,48},{80,64},{96,80},{112,96},{128,112},... | collective-permute-start | bytes 294920 | tf_op jit(solution)/shard_map/ppermute | solution.py:25
  28.9 15.6 %collective-permute-start.6 = (f32[24,4]{1,0:T(8,128)S(1)}, f32[24,4]{1,0:T(8,128)S(1)}, u32[]{:S(2)}, u32[]{:S(2)}) collective-permute-start(f32[24,4]{1,0:T(8,128)S(1)} %get-tuple-element.24), channel_id=1, source_target_pairs={{0,1},{1,2},{2,3},{3,4},{4,5},{5,6},{6,7},{7,8},{8,9},{9,10},{10,1... | collective-permute-start | bytes 1160 | tf_op jit(solution)/shard_map/ppermute | solution.py:22
  30.8 13.6 %collective-permute-start.7 = (f32[24,4]{1,0:T(8,128)S(1)}, f32[24,4]{1,0:T(8,128)S(1)}, u32[]{:S(2)}, u32[]{:S(2)}) collective-permute-start(f32[24,4]{1,0:T(8,128)S(1)} %get-tuple-element.25), channel_id=1, source_target_pairs={{1,0},{2,1},{3,2},{4,3},{5,4},{6,5},{7,6},{8,7},{9,8},{10,9},{11,1... | collective-permute-start | bytes 1160 | tf_op jit(solution)/shard_map/ppermute | solution.py:25
  37.9 6.8 %collective-permute-start.2 = (f32[3,20,2,256]{3,2,1,0:T(2,128)S(1)}, f32[3,20,2,256]{3,2,1,0:T(2,128)S(1)}, u32[]{:S(2)}, u32[]{:S(2)}) collective-permute-start(f32[3,20,2,256]{3,2,1,0:T(2,128)S(1)} %get-tuple-element.14), channel_id=1, source_target_pairs={{0,1},{1,2},{2,3},{3,4},{4,5},{5,6},{6,7},{7,8},{8,9},{9,10},{10,1... | collective-permute-start | bytes 368648 | tf_op jit(solution)/shard_map/ppermute | solution.py:22
  39.8 6.4 collective-permute-start.3
  46.9 10.6 %copy-start.3 = (s32[1,1,128]{2,1,0:T(1,128)S(1)}, s32[1,1,128]{2,1,0:T(1,128)}, u32[]{:S(2)}) copy-start(s32[1,1,128]{2,1,0:T(1,128)} %param.7) | copy-start | bytes 1540
  47.2 10.3 %collective-permute-start.8 = (f32[3,2,16,256]{3,2,1,0:T(8,128)S(1)}, f32[3,2,16,256]{3,2,1,0:T(8,128)S(1)}, u32[]{:S(2)}, u32[]{:S(2)}) collective-permute-start(f32[3,2,16,256]{3,2,1,0:T(8,128)S(1)} %get-tuple-element.18), channel_id=1, source_target_pairs={{0,16},{16,32},{32,48},{48,64},{64,80},{80,96},{96,112},{112,128},... | collective-permute-start | bytes 294920 | tf_op jit(solution)/shard_map/ppermute | solution.py:22
  50.0 8.4 %collective-permute-start.9 = (f32[3,2,16,256]{3,2,1,0:T(8,128)S(1)}, f32[3,2,16,256]{3,2,1,0:T(8,128)S(1)}, u32[]{:S(2)}, u32[]{:S(2)}) collective-permute-start(f32[3,2,16,256]{3,2,1,0:T(8,128)S(1)} %get-tuple-element.19), channel_id=1, source_target_pairs={{16,0},{32,16},{48,32},{64,48},{80,64},{96,80},{112,96},{128,112},... | collective-permute-start | bytes 294920 | tf_op jit(solution)/shard_map/ppermute | solution.py:25
  58.5 7.5 %collective-permute-start.10 = (f32[3,20,2,256]{3,2,1,0:T(2,128)S(1)}, f32[3,20,2,256]{3,2,1,0:T(2,128)S(1)}, u32[]{:S(2)}, u32[]{:S(2)}) collective-permute-start(f32[3,20,2,256]{3,2,1,0:T(2,128)S(1)} %get-tuple-element.12), channel_id=1, source_target_pairs={{0,1},{1,2},{2,3},{3,4},{4,5},{5,6},{6,7},{7,8},{8,9},{9,10},{10,1... | collective-permute-start | bytes 368648 | tf_op jit(solution)/shard_map/ppermute | solution.py:22
  60.5 7.1 %collective-permute-start.11 = (f32[3,20,2,256]{3,2,1,0:T(2,128)S(1)}, f32[3,20,2,256]{3,2,1,0:T(2,128)S(1)}, u32[]{:S(2)}, u32[]{:S(2)}) collective-permute-start(f32[3,20,2,256]{3,2,1,0:T(2,128)S(1)} %get-tuple-element.13), channel_id=1, source_target_pairs={{1,0},{2,1},{3,2},{4,3},{5,4},{6,5},{7,6},{8,7},{9,8},{10,9},{11,1... | collective-permute-start | bytes 368648 | tf_op jit(solution)/shard_map/ppermute | solution.py:25
  68.5 1.2 copy-start.2
  68.5 2.4 copy-start.4
  641.1 4.0 copy-start.1
  651.7 1.7 copy-start
Sparse Core Ops, SparseCore 0:
  182.6 458.3 all-reduce.1
where the time goes:
time: 662 us; the launch traced here: 660 us
  waiting for transfers between devices  463 us (70%)
  blocking collectives  111 us (17%)
  starting transfers between devices  51.2 us (8%)
  between operations  15.4 us (2%)
  matrix products  11.1 us (2%)
    psum x1, waiting for transfers between devices, local(): gram, projected = lax.psum((gram_part, proj_part), ('lon', 'lat'))  459 us
    psum x1, blocking collectives, local(): gram, projected = lax.psum((gram_part, proj_part), ('lon', 'lat'))  111 us
    ppermute x6, starting transfers between devices, padded(): lax.ppermute(lax.slice_in_dim(block, 0, width, axis=dim), axis, backward)  36.2 us
    ppermute x6, starting transfers between devices, padded(): lax.ppermute(lax.slice_in_dim(block, block.shape[dim] - width, None, axis...  15 us
  transfers between devices with their start and end apart: 13, of which 6 were waited for; matrix products, arithmetic and copies ran while one was open for 0% of the time, Pallas kernels for 0%

commit v1 on v0

--- a/solution.py
+++ b/solution.py
@@ -6,25 +6,65 @@
 STEPS = 2
 NS_ITERS = 6
 LEVELS = 16
-
+REACH = 2 * STEPS
 
 time_step = 0.6
 gravity = 1.0
 rotation = 0.3
 
 
-def padded(block, sides, width):
-    for axis, dim in sides:
-        count = lax.axis_size(axis)
-        forward = [(i, i + 1) for i in range(count - 1)]
-        forward.append((count - 1, 0))
-        backward = [(target, source) for source, target in forward]
-        low = lax.ppermute(
-            lax.slice_in_dim(block, block.shape[dim] - width, None, axis=dim), axis, forward
-        )
-        high = lax.ppermute(lax.slice_in_dim(block, 0, width, axis=dim), axis, backward)
-        block = jnp.concatenate([low, block, high], axis=dim)
-    return block
+def shift_up(block, axis, wrap):
+    count = lax.axis_size(axis)
+    pairs = [(i, i + 1) for i in range(count - 1)]
+    if wrap:
+        pairs.append((count - 1, 0))
+    return lax.ppermute(block, axis, pairs)
+
+
+def shift_down(block, axis, wrap):
+    count = lax.axis_size(axis)
+    pairs = [(i + 1, i) for i in range(count - 1)]
+    if wrap:
+        pairs.append((0, count - 1))
+    return lax.ppermute(block, axis, pairs)
+
+
+def with_halo(ensemble, depths):
+    fields, tile_lon, tile_lat, members = ensemble.shape
+
+    def lat_message(start):
+        cells = lax.slice_in_dim(ensemble, start, start + REACH, axis=2)
+        cells = cells.reshape(fields * tile_lon, REACH, members)
+        depth = lax.slice_in_dim(depths, start, start + REACH, axis=1).T
+        depth = jnp.pad(depth, ((0, 0), (0, members - tile_lon)))
+        return jnp.concatenate([cells, depth[None]], axis=0)
+
+    def lat_parts(message):
+        cells = message[: fields * tile_lon].reshape(fields, tile_lon, REACH, members)
+        return cells, message[fields * tile_lon, :, :tile_lon].T
+
+    low, low_depth = lat_parts(shift_up(lat_message(tile_lat - REACH), "lat", False))
+    high, high_depth = lat_parts(shift_down(lat_message(0), "lat", False))
+    state = jnp.concatenate([low, ensemble, high], axis=2)
+    depth = jnp.concatenate([low_depth, depths, high_depth], axis=1)
+    wide = tile_lat + 2 * REACH
+
+    def lon_message(start):
+        cells = lax.slice_in_dim(state, start, start + REACH, axis=1)
+        cells = cells.reshape(fields * REACH, wide, members)
+        strip = lax.slice_in_dim(depth, start, start + REACH, axis=0).T
+        strip = jnp.pad(strip, ((0, 0), (0, members - REACH)))
+        return jnp.concatenate([cells, strip[None]], axis=0)
+
+    def lon_parts(message):
+        cells = message[: fields * REACH].reshape(fields, REACH, wide, members)
+        return cells, message[fields * REACH, :, :REACH].T
+
+    low, low_depth = lon_parts(shift_up(lon_message(tile_lon - REACH), "lon", True))
+    high, high_depth = lon_parts(shift_down(lon_message(0), "lon", True))
+    state = jnp.concatenate([low, state, high], axis=1)
+    depth = jnp.concatenate([low_depth, depth, high_depth], axis=0)
+    return state, depth
 
 
 def advance(fields, depths, coriolis, inside):
@@ -82,32 +122,60 @@
     return (gram_part, proj_part)
 
 
+def reduced(gram, projected):
+    members = gram.shape[0]
+    half = members // 2
+    lon = lax.axis_size("lon")
+    lat = lax.axis_size("lat")
+    packed = jnp.concatenate(
+        [
+            gram[:half, :half],
+            gram[:half, half:],
+            gram[half:, half:],
+            projected.reshape(2, half),
+            jnp.zeros((half - 2, half), jnp.float32),
+        ]
+    )
+    rows = packed.shape[0] // lon
+    pieces = lax.all_to_all(packed.reshape(lon, rows, half), "lon", 0, 0)
+    piece = jnp.sum(pieces, axis=0)
+    pieces = lax.all_to_all(jnp.broadcast_to(piece[None], (lat, rows, half)), "lat", 0, 0)
+    piece = jnp.sum(pieces, axis=0)
+    pieces = lax.all_to_all(jnp.broadcast_to(piece[None], (lon, rows, half)), "lon", 0, 0)
+    packed = pieces.reshape(packed.shape)
+    cross = packed[half : 2 * half]
+    gram = jnp.concatenate(
+        [
+            jnp.concatenate([packed[:half], cross], axis=1),
+            jnp.concatenate([cross.T, packed[2 * half : 3 * half]], axis=1),
+        ]
+    )
+    return gram, packed[3 * half : 3 * half + 2].reshape(members)
+
+
 def local(ensemble, bathymetry, obs_cell, obs_value, obs_weight):
     highest = lax.Precision.HIGHEST
     tile_lon = ensemble.shape[1]
     tile_lat = ensemble.shape[2]
     members = ensemble.shape[3]
     total_lat = tile_lat * lax.axis_size("lat")
-    reach = 2 * STEPS
     depths = (bathymetry.astype(jnp.float32) + 1.0) / LEVELS
-    depth_ext = padded(depths, (("lon", 0), ("lat", 1)), reach)
     rows = (
-        lax.axis_index("lat") * tile_lat - reach + jnp.arange(tile_lat + 2 * reach, dtype=jnp.int32)
+        lax.axis_index("lat") * tile_lat - REACH + jnp.arange(tile_lat + 2 * REACH, dtype=jnp.int32)
     )
     inside = ((rows >= 0) & (rows < total_lat)).astype(jnp.float32)
     coriolis = rotation * (2.0 * (rows.astype(jnp.float32) + 0.5) / total_lat - 1.0)
-    depth_ext = depth_ext * inside[None, :]
-    state = ensemble
-    for _ in range(STEPS):
-        extended = padded(state, (("lon", 1), ("lat", 2)), 2)
-        cut = reach - 2
+    state, depth_ext = with_halo(ensemble, depths)
+    for step in range(STEPS):
+        cut = 2 * step
         lon_end = depth_ext.shape[0] - cut
         lat_end = depth_ext.shape[1] - cut
-        local_depth = depth_ext[cut:lon_end, cut:lat_end]
-        local_turn = coriolis[cut:lat_end]
-        local_inside = inside[cut:lat_end]
-        extended = extended * local_inside[None, None, :, None]
-        state = advance(extended, local_depth, local_turn, local_inside)
+        state = advance(
+            state,
+            depth_ext[cut:lon_end, cut:lat_end],
+            coriolis[cut:lat_end],
+            inside[cut:lat_end],
+        )
     average = jnp.mean(state, axis=-1, keepdims=True)
     anomalies = state - average
     cells = obs_cell.reshape(-1)
@@ -116,8 +184,7 @@
     weight = obs_weight.reshape(-1)
     anomaly_obs = (predicted - ymean[:, None]) * weight[:, None]
     innovation = (obs_value.reshape(-1) - ymean) * weight
-    gram_part, proj_part = products(anomaly_obs, innovation)
-    gram, projected = lax.psum((gram_part, proj_part), ("lon", "lat"))
+    gram, projected = reduced(*products(anomaly_obs, innovation))
     transform = transform_of(gram, projected)
     moved = jnp.dot(
         anomalies.reshape(-1, members),

time: 662 us -> 103 us (0.16)
  waiting for transfers between devices: 463 us -> 12.5 us
  blocking collectives: 111 us -> 46 us
  starting transfers between devices: 51.2 us -> 23.5 us
  between operations: 15.4 us -> 1.96 us
    psum x1 -> x0, waiting for transfers between devices: 459 us -> none  [local(): gram, projected = lax.psum((gram_part, proj_part), ('lon', 'lat'))]
    psum x1 -> x0, blocking collectives: 111 us -> none  [local(): gram, projected = lax.psum((gram_part, proj_part), ('lon', 'lat'))]
    all_to_all x0 -> x2, blocking collectives: none -> 46 us  [the longest x1 24.2 us: reduced(): lax.all_to_all(jnp.broadcast_to(piece[None], (lat, rows, half)), 'lat', 0...]
    ppermute x12 -> x4, starting transfers between devices: 51.2 us -> 17.1 us  [the longest x2 10.5 us: shift_up(): return lax.ppermute(block, axis, pairs)]
    all_to_all x0 -> x1, waiting for transfers between devices: none -> 8.85 us  [reduced(): lax.all_to_all(jnp.broadcast_to(piece[None], (lon, rows, half)), 'lon', 0...]
  transfers between devices with their start and end apart: 13 -> 5, of which waited for: 6 -> 3; matrix products, arithmetic and copies ran while one was open for 0% -> 2% of each run, Pallas kernels for 0% -> 0%
where the time goes in v1:
time: 103 us
  blocking collectives  46 us (45%)
  starting transfers between devices  23.5 us (23%)
  waiting for transfers between devices  12.5 us (12%)
  matrix products  9.42 us (9%)
  local copies, waits for them, and re-layouts  4.86 us (5%)
  other arithmetic  4.63 us (4%)
  between operations  1.96 us (2%)
    all_to_all x1, blocking collectives, reduced(): lax.all_to_all(jnp.broadcast_to(piece[None], (lat, rows, half)), 'lat', 0...  24.2 us
    all_to_all x1, blocking collectives, reduced(): pieces = lax.all_to_all(packed.reshape(lon, rows, half), 'lon', 0, 0)  21.8 us
    ppermute x2, starting transfers between devices, shift_up(): return lax.ppermute(block, axis, pairs)  10.5 us
    all_to_all x1, waiting for transfers between devices, reduced(): lax.all_to_all(jnp.broadcast_to(piece[None], (lon, rows, half)), 'lon', 0...  8.85 us
    ppermute x2, starting transfers between devices, shift_down(): return lax.ppermute(block, axis, pairs)  6.54 us
    all_to_all x1, starting transfers between devices, reduced(): lax.all_to_all(jnp.broadcast_to(piece[None], (lon, rows, half)), 'lon', 0...  6.46 us
    ppermute x2, waiting for transfers between devices, shift_down(): return lax.ppermute(block, axis, pairs)  2.79 us
    dot_general x6, matrix products, transform_of(): factor = 1.5 * identity - 0.5 * jnp.dot(inverse, root, precision=highest)  2.24 us
  transfers between devices with their start and end apart: 5, of which 3 were waited for; matrix products, arithmetic and copies ran while one was open for 2% of the time, Pallas kernels for 0%

profile of v1, /device:TPU:1, one launch (start us, length us, event | category | flops | bytes accessed | tf_op | source)
XLA Modules:
  0.0 102.9 jit_solution(11390718712369200098)
XLA Ops:
  0.6 0.8 copy.35
  1.5 1.2 %fusion.56 = (f32[3,16,4,256]{3,2,1,0:T(4,128)S(1)}, f32[3,16,4,256]{3,2,1,0:T(4,128)S(1)}) fusion(f32[3,16,16,256]{3,2,1,0:T(8,128)} %param.5), kind=kLoop, calls=%fused_computation.121 | loop fusion | bytes 786432 | tf_op jit(solution)/shard_map/slice | solution.py:36
  2.7 1.3 %collective-permute-start.1 = (f32[49,4,256]{2,1,0:T(4,128)S(1)}, f32[49,4,256]{2,1,0:T(4,128)S(1)}, u32[]{:S(2)}, u32[]{:S(2)}) collective-permute-start(f32[49,4,256]{2,1,0:T(4,128)S(1)} %pad_maximum_fusion.8), channel_id=1, source_target_pairs={{1,0},{2,1},{3,2},{4,3},{5,4},{6,5},{7,6},{8,7},{9,8},{10,9},{11,1... | collective-permute-start | bytes 602120 | tf_op jit(solution)/shard_map/ppermute | solution.py:29
  4.1 5.0 %collective-permute-start = (f32[49,4,256]{2,1,0:T(4,128)S(1)}, f32[49,4,256]{2,1,0:T(4,128)S(1)}, u32[]{:S(2)}, u32[]{:S(2)}) collective-permute-start(f32[49,4,256]{2,1,0:T(4,128)S(1)} %pad_maximum_fusion.7), channel_id=1, source_target_pairs={{0,1},{1,2},{2,3},{3,4},{4,5},{5,6},{6,7},{7,8},{8,9},{9,10},{10,1... | collective-permute-start | bytes 602120 | tf_op jit(solution)/shard_map/ppermute | solution.py:21
  9.5 0.7 fusion.49
  10.2 0.7 compare_and_fusion
  10.9 0.8 collective-permute-done
  12.0 5.5 %collective-permute-start.2 = (f32[13,24,256]{2,1,0:T(8,128)S(1)}, f32[13,24,256]{2,1,0:T(8,128)S(1)}, u32[]{:S(2)}, u32[]{:S(2)}) collective-permute-start(f32[13,24,256]{2,1,0:T(8,128)S(1)} %pad_maximum_fusion.2), channel_id=1, source_target_pairs={{0,16},{16,32},{32,48},{48,64},{64,80},{80,96},{96,112},{112,128},... | collective-permute-start | bytes 958472 | tf_op jit(solution)/shard_map/ppermute | solution.py:21
  17.6 5.3 %collective-permute-start.3 = (f32[13,24,256]{2,1,0:T(8,128)S(1)}, f32[13,24,256]{2,1,0:T(8,128)S(1)}, u32[]{:S(2)}, u32[]{:S(2)}) collective-permute-start(f32[13,24,256]{2,1,0:T(8,128)S(1)} %pad_maximum_fusion.3), channel_id=1, source_target_pairs={{16,0},{32,16},{48,32},{64,48},{80,64},{96,80},{112,96},{128,112},... | collective-permute-start | bytes 958472 | tf_op jit(solution)/shard_map/ppermute | solution.py:29
  23.2 2.8 %collective-permute-done.3 = f32[13,24,256]{2,1,0:T(8,128)S(1)} collective-permute-done((f32[13,24,256]{2,1,0:T(8,128)S(1)}, f32[13,24,256]{2,1,0:T(8,128)S(1)}, u32[]{:S(2)}, u32[]{:S(2)}) %collective-permute-start.3) | collective-permute-done | bytes 319520 | tf_op jit(solution)/shard_map/ppermute | solution.py:29
  27.2 0.4 fusion.20
  28.3 0.8 gather_fusion
  29.2 0.5 fusion.44
  30.2 21.8 %all_to_all.15 = f32[32,16,128]{2,1,0:T(8,128)S(1)} all-to-all(f32[32,16,128]{2,1,0:T(8,128)S(1)} %bitcast.141), channel_id=1, replica_groups=mesh['lon'=32,'lat'=16] {'lon'}, dimensions={0} | all-to-all | bytes 524288 | tf_op jit(solution)/shard_map/all_to_all | solution.py:140
  52.1 24.2 %all_to_all.16 = f32[16,16,128]{2,1,0:T(8,128)S(1)} all-to-all(f32[16,16,128]{2,1,0:T(8,128)S(1)} %broadcast_in_dim.55), channel_id=1, replica_groups=mesh['lon'=32,'lat'=16] {'lat'}, dimensions={0} | all-to-all | bytes 262144 | tf_op jit(solution)/shard_map/all_to_all | solution.py:142
  76.3 0.7 broadcast_in_dim.56
  77.0 6.5 %all-to-all-start.2 = ((f32[32,16,128]{2,1,0:T(8,128)}), f32[32,16,128]{2,1,0:T(8,128)S(1)}, u32[]{:S(2)}, u32[]{:S(2)}) async-start(f32[32,16,128]{2,1,0:T(8,128)} %broadcast_in_dim.56), calls=%async_computation.2 | async-start | bytes 524288 | tf_op jit(solution)/shard_map/all_to_all | solution.py:144
  83.5 8.9 %all-to-all-done.2 = f32[32,16,128]{2,1,0:T(8,128)S(1)} async-done(((f32[32,16,128]{2,1,0:T(8,128)}), f32[32,16,128]{2,1,0:T(8,128)S(1)}, u32[]{:S(2)}, u32[]{:S(2)}) %all-to-all-start.2) | async-done | bytes 262176 | tf_op jit(solution)/shard_map/all_to_all | solution.py:144
  92.5 0.7 multiply_reduce_fusion
  94.2 0.4 fusion.54
  94.9 0.4 fusion.4
  95.3 0.4 fusion.61
  95.7 0.4 fusion.60
  96.0 0.4 fusion.3
  97.2 0.4 fusion.2
  97.6 0.4 fusion.65
  98.0 0.4 fusion.64
  98.4 0.4 fusion.1
  99.2 0.4 fusion.66
  99.5 0.4 fusion
  99.9 0.4 fusion.68
  101.2 1.7 %convolution_add_fusion = f32[3,16,16,256]{3,2,1,0:T(8,128)} fusion(f32[3,16,16]{2,1,0:T(8,128)S(1)} %broadcast_multiply_fusion, f32[256,256]{1,0:T(8,128)S(1)} %multiply_add_fusion, f32[1,16,16,256]{3,2,1,0:T(8,128)S(1)} %get-tuple-element.8, f32[1,16,16,256]{3,2,1,0:T(8,128)S(1)} %get-tuple-element.7, f32[1,16,16,256]{3,2,1,0:T(8,128)S(1)} %get-tuple-element.15), kind=kOutput, calls=%fused_computation.2 | convolution fusion | flops 604766208 | bytes 1838080 | tf_op jit(solution)/shard_map/dot_general | solution.py:189
  (79 shorter events, 6.2 us)
Async XLA Ops:
  0.6 11.3 %copy-start = (f32[3,16,16,256]{3,2,1,0:T(8,128)S(1)}, f32[3,16,16,256]{3,2,1,0:T(8,128)}, u32[]{:S(2)}) copy-start(f32[3,16,16,256]{3,2,1,0:T(8,128)} %param.5) | copy-start | bytes 2359300
  2.7 8.2 %collective-permute-start.1 = (f32[49,4,256]{2,1,0:T(4,128)S(1)}, f32[49,4,256]{2,1,0:T(4,128)S(1)}, u32[]{:S(2)}, u32[]{:S(2)}) collective-permute-start(f32[49,4,256]{2,1,0:T(4,128)S(1)} %pad_maximum_fusion.8), channel_id=1, source_target_pairs={{1,0},{2,1},{3,2},{4,3},{5,4},{6,5},{7,6},{8,7},{9,8},{10,9},{11,1... | collective-permute-start | bytes 602120 | tf_op jit(solution)/shard_map/ppermute | solution.py:29
  4.1 7.6 %collective-permute-start = (f32[49,4,256]{2,1,0:T(4,128)S(1)}, f32[49,4,256]{2,1,0:T(4,128)S(1)}, u32[]{:S(2)}, u32[]{:S(2)}) collective-permute-start(f32[49,4,256]{2,1,0:T(4,128)S(1)} %pad_maximum_fusion.7), channel_id=1, source_target_pairs={{0,1},{1,2},{2,3},{3,4},{4,5},{5,6},{6,7},{7,8},{8,9},{9,10},{10,1... | collective-permute-start | bytes 602120 | tf_op jit(solution)/shard_map/ppermute | solution.py:21
  12.0 10.9 %collective-permute-start.2 = (f32[13,24,256]{2,1,0:T(8,128)S(1)}, f32[13,24,256]{2,1,0:T(8,128)S(1)}, u32[]{:S(2)}, u32[]{:S(2)}) collective-permute-start(f32[13,24,256]{2,1,0:T(8,128)S(1)} %pad_maximum_fusion.2), channel_id=1, source_target_pairs={{0,16},{16,32},{32,48},{48,64},{64,80},{80,96},{96,112},{112,128},... | collective-permute-start | bytes 958472 | tf_op jit(solution)/shard_map/ppermute | solution.py:21
  17.6 8.3 %collective-permute-start.3 = (f32[13,24,256]{2,1,0:T(8,128)S(1)}, f32[13,24,256]{2,1,0:T(8,128)S(1)}, u32[]{:S(2)}, u32[]{:S(2)}) collective-permute-start(f32[13,24,256]{2,1,0:T(8,128)S(1)} %pad_maximum_fusion.3), channel_id=1, source_target_pairs={{16,0},{32,16},{48,32},{64,48},{80,64},{96,80},{112,96},{128,112},... | collective-permute-start | bytes 958472 | tf_op jit(solution)/shard_map/ppermute | solution.py:29
  28.1 1.2 %copy-start.2 = (f32[1,1,128]{2,1,0:T(1,128)S(1)}, f32[1,1,128]{2,1,0:T(1,128)}, u32[]{:S(2)}) copy-start(f32[1,1,128]{2,1,0:T(1,128)} %param.9) | copy-start | bytes 1540
  28.1 1.7 %copy-start.3 = (f32[1,1,128]{2,1,0:T(1,128)S(1)}, f32[1,1,128]{2,1,0:T(1,128)}, u32[]{:S(2)}) copy-start(f32[1,1,128]{2,1,0:T(1,128)} %param.8) | copy-start | bytes 1540
  77.0 15.3 %all-to-all-start.2 = ((f32[32,16,128]{2,1,0:T(8,128)}), f32[32,16,128]{2,1,0:T(8,128)S(1)}, u32[]{:S(2)}, u32[]{:S(2)}) async-start(f32[32,16,128]{2,1,0:T(8,128)} %broadcast_in_dim.56), calls=%async_computation.2 | async-start | bytes 524288 | tf_op jit(solution)/shard_map/all_to_all | solution.py:144
  101.2 1.7 %copy-start.1 = (f32[256,256]{1,0:T(8,128)}, f32[256,256]{1,0:T(8,128)S(1)}, u32[]{:S(2)}) copy-start(f32[256,256]{1,0:T(8,128)S(1)} %multiply_add_fusion) | copy-start | bytes 786436

commit v2 on v1

--- a/solution.py
+++ b/solution.py
@@ -1,12 +1,17 @@
+import functools
+
 import jax
 import jax.numpy as jnp
 from jax import lax
+from jax.experimental import pallas as pl
+from jax.experimental.pallas import tpu as pltpu
 from jax.sharding import PartitionSpec as P
 
 STEPS = 2
 NS_ITERS = 6
 LEVELS = 16
 REACH = 2 * STEPS
+VMEM_BYTES = 24 * 1024 * 1024
 
 time_step = 0.6
 gravity = 1.0
@@ -92,23 +97,82 @@
     return jnp.stack([new_height[1:-1, 1:-1], new_east, new_north])
 
 
-def transform_of(gram, projected):
-    members = gram.shape[0]
-    highest = lax.Precision.HIGHEST
-    identity = jnp.eye(members, dtype=jnp.float32)
-    system = (members - 1.0) * identity + gram
-    scaler = jnp.sqrt(jnp.sum(system * system))
-    root = system / scaler
-    inverse = identity
-    for _ in range(NS_ITERS):
-        factor = 1.5 * identity - 0.5 * jnp.dot(inverse, root, precision=highest)
-        root = jnp.dot(root, factor, precision=highest)
-        inverse = jnp.dot(factor, inverse, precision=highest)
-    spread = jnp.sqrt((members - 1.0) / scaler) * inverse
-    offset = (
-        jnp.dot(inverse, jnp.dot(inverse, projected, precision=highest), precision=highest) / scaler
-    )
-    return spread + offset[:, None]
+def halves(value):
+    high = value.astype(jnp.bfloat16)
+    return high, (value - high.astype(jnp.float32)).astype(jnp.bfloat16)
+
+
+def dot3(left, right):
+    left_high, left_low = left
+    right_high, right_low = right
+    dot = functools.partial(jnp.dot, preferred_element_type=jnp.float32)
+    return dot(left_high, right_high) + (dot(left_high, right_low) + dot(left_low, right_high))
+
+
+def finish_kernel(packed_ref, state_ref, analysis_ref, transform_ref):
+    half = packed_ref.shape[1]
+    members = 2 * half
+    square = packed_ref[:half]
+    cross = packed_ref[half : 2 * half]
+    diagonal = packed_ref[2 * half : 2 * half + 1]
+    turned = square.T
+    row = lax.broadcasted_iota(jnp.int32, (half, half), 0)
+    column = lax.broadcasted_iota(jnp.int32, (half, half), 1)
+    first = jnp.where(row <= column, square, turned)
+    last = jnp.where(row == column, diagonal, jnp.where(row < column, turned, square))
+    gram = jnp.concatenate(
+        [jnp.concatenate([first, cross], axis=1), jnp.concatenate([cross.T, last], axis=1)]
+    )
+    row = lax.broadcasted_iota(jnp.int32, (members, members), 0)
+    column = lax.broadcasted_iota(jnp.int32, (members, members), 1)
+    on_diagonal = row == column
+    system = gram + jnp.where(on_diagonal, members - 1.0, 0.0)
+    scaler = jnp.sqrt(
+        jnp.sum(jnp.sum(system * system, axis=0, keepdims=True), axis=1, keepdims=True)
+    )
+    root = system * (1.0 / scaler)
+    triple = jnp.where(on_diagonal, 1.5, 0.0)
+
+    inverse = triple - 0.5 * root
+    factor = halves(inverse)
+    root = halves(dot3(halves(root), factor))
+    inverse = factor
+    for step in range(1, NS_ITERS):
+        factor = halves(triple - 0.5 * dot3(inverse, root))
+        if step < NS_ITERS - 1:
+            root = halves(dot3(root, factor))
+            inverse = halves(dot3(factor, inverse))
+        else:
+            inverse = dot3(factor, inverse)
+    projected = jnp.concatenate(
+        [packed_ref[2 * half + 1 : 2 * half + 2], packed_ref[2 * half + 2 : 2 * half + 3]], axis=1
+    )
+    once = jnp.sum(inverse * projected, axis=1, keepdims=True)
+    once = jnp.sum(jnp.where(on_diagonal, once, 0.0), axis=0, keepdims=True)
+    offset = jnp.sum(inverse * once, axis=1, keepdims=True) / scaler
+    transform = jnp.sqrt((members - 1.0) / scaler) * inverse + offset
+    transform_ref[...] = transform
+    transform = halves(transform)
+    block = 256
+    for start in range(0, state_ref.shape[0], block):
+        state = state_ref[start : start + block]
+        average = jnp.sum(state, axis=1, keepdims=True) * (1.0 / members)
+        analysis_ref[start : start + block] = average + dot3(halves(state - average), transform)
+
+
+def finish(packed, state):
+    vmem = pl.BlockSpec(memory_space=pltpu.VMEM)
+    members = state.shape[1]
+    return pl.pallas_call(
+        finish_kernel,
+        out_shape=(
+            jax.ShapeDtypeStruct(state.shape, jnp.float32),
+            jax.ShapeDtypeStruct((members, members), jnp.float32),
+        ),
+        in_specs=[vmem, vmem],
+        out_specs=(vmem, vmem),
+        compiler_params=pltpu.CompilerParams(vmem_limit_bytes=VMEM_BYTES),
+    )(packed, state)
 
 
 def products(anomaly_obs, innovation):
@@ -127,34 +191,29 @@
     half = members // 2
     lon = lax.axis_size("lon")
     lat = lax.axis_size("lat")
+    first = gram[:half, :half]
+    last = gram[half:, half:]
+    line = jnp.arange(half)
+    upper = line[:, None] <= line[None, :]
     packed = jnp.concatenate(
         [
-            gram[:half, :half],
+            jnp.where(upper, first, last),
             gram[:half, half:],
-            gram[half:, half:],
+            jnp.sum(jnp.where(line[:, None] == line[None, :], last, 0.0), axis=0)[None],
             projected.reshape(2, half),
-            jnp.zeros((half - 2, half), jnp.float32),
+            jnp.zeros((lon - 3, half), jnp.float32),
         ]
     )
-    rows = packed.shape[0] // lon
-    pieces = lax.all_to_all(packed.reshape(lon, rows, half), "lon", 0, 0)
+    width = packed.size // lon
+    pieces = lax.all_to_all(packed.reshape(lon, 1, width), "lon", 0, 0)
     piece = jnp.sum(pieces, axis=0)
-    pieces = lax.all_to_all(jnp.broadcast_to(piece[None], (lat, rows, half)), "lat", 0, 0)
+    pieces = lax.all_to_all(jnp.broadcast_to(piece[None], (lat, 1, width)), "lat", 0, 0)
     piece = jnp.sum(pieces, axis=0)
-    pieces = lax.all_to_all(jnp.broadcast_to(piece[None], (lon, rows, half)), "lon", 0, 0)
-    packed = pieces.reshape(packed.shape)
-    cross = packed[half : 2 * half]
-    gram = jnp.concatenate(
-        [
-            jnp.concatenate([packed[:half], cross], axis=1),
-            jnp.concatenate([cross.T, packed[2 * half : 3 * half]], axis=1),
-        ]
-    )
-    return gram, packed[3 * half : 3 * half + 2].reshape(members)
+    pieces = lax.all_to_all(jnp.broadcast_to(piece[None], (lon, 1, width)), "lon", 0, 0)
+    return pieces.reshape(packed.shape)
 
 
 def local(ensemble, bathymetry, obs_cell, obs_value, obs_weight):
-    highest = lax.Precision.HIGHEST
     tile_lon = ensemble.shape[1]
     tile_lat = ensemble.shape[2]
     members = ensemble.shape[3]
@@ -176,24 +235,17 @@
             coriolis[cut:lat_end],
             inside[cut:lat_end],
         )
-    average = jnp.mean(state, axis=-1, keepdims=True)
-    anomalies = state - average
+    shape = state.shape
+    state = state.reshape(3 * tile_lon * tile_lat, members)
     cells = obs_cell.reshape(-1)
-    predicted = jnp.take(state.reshape(3 * tile_lon * tile_lat, members), cells, axis=0)
+    predicted = jnp.take(state, cells, axis=0)
     ymean = jnp.mean(predicted, axis=-1)
     weight = obs_weight.reshape(-1)
     anomaly_obs = (predicted - ymean[:, None]) * weight[:, None]
     innovation = (obs_value.reshape(-1) - ymean) * weight
-    gram, projected = reduced(*products(anomaly_obs, innovation))
-    transform = transform_of(gram, projected)
-    moved = jnp.dot(
-        anomalies.reshape(-1, members),
-        transform,
-        precision=highest,
-        preferred_element_type=jnp.float32,
-    )
-    analysis = average + moved.reshape(state.shape)
-    return (analysis, transform)
+    packed = reduced(*products(anomaly_obs, innovation))
+    analysis, transform = finish(packed, state)
+    return (analysis.reshape(shape), transform)
 
 
 def solution(mesh):

time: 103 us -> 93.7 us (0.910)
  blocking collectives: 46 us -> 57.4 us
  waiting for transfers between devices: 12.5 us -> 3.7 us
  matrix products: 9.42 us -> 0.78 us
  starting transfers between devices: 23.5 us -> 17.1 us
  Pallas kernels: 0 us -> 5.37 us
    all_to_all x2 -> x3, blocking collectives: 46 us -> 57.4 us  [the longest x1 23.8 us: reduced(): lax.all_to_all(jnp.broadcast_to(piece[None], (lat, 1, width)), 'lat', 0, 0)]
    all_to_all x1 -> x0, waiting for transfers between devices: 8.85 us -> none  [reduced(): lax.all_to_all(jnp.broadcast_to(piece[None], (lon, rows, half)), 'lon', 0...]
    dot_general x20 -> x0, matrix products: 8.63 us -> none  [the longest x6 2.24 us: transform_of(): factor = 1.5 * identity - 0.5 * jnp.dot(inverse, root, precision=highest)]
    all_to_all x1 -> x0, starting transfers between devices: 6.46 us -> none  [reduced(): lax.all_to_all(jnp.broadcast_to(piece[None], (lon, rows, half)), 'lon', 0...]
    pallas_call x0 -> x1, Pallas kernels: none -> 5.37 us  [finish(): pl.pallas_call(finish_kernel, out_shape=(jax.ShapeDtypeStruct(state.shape...]
  transfers between devices with their start and end apart: 5 -> 4, of which waited for: 3 -> 2; matrix products, arithmetic and copies ran while one was open for 2% -> 2% of each run, Pallas kernels for 0% -> 0%
where the time goes in v2:
time: 93.7 us; the launch traced here: 93.3 us
  blocking collectives  57.4 us (61%)
  starting transfers between devices  17.1 us (18%)
  Pallas kernels  5.37 us (6%)
  local copies, waits for them, and re-layouts  4.22 us (5%)
  other arithmetic  3.73 us (4%)
  waiting for transfers between devices  3.7 us (4%)
    all_to_all x1, blocking collectives, reduced(): lax.all_to_all(jnp.broadcast_to(piece[None], (lat, 1, width)), 'lat', 0, 0)  23.8 us
    all_to_all x1, blocking collectives, reduced(): pieces = lax.all_to_all(packed.reshape(lon, 1, width), 'lon', 0, 0)  20.7 us
    all_to_all x1, blocking collectives, reduced(): lax.all_to_all(jnp.broadcast_to(piece[None], (lon, 1, width)), 'lon', 0, 0)  12.9 us
    ppermute x2, starting transfers between devices, shift_up(): return lax.ppermute(block, axis, pairs)  10.5 us
    ppermute x2, starting transfers between devices, shift_down(): return lax.ppermute(block, axis, pairs)  6.54 us
    pallas_call x1, Pallas kernels, finish(): pl.pallas_call(finish_kernel, out_shape=(jax.ShapeDtypeStruct(state.shape...  5.37 us
    ppermute x2, waiting for transfers between devices, shift_down(): return lax.ppermute(block, axis, pairs)  2.79 us
  transfers between devices with their start and end apart: 4, of which 2 were waited for; matrix products, arithmetic and copies ran while one was open for 2% of the time, Pallas kernels for 0%

profile of v2, /device:TPU:1, one launch (start us, length us, event | category | flops | bytes accessed | tf_op | source)
XLA Modules:
  0.0 93.3 jit_solution(16057811359668846212)
XLA Ops:
  0.6 0.8 copy.31
  1.5 1.2 %fusion.44 = (f32[3,16,4,256]{3,2,1,0:T(4,128)S(1)}, f32[3,16,4,256]{3,2,1,0:T(4,128)S(1)}) fusion(f32[3,16,16,256]{3,2,1,0:T(8,128)} %param.5), kind=kLoop, calls=%fused_computation.97 | loop fusion | bytes 786432 | tf_op jit(solution)/shard_map/slice | solution.py:41
  2.7 1.3 %collective-permute-start.1 = (f32[49,4,256]{2,1,0:T(4,128)S(1)}, f32[49,4,256]{2,1,0:T(4,128)S(1)}, u32[]{:S(2)}, u32[]{:S(2)}) collective-permute-start(f32[49,4,256]{2,1,0:T(4,128)S(1)} %pad_maximum_fusion.8), channel_id=1, source_target_pairs={{1,0},{2,1},{3,2},{4,3},{5,4},{6,5},{7,6},{8,7},{9,8},{10,9},{11,1... | collective-permute-start | bytes 602120 | tf_op jit(solution)/shard_map/ppermute | solution.py:34
  4.1 5.0 %collective-permute-start = (f32[49,4,256]{2,1,0:T(4,128)S(1)}, f32[49,4,256]{2,1,0:T(4,128)S(1)}, u32[]{:S(2)}, u32[]{:S(2)}) collective-permute-start(f32[49,4,256]{2,1,0:T(4,128)S(1)} %pad_maximum_fusion.7), channel_id=1, source_target_pairs={{0,1},{1,2},{2,3},{3,4},{4,5},{5,6},{6,7},{7,8},{8,9},{9,10},{10,1... | collective-permute-start | bytes 602120 | tf_op jit(solution)/shard_map/ppermute | solution.py:26
  9.5 0.7 fusion.39
  10.2 0.7 compare_and_fusion
  10.8 0.9 collective-permute-done
  11.9 0.1 pad_maximum_fusion.6
  12.0 5.5 %collective-permute-start.2 = (f32[13,24,256]{2,1,0:T(8,128)S(1)}, f32[13,24,256]{2,1,0:T(8,128)S(1)}, u32[]{:S(2)}, u32[]{:S(2)}) collective-permute-start(f32[13,24,256]{2,1,0:T(8,128)S(1)} %pad_maximum_fusion.2), channel_id=1, source_target_pairs={{0,16},{16,32},{32,48},{48,64},{64,80},{80,96},{96,112},{112,128},... | collective-permute-start | bytes 958472 | tf_op jit(solution)/shard_map/ppermute | solution.py:26
  17.6 5.3 %collective-permute-start.3 = (f32[13,24,256]{2,1,0:T(8,128)S(1)}, f32[13,24,256]{2,1,0:T(8,128)S(1)}, u32[]{:S(2)}, u32[]{:S(2)}) collective-permute-start(f32[13,24,256]{2,1,0:T(8,128)S(1)} %pad_maximum_fusion.3), channel_id=1, source_target_pairs={{16,0},{32,16},{48,32},{64,48},{80,64},{96,80},{112,96},{128,112},... | collective-permute-start | bytes 958472 | tf_op jit(solution)/shard_map/ppermute | solution.py:34
  23.0 0.1 copy.32
  23.1 0.1 copy.34
  23.2 2.8 %collective-permute-done.3 = f32[13,24,256]{2,1,0:T(8,128)S(1)} collective-permute-done((f32[13,24,256]{2,1,0:T(8,128)S(1)}, f32[13,24,256]{2,1,0:T(8,128)S(1)}, u32[]{:S(2)}, u32[]{:S(2)}) %collective-permute-start.3) | collective-permute-done | bytes 319520 | tf_op jit(solution)/shard_map/ppermute | solution.py:34
  26.0 0.1 copy.35
  26.3 0.1 copy.36
  26.5 0.2 pad_maximum_fusion
  26.7 0.1 slice_bitcast_fusion.2
  26.9 0.1 copy.37
  27.0 0.2 fusion.3
  27.2 0.4 fusion.13
  27.6 0.2 fusion.17
  27.8 0.2 fusion.29
  28.1 0.8 gather_fusion
  28.9 0.2 select_reduce_fusion
  29.1 0.5 fusion.34
  29.7 0.3 fusion.30
  30.0 0.2 concatenate.35
  30.2 20.7 %all_to_all.15 = f32[32,1,1152]{2,1,0:T(1,128)S(1)} all-to-all(f32[32,1,1152]{2,1,0:T(1,128)S(1)} %bitcast.97), channel_id=1, replica_groups=mesh['lon'=32,'lat'=16] {'lon'}, dimensions={0} | all-to-all | bytes 294912 | tf_op jit(solution)/shard_map/all_to_all | solution.py:208
  50.9 0.1 reduce_sum.38
  51.0 23.8 %all_to_all.16 = f32[16,1,1152]{2,1,0:T(1,128)S(1)} all-to-all(f32[16,1,1152]{2,1,0:T(1,128)S(1)} %broadcast_in_dim.66), channel_id=1, replica_groups=mesh['lon'=32,'lat'=16] {'lat'}, dimensions={0} | all-to-all | bytes 147456 | tf_op jit(solution)/shard_map/all_to_all | solution.py:210
  75.0 12.9 %all_to_all.17 = f32[32,1,1152]{2,1,0:T(1,128)S(1)} all-to-all(f32[32,1,1152]{2,1,0:T(1,128)S(1)} %broadcast_in_dim.67), channel_id=1, replica_groups=mesh['lon'=32,'lat'=16] {'lon'}, dimensions={0} | all-to-all | bytes 294912 | tf_op jit(solution)/shard_map/all_to_all | solution.py:212
  87.9 5.4 %shard_map.68 = (f32[768,256]{1,0:T(8,128)}, f32[256,256]{1,0:T(8,128)}) custom-call(f32[288,128]{1,0:T(8,128)S(1)} %bitcast.86, f32[768,256]{1,0:T(8,128)S(1)} %bitcast.85), custom_call_target="tpu_custom_call" | custom-call | tf_op jit(solution)/shard_map/pallas_call | solution.py:166
  (48 shorter events, 1.4 us)
Async XLA Ops:
  0.6 11.3 %copy-start = (f32[3,16,16,256]{3,2,1,0:T(8,128)S(1)}, f32[3,16,16,256]{3,2,1,0:T(8,128)}, u32[]{:S(2)}) copy-start(f32[3,16,16,256]{3,2,1,0:T(8,128)} %param.5) | copy-start | bytes 2359300
  2.7 8.1 %collective-permute-start.1 = (f32[49,4,256]{2,1,0:T(4,128)S(1)}, f32[49,4,256]{2,1,0:T(4,128)S(1)}, u32[]{:S(2)}, u32[]{:S(2)}) collective-permute-start(f32[49,4,256]{2,1,0:T(4,128)S(1)} %pad_maximum_fusion.8), channel_id=1, source_target_pairs={{1,0},{2,1},{3,2},{4,3},{5,4},{6,5},{7,6},{8,7},{9,8},{10,9},{11,1... | collective-permute-start | bytes 602120 | tf_op jit(solution)/shard_map/ppermute | solution.py:34
  4.1 7.6 %collective-permute-start = (f32[49,4,256]{2,1,0:T(4,128)S(1)}, f32[49,4,256]{2,1,0:T(4,128)S(1)}, u32[]{:S(2)}, u32[]{:S(2)}) collective-permute-start(f32[49,4,256]{2,1,0:T(4,128)S(1)} %pad_maximum_fusion.7), channel_id=1, source_target_pairs={{0,1},{1,2},{2,3},{3,4},{4,5},{5,6},{6,7},{7,8},{8,9},{9,10},{10,1... | collective-permute-start | bytes 602120 | tf_op jit(solution)/shard_map/ppermute | solution.py:26
  12.0 10.9 %collective-permute-start.2 = (f32[13,24,256]{2,1,0:T(8,128)S(1)}, f32[13,24,256]{2,1,0:T(8,128)S(1)}, u32[]{:S(2)}, u32[]{:S(2)}) collective-permute-start(f32[13,24,256]{2,1,0:T(8,128)S(1)} %pad_maximum_fusion.2), channel_id=1, source_target_pairs={{0,16},{16,32},{32,48},{48,64},{64,80},{80,96},{96,112},{112,128},... | collective-permute-start | bytes 958472 | tf_op jit(solution)/shard_map/ppermute | solution.py:26
  17.6 8.3 %collective-permute-start.3 = (f32[13,24,256]{2,1,0:T(8,128)S(1)}, f32[13,24,256]{2,1,0:T(8,128)S(1)}, u32[]{:S(2)}, u32[]{:S(2)}) collective-permute-start(f32[13,24,256]{2,1,0:T(8,128)S(1)} %pad_maximum_fusion.3), channel_id=1, source_target_pairs={{16,0},{32,16},{48,32},{64,48},{80,64},{96,80},{112,96},{128,112},... | collective-permute-start | bytes 958472 | tf_op jit(solution)/shard_map/ppermute | solution.py:34
  28.1 1.0 %copy-start.1 = (f32[1,1,128]{2,1,0:T(1,128)S(1)}, f32[1,1,128]{2,1,0:T(1,128)}, u32[]{:S(2)}) copy-start(f32[1,1,128]{2,1,0:T(1,128)} %param.9) | copy-start | bytes 1540
  28.1 1.6 %copy-start.2 = (f32[1,1,128]{2,1,0:T(1,128)S(1)}, f32[1,1,128]{2,1,0:T(1,128)}, u32[]{:S(2)}) copy-start(f32[1,1,128]{2,1,0:T(1,128)} %param.8) | copy-start | bytes 1540

commit v3 on v2

--- a/solution.py
+++ b/solution.py
@@ -18,29 +18,28 @@
 rotation = 0.3
 
 
-def shift_up(block, axis, wrap):
+def swaps(edge, axis, wrap):
     count = lax.axis_size(axis)
-    pairs = [(i, i + 1) for i in range(count - 1)]
+    even = lax.axis_index(axis) % 2 == 0
+    across = [(i, i + 1) for i in range(1, count - 1, 2)]
     if wrap:
-        pairs.append((count - 1, 0))
-    return lax.ppermute(block, axis, pairs)
-
-
-def shift_down(block, axis, wrap):
-    count = lax.axis_size(axis)
-    pairs = [(i + 1, i) for i in range(count - 1)]
-    if wrap:
-        pairs.append((0, count - 1))
-    return lax.ppermute(block, axis, pairs)
+        across.append((count - 1, 0))
+    within = [(i, i + 1) for i in range(0, count, 2)]
+    first = lax.ppermute(edge(~even), axis, across + [(j, i) for i, j in across])
+    second = lax.ppermute(edge(even), axis, within + [(j, i) for i, j in within])
+    low = jnp.where(even, first, second)
+    high = jnp.where(even, second, first)
+    return low, high
 
 
 def with_halo(ensemble, depths):
     fields, tile_lon, tile_lat, members = ensemble.shape
 
-    def lat_message(start):
-        cells = lax.slice_in_dim(ensemble, start, start + REACH, axis=2)
+    def lat_message(upper):
+        start = jnp.where(upper, tile_lat - REACH, 0)
+        cells = lax.dynamic_slice_in_dim(ensemble, start, REACH, axis=2)
         cells = cells.reshape(fields * tile_lon, REACH, members)
-        depth = lax.slice_in_dim(depths, start, start + REACH, axis=1).T
+        depth = lax.dynamic_slice_in_dim(depths, start, REACH, axis=1).T
         depth = jnp.pad(depth, ((0, 0), (0, members - tile_lon)))
         return jnp.concatenate([cells, depth[None]], axis=0)
 
@@ -48,16 +47,18 @@
         cells = message[: fields * tile_lon].reshape(fields, tile_lon, REACH, members)
         return cells, message[fields * tile_lon, :, :tile_lon].T
 
-    low, low_depth = lat_parts(shift_up(lat_message(tile_lat - REACH), "lat", False))
-    high, high_depth = lat_parts(shift_down(lat_message(0), "lat", False))
+    low, high = swaps(lat_message, "lat", False)
+    low, low_depth = lat_parts(low)
+    high, high_depth = lat_parts(high)
     state = jnp.concatenate([low, ensemble, high], axis=2)
     depth = jnp.concatenate([low_depth, depths, high_depth], axis=1)
     wide = tile_lat + 2 * REACH
 
-    def lon_message(start):
-        cells = lax.slice_in_dim(state, start, start + REACH, axis=1)
+    def lon_message(upper):
+        start = jnp.where(upper, tile_lon - REACH, 0)
+        cells = lax.dynamic_slice_in_dim(state, start, REACH, axis=1)
         cells = cells.reshape(fields * REACH, wide, members)
-        strip = lax.slice_in_dim(depth, start, start + REACH, axis=0).T
+        strip = lax.dynamic_slice_in_dim(depth, start, REACH, axis=0).T
         strip = jnp.pad(strip, ((0, 0), (0, members - REACH)))
         return jnp.concatenate([cells, strip[None]], axis=0)
 
@@ -65,8 +66,9 @@
         cells = message[: fields * REACH].reshape(fields, REACH, wide, members)
         return cells, message[fields * REACH, :, :REACH].T
 
-    low, low_depth = lon_parts(shift_up(lon_message(tile_lon - REACH), "lon", True))
-    high, high_depth = lon_parts(shift_down(lon_message(0), "lon", True))
+    low, high = swaps(lon_message, "lon", True)
+    low, low_depth = lon_parts(low)
+    high, high_depth = lon_parts(high)
     state = jnp.concatenate([low, state, high], axis=1)
     depth = jnp.concatenate([low_depth, depth, high_depth], axis=0)
     return state, depth

time: 93.7 us -> 94.8 us (1.012)
  waiting for transfers between devices: 3.7 us -> 7.2 us
  starting transfers between devices: 17.1 us -> 15.9 us
  blocking collectives: 57.4 us -> 56.3 us
    all_to_all x1, blocking collectives: 20.7 us -> 13.5 us  [reduced(): pieces = lax.all_to_all(packed.reshape(lon, 1, width), 'lon', 0, 0)]
    all_to_all x1, blocking collectives: 23.8 us -> 29.8 us  [reduced(): lax.all_to_all(jnp.broadcast_to(piece[None], (lat, 1, width)), 'lat', 0, 0)]
    ppermute x4, waiting for transfers between devices: 3.7 us -> 7.2 us  [the longest x2 6.58 us: swaps(): lax.ppermute(edge(~even), axis, across + [(j, i) for i, j in across])]
    slice x5 -> x0, local copies, waits for them, and re-layouts: 1.35 us -> none  [the longest x1 1.19 us: lat_message(): cells = lax.slice_in_dim(ensemble, start, start + REACH, axis=2)]
    ppermute x4, starting transfers between devices: 17.1 us -> 15.9 us  [the longest x2 13.3 us: swaps(): lax.ppermute(edge(even), axis, within + [(j, i) for i, j in within])]
    dynamic_slice x0 -> x2, local copies, waits for them, and re-layouts: none -> 1.23 us  [the longest x1 1.19 us: lat_message(): cells = lax.dynamic_slice_in_dim(ensemble, start, REACH, axis=2)]
where the time goes in v3:
time: 94.8 us; the launch traced here: 94.4 us
  blocking collectives  56.3 us (59%)
  starting transfers between devices  15.9 us (17%)
  waiting for transfers between devices  7.2 us (8%)
  Pallas kernels  5.37 us (6%)
  other arithmetic  3.94 us (4%)
  local copies, waits for them, and re-layouts  3.93 us (4%)
  between operations  1.02 us (1%)
    all_to_all x1, blocking collectives, reduced(): lax.all_to_all(jnp.broadcast_to(piece[None], (lat, 1, width)), 'lat', 0, 0)  29.8 us
    all_to_all x1, blocking collectives, reduced(): pieces = lax.all_to_all(packed.reshape(lon, 1, width), 'lon', 0, 0)  13.5 us
    ppermute x2, starting transfers between devices, swaps(): lax.ppermute(edge(even), axis, within + [(j, i) for i, j in within])  13.3 us
    all_to_all x1, blocking collectives, reduced(): lax.all_to_all(jnp.broadcast_to(piece[None], (lon, 1, width)), 'lon', 0, 0)  12.9 us
    ppermute x2, waiting for transfers between devices, swaps(): lax.ppermute(edge(~even), axis, across + [(j, i) for i, j in across])  6.58 us
    pallas_call x1, Pallas kernels, finish(): pl.pallas_call(finish_kernel, out_shape=(jax.ShapeDtypeStruct(state.shape...  5.37 us
    ppermute x2, starting transfers between devices, swaps(): lax.ppermute(edge(~even), axis, across + [(j, i) for i, j in across])  2.59 us
  transfers between devices with their start and end apart: 4, of which 2 were waited for; matrix products, arithmetic and copies ran while one was open for 2% of the time, Pallas kernels for 0%

profile of v3, /device:TPU:1, one launch (start us, length us, event | category | flops | bytes accessed | tf_op | source)
XLA Modules:
  0.0 94.4 jit_solution(9393046770521052956)
XLA Ops:
  0.7 0.8 copy.36
  1.5 1.2 %constant_dynamic-slice_fusion.3 = (f32[3,16,4,256]{3,2,1,0:T(4,128)S(1)}, f32[3,16,4,256]{3,2,1,0:T(4,128)S(1)}) fusion(f32[3,16,16,256]{3,2,1,0:T(8,128)} %param.5, s32[]{:T(128)S(6)} %select_n.91, s32[]{:T(128)S(6)} %select_n.92), kind=kLoop, calls=%fused_computation.92 | loop fusion | bytes 786440 | tf_op jit(solution)/shard_map/dynamic_slice | solution.py:40
  2.8 4.4 %collective-permute-start.1 = (f32[49,4,256]{2,1,0:T(4,128)S(1)}, f32[49,4,256]{2,1,0:T(4,128)S(1)}, u32[]{:S(2)}, u32[]{:S(2)}) collective-permute-start(f32[49,4,256]{2,1,0:T(4,128)S(1)} %pad_maximum_fusion.6), channel_id=1, source_target_pairs={{0,1},{2,3},{4,5},{6,7},{8,9},{10,11},{12,13},{14,15},{1,0},{3,2},... | collective-permute-start | bytes 602120 | tf_op jit(solution)/shard_map/ppermute | solution.py:29
  7.2 0.7 collective-permute-start
  8.3 0.7 fusion.39
  9.0 0.7 compare_and_fusion
  9.6 0.6 collective-permute-done.1
  10.4 0.2 pad_maximum_fusion.1
  10.6 0.1 dynamic-slice_bitcast_fusion.1
  10.8 8.9 %collective-permute-start.3 = (f32[13,24,256]{2,1,0:T(8,128)S(1)}, f32[13,24,256]{2,1,0:T(8,128)S(1)}, u32[]{:S(2)}, u32[]{:S(2)}) collective-permute-start(f32[13,24,256]{2,1,0:T(8,128)S(1)} %pad_maximum_fusion.4), channel_id=1, source_target_pairs={{0,16},{32,48},{64,80},{96,112},{128,144},{160,176},{192,208},{224... | collective-permute-start | bytes 958472 | tf_op jit(solution)/shard_map/ppermute | solution.py:29
  19.7 1.9 %collective-permute-start.2 = (f32[13,24,256]{2,1,0:T(8,128)S(1)}, f32[13,24,256]{2,1,0:T(8,128)S(1)}, u32[]{:S(2)}, u32[]{:S(2)}) collective-permute-start(f32[13,24,256]{2,1,0:T(8,128)S(1)} %pad_maximum_fusion.3), channel_id=1, source_target_pairs={{16,32},{48,64},{80,96},{112,128},{144,160},{176,192},{208,224},{2... | collective-permute-start | bytes 958472 | tf_op jit(solution)/shard_map/ppermute | solution.py:28
  21.7 6.6 %collective-permute-done.2 = f32[13,24,256]{2,1,0:T(8,128)S(1)} collective-permute-done((f32[13,24,256]{2,1,0:T(8,128)S(1)}, f32[13,24,256]{2,1,0:T(8,128)S(1)}, u32[]{:S(2)}, u32[]{:S(2)}) %collective-permute-start.2) | collective-permute-done | bytes 319520 | tf_op jit(solution)/shard_map/ppermute | solution.py:28
  28.4 0.1 pad_maximum_fusion.8
  28.7 0.1 copy.41
  28.8 0.2 pad_maximum_fusion
  29.0 0.1 slice_bitcast_fusion.2
  29.1 0.1 copy.42
  29.2 0.2 fusion.3
  29.5 0.4 fusion.13
  29.9 0.2 fusion.17
  30.1 0.2 fusion.29
  30.4 0.8 gather_fusion
  31.2 0.2 select_reduce_fusion
  31.4 0.5 fusion.34
  31.9 0.3 fusion.30
  32.2 0.2 concatenate.35
  32.4 13.5 %all_to_all.15 = f32[32,1,1152]{2,1,0:T(1,128)S(1)} all-to-all(f32[32,1,1152]{2,1,0:T(1,128)S(1)} %bitcast.99), channel_id=1, replica_groups=mesh['lon'=32,'lat'=16] {'lon'}, dimensions={0} | all-to-all | bytes 294912 | tf_op jit(solution)/shard_map/all_to_all | solution.py:210
  46.0 0.1 reduce_sum.38
  46.1 29.8 %all_to_all.16 = f32[16,1,1152]{2,1,0:T(1,128)S(1)} all-to-all(f32[16,1,1152]{2,1,0:T(1,128)S(1)} %broadcast_in_dim.66), channel_id=1, replica_groups=mesh['lon'=32,'lat'=16] {'lat'}, dimensions={0} | all-to-all | bytes 147456 | tf_op jit(solution)/shard_map/all_to_all | solution.py:212
  76.0 0.1 broadcast_in_dim.67
  76.1 12.9 %all_to_all.17 = f32[32,1,1152]{2,1,0:T(1,128)S(1)} all-to-all(f32[32,1,1152]{2,1,0:T(1,128)S(1)} %broadcast_in_dim.67), channel_id=1, replica_groups=mesh['lon'=32,'lat'=16] {'lon'}, dimensions={0} | all-to-all | bytes 294912 | tf_op jit(solution)/shard_map/all_to_all | solution.py:214
  89.0 5.4 %shard_map.68 = (f32[768,256]{1,0:T(8,128)}, f32[256,256]{1,0:T(8,128)}) custom-call(f32[288,128]{1,0:T(8,128)S(1)} %bitcast.88, f32[768,256]{1,0:T(8,128)S(1)} %bitcast.87), custom_call_target="tpu_custom_call" | custom-call | tf_op jit(solution)/shard_map/pallas_call | solution.py:168
  (46 shorter events, 1.3 us)
Async XLA Ops:
  0.6 9.7 %copy-start = (f32[3,16,16,256]{3,2,1,0:T(8,128)S(1)}, f32[3,16,16,256]{3,2,1,0:T(8,128)}, u32[]{:S(2)}) copy-start(f32[3,16,16,256]{3,2,1,0:T(8,128)} %param.5) | copy-start | bytes 2359300
  2.8 7.5 %collective-permute-start.1 = (f32[49,4,256]{2,1,0:T(4,128)S(1)}, f32[49,4,256]{2,1,0:T(4,128)S(1)}, u32[]{:S(2)}, u32[]{:S(2)}) collective-permute-start(f32[49,4,256]{2,1,0:T(4,128)S(1)} %pad_maximum_fusion.6), channel_id=1, source_target_pairs={{0,1},{2,3},{4,5},{6,7},{8,9},{10,11},{12,13},{14,15},{1,0},{3,2},... | collective-permute-start | bytes 602120 | tf_op jit(solution)/shard_map/ppermute | solution.py:29
  7.2 3.0 %collective-permute-start = (f32[49,4,256]{2,1,0:T(4,128)S(1)}, f32[49,4,256]{2,1,0:T(4,128)S(1)}, u32[]{:S(2)}, u32[]{:S(2)}) collective-permute-start(f32[49,4,256]{2,1,0:T(4,128)S(1)} %pad_maximum_fusion.5), channel_id=1, source_target_pairs={{1,2},{3,4},{5,6},{7,8},{9,10},{11,12},{13,14},{2,1},{4,3},{6,5},{... | collective-permute-start | bytes 602120 | tf_op jit(solution)/shard_map/ppermute | solution.py:28
  10.8 11.0 %collective-permute-start.3 = (f32[13,24,256]{2,1,0:T(8,128)S(1)}, f32[13,24,256]{2,1,0:T(8,128)S(1)}, u32[]{:S(2)}, u32[]{:S(2)}) collective-permute-start(f32[13,24,256]{2,1,0:T(8,128)S(1)} %pad_maximum_fusion.4), channel_id=1, source_target_pairs={{0,16},{32,48},{64,80},{96,112},{128,144},{160,176},{192,208},{224... | collective-permute-start | bytes 958472 | tf_op jit(solution)/shard_map/ppermute | solution.py:29
  19.7 8.6 %collective-permute-start.2 = (f32[13,24,256]{2,1,0:T(8,128)S(1)}, f32[13,24,256]{2,1,0:T(8,128)S(1)}, u32[]{:S(2)}, u32[]{:S(2)}) collective-permute-start(f32[13,24,256]{2,1,0:T(8,128)S(1)} %pad_maximum_fusion.3), channel_id=1, source_target_pairs={{16,32},{48,64},{80,96},{112,128},{144,160},{176,192},{208,224},{2... | collective-permute-start | bytes 958472 | tf_op jit(solution)/shard_map/ppermute | solution.py:28
  30.3 1.0 %copy-start.1 = (f32[1,1,128]{2,1,0:T(1,128)S(1)}, f32[1,1,128]{2,1,0:T(1,128)}, u32[]{:S(2)}) copy-start(f32[1,1,128]{2,1,0:T(1,128)} %param.9) | copy-start | bytes 1540
  30.3 1.6 %copy-start.2 = (f32[1,1,128]{2,1,0:T(1,128)S(1)}, f32[1,1,128]{2,1,0:T(1,128)}, u32[]{:S(2)}) copy-start(f32[1,1,128]{2,1,0:T(1,128)} %param.8) | copy-start | bytes 1540

commit v4 on v2

v4 whole, which is shorter than its diff:
```python
import functools

import jax
import jax.numpy as jnp
from jax import lax
from jax.experimental import pallas as pl
from jax.experimental.pallas import tpu as pltpu
from jax.sharding import PartitionSpec as P

STEPS = 2
NS_ITERS = 6
LEVELS = 16
REACH = 2 * STEPS
VMEM_BYTES = 24 * 1024 * 1024
TILE = 16
LAT_ROWS = (3, 3, 4)
ROWS = sum(LAT_ROWS)
LON_ROWS = 192

time_step = 0.6
gravity = 1.0
rotation = 0.3


def shift_up(block, axis, wrap):
    count = lax.axis_size(axis)
    pairs = [(i, i + 1) for i in range(count - 1)]
    if wrap:
        pairs.append((count - 1, 0))
    return lax.ppermute(block, axis, pairs)


def shift_down(block, axis, wrap):
    count = lax.axis_size(axis)
    pairs = [(i + 1, i) for i in range(count - 1)]
    if wrap:
        pairs.append((0, count - 1))
    return lax.ppermute(block, axis, pairs)


def pack_lat_kernel(state_ref, bottom_ref, up_ref, down_ref, depth_ref, square_ref):
    lon, lat = state_ref.shape[1], state_ref.shape[2]
    square_ref[...] = jnp.zeros_like(square_ref)
    square_ref[:lon, :lat] = (bottom_ref[...].astype(jnp.float32) + 1.0) * (1.0 / LEVELS)
    turned = square_ref[...].T[:lat]
    depth_ref[...] = turned
    depth_at = ROWS * lon
    for ref in (up_ref, down_ref):
        ref[depth_at:] = jnp.zeros((ref.shape[0] - depth_at, ref.shape[1]), jnp.float32)
    up_ref[depth_at : depth_at + 3, :128] = turned[lat - 3 : lat]
    down_ref[depth_at : depth_at + 3, :128] = turned[:3]
    for field, count in enumerate(LAT_ROWS):
        for x in range(lon):
            at = lon * sum(LAT_ROWS[:field]) + x * count
            plane = state_ref[field, x]
            up_ref[at : at + count] = plane[lat - count :]
            down_ref[at : at + count] = plane[:count]


def lat_rows(ref, field, x, lon):
    at = lon * sum(LAT_ROWS[:field]) + x * LAT_ROWS[field]
    return ref[at : at + LAT_ROWS[field]]


def lon_layout():
    at = 0
    for field, width, reach in ((0, 3, 3), (1, 4, 4), (2, 3, 4)):
        for distance in range(1, width + 1):
            beyond = reach - distance
            yield field, distance, beyond, at
            at += TILE + 2 * beyond


def pack_lon_kernel(state_ref, low_ref, high_ref, depth_ref, up_ref, down_ref, strip_ref):
    lon = state_ref.shape[1]
    depth_at = ROWS * lon
    strip_ref[...] = jnp.zeros_like(strip_ref)
    strip_ref[1:4] = low_ref[depth_at : depth_at + 3, :128]
    strip_ref[4:20] = depth_ref[...]
    strip_ref[20:23] = high_ref[depth_at : depth_at + 3, :128]
    for ref in (up_ref, down_ref):
        ref[LON_ROWS:, 128:] = jnp.zeros((ref.shape[0] - LON_ROWS, 128), jnp.float32)
        ref[LON_ROWS - 2 : LON_ROWS] = jnp.zeros((2, ref.shape[1]), jnp.float32)
        ref[LON_ROWS:, :128] = strip_ref[...]
    for field, distance, beyond, at in lon_layout():
        for ref, x in ((up_ref, lon - distance), (down_ref, distance - 1)):
            if beyond:
                low = lat_rows(low_ref, field, x, lon)
                ref[at : at + beyond] = low[LAT_ROWS[field] - beyond :]
                high = lat_rows(high_ref, field, x, lon)
                ref[at + beyond + TILE : at + TILE + 2 * beyond] = high[:beyond]
            ref[at + beyond : at + beyond + TILE] = state_ref[field, x]


def dot3_first(left, right):
    dims = (((0,), (0,)), ((), ()))
    dot = functools.partial(lax.dot_general, dimension_numbers=dims, preferred_element_type=jnp.float32)
    left_high, left_low = left
    right_high, right_low = right
    return dot(left_high, right_high) + (dot(left_high, right_low) + dot(left_low, right_high))


def step_kernel(
    state_ref,
    low_ref,
    high_ref,
    west_ref,
    east_ref,
    strip_ref,
    turning_ref,
    inside_ref,
    cell_ref,
    value_ref,
    weight_ref,
    forecast_ref,
    packed_ref,
    field_ref,
    next_ref,
    last_ref,
    picked_ref,
):
    lon = state_ref.shape[1]
    members = state_ref.shape[3]
    wide = TILE + 2 * REACH
    for field, count in enumerate(LAT_ROWS):
        for x in range(lon):
            field_ref[field, REACH + x, REACH : REACH + TILE] = state_ref[field, x]
            field_ref[field, REACH + x, REACH - count : REACH] = lat_rows(low_ref, field, x, lon)
            field_ref[field, REACH + x, REACH + TILE : REACH + TILE + count] = lat_rows(
                high_ref, field, x, lon
            )
    for field, distance, beyond, at in lon_layout():
        rows = slice(REACH - beyond, REACH + TILE + beyond)
        taken = slice(at, at + TILE + 2 * beyond)
        field_ref[field, REACH - distance, rows] = west_ref[taken]
        field_ref[field, REACH + lon - 1 + distance, rows] = east_ref[taken]
    turning = time_step * jnp.broadcast_to(turning_ref[:, :1], (wide, members))
    keeper = jnp.broadcast_to(inside_ref[:, :1], (wide, members))
    pull = 0.5 * time_step * gravity

    def column(x):
        if x < REACH:
            depth = west_ref[LON_ROWS:, lon - REACH + x : lon - REACH + x + 1]
        elif x < REACH + lon:
            depth = strip_ref[:, x - REACH : x - REACH + 1]
        else:
            depth = east_ref[LON_ROWS:, x - REACH - lon : x - REACH - lon + 1]
        return jnp.broadcast_to(0.5 * time_step * depth, (wide, members))

    def along(plane):
        return pltpu.roll(plane, wide - 1, 0) - pltpu.roll(plane, 1, 0)

    def advance_height(source, target, x):
        spread = source[1, x + 1] - source[1, x - 1] + along(source[2, x])
        target[0, x] = source[0, x] - column(x) * spread

    def advance_flow(source, heights, x):
        east = source[1, x]
        north = source[2, x]
        slope_east = heights[0, x + 1] - heights[0, x - 1]
        slope_north = along(heights[0, x])
        return (
            east + (turning * north - pull * slope_east),
            north - (turning * east + pull * slope_north),
        )

    for x in range(1, wide - 1):
        advance_height(field_ref, next_ref, x)
    for x in range(2, wide - 2):
        east, north = advance_flow(field_ref, next_ref, x)
        next_ref[1, x] = east
        next_ref[2, x] = north * keeper
    for x in range(3, wide - 3):
        advance_height(next_ref, last_ref, x)
    for x in range(REACH, REACH + lon):
        east, north = advance_flow(next_ref, last_ref, x)
        for field, plane in enumerate((last_ref[0, x], east, north)):
            at = (field * lon + x - REACH) * TILE
            forecast_ref[at : at + TILE] = plane[REACH : REACH + TILE]

    count = picked_ref.shape[0]
    for k in range(count):
        picked_ref[k : k + 1] = forecast_ref[pl.ds(cell_ref[0, 0, k], 1)]
    picked = picked_ref[...]
    ymean = jnp.sum(picked, axis=1, keepdims=True) * (1.0 / members)
    half = members // 2
    row = lax.broadcasted_iota(jnp.int32, (half, half), 0)
    line = lax.broadcasted_iota(jnp.int32, (half, half), 1)
    on_diagonal = row == line
    weight = jnp.sum(jnp.where(on_diagonal, weight_ref[0], 0.0), axis=1, keepdims=True)
    value = jnp.sum(jnp.where(on_diagonal, value_ref[0], 0.0), axis=1, keepdims=True)
    anomaly = (picked - ymean) * weight
    innovation = (value - ymean) * weight
    projected = jnp.sum(innovation * anomaly, axis=0, keepdims=True)
    left_high, left_low = halves(anomaly[:, :half])
    right_high, right_low = halves(anomaly[:, half:])
    first = dot3_first((left_high, left_low), (left_high, left_low))
    cross = dot3_first((left_high, left_low), (right_high, right_low))
    final = dot3_first((right_high, right_low), (right_high, right_low))
    packed_ref[:half] = jnp.where(row <= line, first, final)
    packed_ref[half : 2 * half] = cross
    packed_ref[2 * half :] = jnp.zeros((packed_ref.shape[0] - 2 * half, half), jnp.float32)
    packed_ref[2 * half : 2 * half + 1] = jnp.sum(
        jnp.where(on_diagonal, final, 0.0), axis=0, keepdims=True
    )
    packed_ref[2 * half + 1 : 2 * half + 2] = projected[:, :half]
    packed_ref[2 * half + 2 : 2 * half + 3] = projected[:, half:]


def on_core(kernel, outs, spaces, scratch):
    return pl.pallas_call(
        kernel,
        out_shape=tuple(jax.ShapeDtypeStruct(shape, jnp.float32) for shape in outs),
        in_specs=[pl.BlockSpec(memory_space=space) for space in spaces],
        out_specs=tuple(pl.BlockSpec(memory_space=pltpu.VMEM) for _ in outs),
        scratch_shapes=scratch,
        compiler_params=pltpu.CompilerParams(vmem_limit_bytes=VMEM_BYTES),
    )


def halves(value):
    high = value.astype(jnp.bfloat16)
    return high, (value - high.astype(jnp.float32)).astype(jnp.bfloat16)


def dot3(left, right):
    left_high, left_low = left
    right_high, right_low = right
    dot = functools.partial(jnp.dot, preferred_element_type=jnp.float32)
    return dot(left_high, right_high) + (dot(left_high, right_low) + dot(left_low, right_high))


def finish_kernel(packed_ref, state_ref, analysis_ref, transform_ref):
    half = packed_ref.shape[1]
    members = 2 * half
    square = packed_ref[:half]
    cross = packed_ref[half : 2 * half]
    diagonal = packed_ref[2 * half : 2 * half + 1]
    turned = square.T
    row = lax.broadcasted_iota(jnp.int32, (half, half), 0)
    column = lax.broadcasted_iota(jnp.int32, (half, half), 1)
    first = jnp.where(row <= column, square, turned)
    last = jnp.where(row == column, diagonal, jnp.where(row < column, turned, square))
    gram = jnp.concatenate(
        [jnp.concatenate([first, cross], axis=1), jnp.concatenate([cross.T, last], axis=1)]
    )
    row = lax.broadcasted_iota(jnp.int32, (members, members), 0)
    column = lax.broadcasted_iota(jnp.int32, (members, members), 1)
    on_diagonal = row == column
    system = gram + jnp.where(on_diagonal, members - 1.0, 0.0)
    scaler = jnp.sqrt(
        jnp.sum(jnp.sum(system * system, axis=0, keepdims=True), axis=1, keepdims=True)
    )
    root = system * (1.0 / scaler)
    triple = jnp.where(on_diagonal, 1.5, 0.0)

    inverse = triple - 0.5 * root
    factor = halves(inverse)
    root = halves(dot3(halves(root), factor))
    inverse = factor
    for step in range(1, NS_ITERS):
        factor = halves(triple - 0.5 * dot3(inverse, root))
        if step < NS_ITERS - 1:
            root = halves(dot3(root, factor))
            inverse = halves(dot3(factor, inverse))
        else:
            inverse = dot3(factor, inverse)
    projected = jnp.concatenate(
        [packed_ref[2 * half + 1 : 2 * half + 2], packed_ref[2 * half + 2 : 2 * half + 3]], axis=1
    )
    once = jnp.sum(inverse * projected, axis=1, keepdims=True)
    once = jnp.sum(jnp.where(on_diagonal, once, 0.0), axis=0, keepdims=True)
    offset = jnp.sum(inverse * once, axis=1, keepdims=True) / scaler
    transform = jnp.sqrt((members - 1.0) / scaler) * inverse + offset
    transform_ref[...] = transform
    transform = halves(transform)
    block = 256
    for start in range(0, state_ref.shape[0], block):
        state = state_ref[start : start + block]
        average = jnp.sum(state, axis=1, keepdims=True) * (1.0 / members)
        analysis_ref[start : start + block] = average + dot3(halves(state - average), transform)


def finish(packed, state):
    vmem = pl.BlockSpec(memory_space=pltpu.VMEM)
    members = state.shape[1]
    return pl.pallas_call(
        finish_kernel,
        out_shape=(
            jax.ShapeDtypeStruct(state.shape, jnp.float32),
            jax.ShapeDtypeStruct((members, members), jnp.float32),
        ),
        in_specs=[vmem, vmem],
        out_specs=(vmem, vmem),
        compiler_params=pltpu.CompilerParams(vmem_limit_bytes=VMEM_BYTES),
    )(packed, state)


def reduced(packed):
    lon = lax.axis_size("lon")
    lat = lax.axis_size("lat")
    width = packed.size // lon
    pieces = lax.all_to_all(packed.reshape(lon, 1, width), "lon", 0, 0)
    piece = jnp.sum(pieces, axis=0)
    pieces = lax.all_to_all(jnp.broadcast_to(piece[None], (lat, 1, width)), "lat", 0, 0)
    piece = jnp.sum(pieces, axis=0)
    pieces = lax.all_to_all(jnp.broadcast_to(piece[None], (lon, 1, width)), "lon", 0, 0)
    return pieces.reshape(packed.shape)


def local(ensemble, bathymetry, obs_cell, obs_value, obs_weight):
    fields, lon, lat, members = ensemble.shape
    vmem = pltpu.VMEM
    total_lat = lat * lax.axis_size("lat")
    wide = lat + 2 * REACH
    rows = lax.axis_index("lat") * lat - REACH + lax.broadcasted_iota(jnp.int32, (wide, 128), 0)
    inside = ((rows >= 0) & (rows < total_lat)).astype(jnp.float32)
    turning = rotation * (2.0 * (rows.astype(jnp.float32) + 0.5) / total_lat - 1.0)
    lat_shape = (ROWS * lon + 8, members)
    lon_shape = (LON_ROWS + wide, members)
    up, down, depth = on_core(
        pack_lat_kernel,
        (lat_shape, lat_shape, (lat, 128)),
        [vmem] * 2,
        [pltpu.VMEM((128, 128), jnp.float32)],
    )(ensemble, bathymetry)
    low = shift_up(up, "lat", False)
    high = shift_down(down, "lat", False)
    up, down, strip = on_core(
        pack_lon_kernel, (lon_shape, lon_shape, (wide, 128)), [vmem] * 4, []
    )(ensemble, low, high, depth)
    west = shift_up(up, "lon", True)
    east = shift_down(down, "lon", True)
    planes = (fields, lon + 2 * REACH, wide, members)
    forecast, packed = on_core(
        step_kernel,
        ((fields * lon * lat, members), (members + 32, members // 2)),
        [vmem] * 8 + [pltpu.SMEM] + [vmem] * 2,
        [pltpu.VMEM(planes, jnp.float32)] * 2
        + [pltpu.VMEM((1,) + planes[1:], jnp.float32)]
        + [pltpu.VMEM((obs_cell.shape[2], members), jnp.float32)],
    )(ensemble, low, high, west, east, strip, turning, inside, obs_cell, obs_value, obs_weight)
    analysis, transform = finish(reduced(packed), forecast)
    return (analysis.reshape(ensemble.shape), transform)


def solution(mesh):
    return jax.shard_map(
        local,
        mesh=mesh,
        in_specs=(
            P(None, "lon", "lat", None),
            P("lon", "lat"),
            P("lon", "lat", None),
            P("lon", "lat", None),
            P("lon", "lat", None),
        ),
        out_specs=(P(None, "lon", "lat", None), P()),
        check_vma=False,
    )
```

time: 93.7 us -> 90.8 us (0.969)
  waiting for transfers between devices: 3.7 us -> 9.5 us
  other arithmetic: 3.73 us -> 0.17 us
  starting transfers between devices: 17.1 us -> 14.4 us
  Pallas kernels: 5.37 us -> 7.81 us
  blocking collectives: 57.4 us -> 55 us
  local copies, waits for them, and re-layouts: 4.22 us -> 2.77 us
    ppermute x2, waiting for transfers between devices: 2.79 us -> 8.47 us  [shift_down(): return lax.ppermute(block, axis, pairs)]
    all_to_all x1, blocking collectives: 20.7 us -> 18.2 us  [reduced(): pieces = lax.all_to_all(packed.reshape(lon, 1, width), 'lon', 0, 0)]
    pallas_call x0 -> x3, Pallas kernels: none -> 2.44 us  [the longest x1 2.25 us: local(): on_core(step_kernel, ((fields * lon * lat, members), (members + 32, membe...]
    ppermute x2, starting transfers between devices: 6.54 us -> 4.32 us  [shift_down(): return lax.ppermute(block, axis, pairs)]
    slice x13 -> x0, local copies, waits for them, and re-layouts: 1.72 us -> none  [the longest x1 1.19 us: lat_message(): cells = lax.slice_in_dim(ensemble, start, start + REACH, axis=2)]
    unnamed x7 -> x12, local copies, waits for them, and re-layouts: 0.86 us -> 2.51 us
    mul x5 -> x0, other arithmetic: 1.01 us -> none  [the longest x2 0.46 us: advance(): (height[1:-1, 1:-1] - time_step * depths[1:-1, 1:-1, None] * spread_in) *...]
  transfers between devices with their start and end apart: 4 -> 4, of which waited for: 2 -> 3; matrix products, arithmetic and copies ran while one was open for 2% -> 0% of each run, Pallas kernels for 0% -> 0%
where the time goes in v4:
time: 90.8 us; the launch traced here: 90.4 us
  blocking collectives  55 us (61%)
  starting transfers between devices  14.4 us (16%)
  waiting for transfers between devices  9.5 us (10%)
  Pallas kernels  7.81 us (9%)
  local copies, waits for them, and re-layouts  2.77 us (3%)
    all_to_all x1, blocking collectives, reduced(): lax.all_to_all(jnp.broadcast_to(piece[None], (lat, 1, width)), 'lat', 0, 0)  23.9 us
    all_to_all x1, blocking collectives, reduced(): pieces = lax.all_to_all(packed.reshape(lon, 1, width), 'lon', 0, 0)  18.2 us
    all_to_all x1, blocking collectives, reduced(): lax.all_to_all(jnp.broadcast_to(piece[None], (lon, 1, width)), 'lon', 0, 0)  12.9 us
    ppermute x2, starting transfers between devices, shift_up(): return lax.ppermute(block, axis, pairs)  10 us
    ppermute x2, waiting for transfers between devices, shift_down(): return lax.ppermute(block, axis, pairs)  8.47 us
    pallas_call x1, Pallas kernels, finish(): pl.pallas_call(finish_kernel, out_shape=(jax.ShapeDtypeStruct(state.shape...  5.37 us
    ppermute x2, starting transfers between devices, shift_down(): return lax.ppermute(block, axis, pairs)  4.32 us
    unnamed x12, local copies, waits for them, and re-layouts  2.51 us
  transfers between devices with their start and end apart: 4, of which 3 were waited for; matrix products, arithmetic and copies ran while one was open for 0% of the time, Pallas kernels for 0%

profile of v4, /device:TPU:1, one launch (start us, length us, event | category | flops | bytes accessed | tf_op | source)
XLA Modules:
  0.0 90.4 jit_solution(12968438175259785618)
XLA Ops:
  0.6 0.0 copy-start
  0.6 1.1 %copy-done = f32[3,16,16,256]{3,2,1,0:T(8,128)S(1)} copy-done((f32[3,16,16,256]{3,2,1,0:T(8,128)S(1)}, f32[3,16,16,256]{3,2,1,0:T(8,128)}, u32[]{:S(2)}) %copy-start) | copy-done | bytes 786456
  1.8 0.0 copy-start.2
  1.8 0.7 copy-done.2
  2.5 0.0 copy-start.1
  2.5 0.1 shard_map.68
  2.6 4.5 %collective-permute-start = (f32[168,256]{1,0:T(8,128)S(1)}, f32[168,256]{1,0:T(8,128)S(1)}, u32[]{:S(2)}, u32[]{:S(2)}) collective-permute-start(f32[168,256]{1,0:T(8,128)S(1)} %get-tuple-element.12), channel_id=1, source_target_pairs={{0,1},{1,2},{2,3},{3,4},{4,5},{5,6},{6,7},{7,8},{8,9},{9,10},{10,1... | collective-permute-start | bytes 516104 | tf_op jit(solution)/shard_map/ppermute | solution.py:30
  7.1 1.3 %collective-permute-start.1 = (f32[168,256]{1,0:T(8,128)S(1)}, f32[168,256]{1,0:T(8,128)S(1)}, u32[]{:S(2)}, u32[]{:S(2)}) collective-permute-start(f32[168,256]{1,0:T(8,128)S(1)} %get-tuple-element.13), channel_id=1, source_target_pairs={{1,0},{2,1},{3,2},{4,3},{5,4},{6,5},{7,6},{8,7},{9,8},{10,9},{11,1... | collective-permute-start | bytes 516104 | tf_op jit(solution)/shard_map/ppermute | solution.py:38
  8.4 1.0 %collective-permute-done.low_ref = f32[168,256]{1,0:T(8,128)S(1)} collective-permute-done((f32[168,256]{1,0:T(8,128)S(1)}, f32[168,256]{1,0:T(8,128)S(1)}, u32[]{:S(2)}, u32[]{:S(2)}) %collective-permute-start) | collective-permute-done | bytes 172064 | tf_op jit(solution)/shard_map/ppermute | solution.py:30
  9.4 4.0 %collective-permute-done.1.high_ref = f32[168,256]{1,0:T(8,128)S(1)} collective-permute-done((f32[168,256]{1,0:T(8,128)S(1)}, f32[168,256]{1,0:T(8,128)S(1)}, u32[]{:S(2)}, u32[]{:S(2)}) %collective-permute-start.1) | collective-permute-done | bytes 172064 | tf_op jit(solution)/shard_map/ppermute | solution.py:38
  13.4 0.0 copy-done.1
  13.4 0.1 shard_map.69
  13.5 5.5 %collective-permute-start.2 = (f32[216,256]{1,0:T(8,128)S(1)}, f32[216,256]{1,0:T(8,128)S(1)}, u32[]{:S(2)}, u32[]{:S(2)}) collective-permute-start(f32[216,256]{1,0:T(8,128)S(1)} %get-tuple-element.15), channel_id=1, source_target_pairs={{0,16},{16,32},{32,48},{48,64},{64,80},{80,96},{96,112},{112,128},... | collective-permute-start | bytes 663560 | tf_op jit(solution)/shard_map/ppermute | solution.py:30
  19.1 3.0 %collective-permute-start.3 = (f32[216,256]{1,0:T(8,128)S(1)}, f32[216,256]{1,0:T(8,128)S(1)}, u32[]{:S(2)}, u32[]{:S(2)}) collective-permute-start(f32[216,256]{1,0:T(8,128)S(1)} %get-tuple-element.16), channel_id=1, source_target_pairs={{16,0},{32,16},{48,32},{64,48},{80,64},{96,80},{112,96},{128,112},... | collective-permute-start | bytes 663560 | tf_op jit(solution)/shard_map/ppermute | solution.py:38
  22.1 0.0 collective-permute-done.2.west_ref
  22.1 4.5 %collective-permute-done.3.east_ref = f32[216,256]{1,0:T(8,128)S(1)} collective-permute-done((f32[216,256]{1,0:T(8,128)S(1)}, f32[216,256]{1,0:T(8,128)S(1)}, u32[]{:S(2)}, u32[]{:S(2)}) %collective-permute-start.3) | collective-permute-done | bytes 221216 | tf_op jit(solution)/shard_map/ppermute | solution.py:38
  26.6 0.1 iota.9.turning_ref
  26.7 0.1 iota.10.inside_ref
  26.7 0.0 copy-start.3
  26.7 0.0 copy-start.4
  26.7 0.0 copy-start.5
  26.7 0.7 copy-done.3
  27.4 0.0 copy-done.4
  27.4 0.0 copy-done.5
  27.4 2.3 %shard_map.70 = (f32[768,256]{1,0:T(8,128)S(1)}, f32[288,128]{1,0:T(8,128)S(1)}) custom-call(f32[3,16,16,256]{3,2,1,0:T(8,128)S(1)} %copy-done.1, f32[168,256]{1,0:T(8,128)S(1)} %collective-permute-done.low_ref, f32[168,256]{1,0:T(8,128)S(1)} %collective-permute-done.1.high_ref, f32[216,256]{1,0:T(8,128)S(1)} %collective-permute-done.2.west_ref, ...), custom_call_target="tpu_custom_call" | custom-call | tf_op jit(solution)/shard_map/pallas_call | solution.py:335
  29.7 18.2 %all_to_all.15 = f32[32,1,1152]{2,1,0:T(1,128)S(1)} all-to-all(f32[32,1,1152]{2,1,0:T(1,128)S(1)} %bitcast.4), channel_id=1, replica_groups=mesh['lon'=32,'lat'=16] {'lon'}, dimensions={0} | all-to-all | bytes 294912 | tf_op jit(solution)/shard_map/all_to_all | solution.py:303
  47.9 0.1 reduce_sum.18
  48.0 23.9 %all_to_all.16 = f32[16,1,1152]{2,1,0:T(1,128)S(1)} all-to-all(f32[16,1,1152]{2,1,0:T(1,128)S(1)} %broadcast_in_dim.4), channel_id=1, replica_groups=mesh['lon'=32,'lat'=16] {'lat'}, dimensions={0} | all-to-all | bytes 147456 | tf_op jit(solution)/shard_map/all_to_all | solution.py:305
  72.0 0.1 reduce_sum.19
  72.0 0.1 broadcast_in_dim.5
  72.1 12.9 %all_to_all.17 = f32[32,1,1152]{2,1,0:T(1,128)S(1)} all-to-all(f32[32,1,1152]{2,1,0:T(1,128)S(1)} %broadcast_in_dim.5), channel_id=1, replica_groups=mesh['lon'=32,'lat'=16] {'lon'}, dimensions={0} | all-to-all | bytes 294912 | tf_op jit(solution)/shard_map/all_to_all | solution.py:307
  85.0 5.4 %shard_map.71 = (f32[768,256]{1,0:T(8,128)}, f32[256,256]{1,0:T(8,128)}) custom-call(f32[288,128]{1,0:T(8,128)S(1)} %bitcast.3, f32[768,256]{1,0:T(8,128)S(1)} %get-tuple-element.19.state_ref), custom_call_target="tpu_custom_call" | custom-call | tf_op jit(solution)/shard_map/pallas_call | solution.py:287
  (3 shorter events, 0.1 us)
Async XLA Ops:
  0.6 1.1 %copy-start = (f32[3,16,16,256]{3,2,1,0:T(8,128)S(1)}, f32[3,16,16,256]{3,2,1,0:T(8,128)}, u32[]{:S(2)}) copy-start(f32[3,16,16,256]{3,2,1,0:T(8,128)} %state_ref.5) | copy-start | bytes 2359300
  1.8 0.7 copy-start.2
  2.5 11.0 %copy-start.1 = (f32[3,16,16,256]{3,2,1,0:T(8,128)S(1)}, f32[3,16,16,256]{3,2,1,0:T(8,128)}, u32[]{:S(2)}) copy-start(f32[3,16,16,256]{3,2,1,0:T(8,128)} %state_ref.5) | copy-start | bytes 2359300
  2.6 6.8 %collective-permute-start = (f32[168,256]{1,0:T(8,128)S(1)}, f32[168,256]{1,0:T(8,128)S(1)}, u32[]{:S(2)}, u32[]{:S(2)}) collective-permute-start(f32[168,256]{1,0:T(8,128)S(1)} %get-tuple-element.12), channel_id=1, source_target_pairs={{0,1},{1,2},{2,3},{3,4},{4,5},{5,6},{6,7},{7,8},{8,9},{9,10},{10,1... | collective-permute-start | bytes 516104 | tf_op jit(solution)/shard_map/ppermute | solution.py:30
  7.1 6.3 %collective-permute-start.1 = (f32[168,256]{1,0:T(8,128)S(1)}, f32[168,256]{1,0:T(8,128)S(1)}, u32[]{:S(2)}, u32[]{:S(2)}) collective-permute-start(f32[168,256]{1,0:T(8,128)S(1)} %get-tuple-element.13), channel_id=1, source_target_pairs={{1,0},{2,1},{3,2},{4,3},{5,4},{6,5},{7,6},{8,7},{9,8},{10,9},{11,1... | collective-permute-start | bytes 516104 | tf_op jit(solution)/shard_map/ppermute | solution.py:38
  13.5 8.6 %collective-permute-start.2 = (f32[216,256]{1,0:T(8,128)S(1)}, f32[216,256]{1,0:T(8,128)S(1)}, u32[]{:S(2)}, u32[]{:S(2)}) collective-permute-start(f32[216,256]{1,0:T(8,128)S(1)} %get-tuple-element.15), channel_id=1, source_target_pairs={{0,16},{16,32},{32,48},{48,64},{64,80},{80,96},{96,112},{112,128},... | collective-permute-start | bytes 663560 | tf_op jit(solution)/shard_map/ppermute | solution.py:30
  19.1 7.5 %collective-permute-start.3 = (f32[216,256]{1,0:T(8,128)S(1)}, f32[216,256]{1,0:T(8,128)S(1)}, u32[]{:S(2)}, u32[]{:S(2)}) collective-permute-start(f32[216,256]{1,0:T(8,128)S(1)} %get-tuple-element.16), channel_id=1, source_target_pairs={{16,0},{32,16},{48,32},{64,48},{80,64},{96,80},{112,96},{128,112},... | collective-permute-start | bytes 663560 | tf_op jit(solution)/shard_map/ppermute | solution.py:38
  26.7 0.7 copy-start.3
  26.7 0.7 copy-start.4
  26.7 0.7 copy-start.5

commit v5 on v4

--- a/solution.py
+++ b/solution.py
@@ -38,28 +38,57 @@
     return lax.ppermute(block, axis, pairs)
 
 
-def pack_lat_kernel(state_ref, bottom_ref, up_ref, down_ref, depth_ref, square_ref):
+def fetch(sources, targets, sems):
+    copies = [
+        pltpu.make_async_copy(source, target, sems.at[k])
+        for k, (source, target) in enumerate(zip(sources, targets))
+    ]
+    for copy in copies:
+        copy.start()
+    return copies
+
+
+def pack_lat_kernel(
+    even_ref, ensemble_ref, bathymetry_ref, first_ref, second_ref, depth_ref, state_ref, bottom_ref, square_ref, sems
+):
     lon, lat = state_ref.shape[1], state_ref.shape[2]
+    copies = fetch((bathymetry_ref, ensemble_ref), (bottom_ref, state_ref), sems)
     square_ref[...] = jnp.zeros_like(square_ref)
+    depth_at = ROWS * lon
+    for ref in (first_ref, second_ref):
+        ref[depth_at:] = jnp.zeros((ref.shape[0] - depth_at, ref.shape[1]), jnp.float32)
+    copies[0].wait()
     square_ref[:lon, :lat] = (bottom_ref[...].astype(jnp.float32) + 1.0) * (1.0 / LEVELS)
     turned = square_ref[...].T[:lat]
     depth_ref[...] = turned
-    depth_at = ROWS * lon
-    for ref in (up_ref, down_ref):
-        ref[depth_at:] = jnp.zeros((ref.shape[0] - depth_at, ref.shape[1]), jnp.float32)
-    up_ref[depth_at : depth_at + 3, :128] = turned[lat - 3 : lat]
-    down_ref[depth_at : depth_at + 3, :128] = turned[:3]
-    for field, count in enumerate(LAT_ROWS):
-        for x in range(lon):
-            at = lon * sum(LAT_ROWS[:field]) + x * count
-            plane = state_ref[field, x]
-            up_ref[at : at + count] = plane[lat - count :]
-            down_ref[at : at + count] = plane[:count]
-
-
-def lat_rows(ref, field, x, lon):
+    copies[1].wait()
+
+    def pack(up_ref, down_ref):
+        up_ref[depth_at : depth_at + 3, :128] = turned[lat - 3 : lat]
+        down_ref[depth_at : depth_at + 3, :128] = turned[:3]
+        for field, count in enumerate(LAT_ROWS):
+            for x in range(lon):
+                at = lon * sum(LAT_ROWS[:field]) + x * count
+                plane = state_ref[field, x]
+                up_ref[at : at + count] = plane[lat - count :]
+                down_ref[at : at + count] = plane[:count]
+
+    @pl.when(even_ref[0] == 1)
+    def _():
+        pack(first_ref, second_ref)
+
+    @pl.when(even_ref[0] != 1)
+    def _():
+        pack(second_ref, first_ref)
+
+
+def chosen(even, first_ref, second_ref, rows, lanes=slice(None)):
+    return jnp.where(even, first_ref[rows, lanes], second_ref[rows, lanes])
+
+
+def lat_rows(even, first_ref, second_ref, field, x, lon):
     at = lon * sum(LAT_ROWS[:field]) + x * LAT_ROWS[field]
-    return ref[at : at + LAT_ROWS[field]]
+    return chosen(even, first_ref, second_ref, slice(at, at + LAT_ROWS[field]))
 
 
 def lon_layout():
@@ -71,13 +100,19 @@
             at += TILE + 2 * beyond
 
 
-def pack_lon_kernel(state_ref, low_ref, high_ref, depth_ref, up_ref, down_ref, strip_ref):
+def pack_lon_kernel(
+    even_ref, state_ref, first_ref, second_ref, depth_ref, up_ref, down_ref, strip_ref
+):
     lon = state_ref.shape[1]
+    even = even_ref[0] == 1
+    low_rows = functools.partial(lat_rows, even, first_ref, second_ref)
+    high_rows = functools.partial(lat_rows, even, second_ref, first_ref)
     depth_at = ROWS * lon
     strip_ref[...] = jnp.zeros_like(strip_ref)
-    strip_ref[1:4] = low_ref[depth_at : depth_at + 3, :128]
+    depths = slice(depth_at, depth_at + 3)
+    strip_ref[1:4] = chosen(even, first_ref, second_ref, depths, slice(0, 128))
     strip_ref[4:20] = depth_ref[...]
-    strip_ref[20:23] = high_ref[depth_at : depth_at + 3, :128]
+    strip_ref[20:23] = chosen(even, second_ref, first_ref, depths, slice(0, 128))
     for ref in (up_ref, down_ref):
         ref[LON_ROWS:, 128:] = jnp.zeros((ref.shape[0] - LON_ROWS, 128), jnp.float32)
         ref[LON_ROWS - 2 : LON_ROWS] = jnp.zeros((2, ref.shape[1]), jnp.float32)
@@ -85,9 +120,9 @@
     for field, distance, beyond, at in lon_layout():
         for ref, x in ((up_ref, lon - distance), (down_ref, distance - 1)):
             if beyond:
-                low = lat_rows(low_ref, field, x, lon)
+                low = low_rows(field, x, lon)
                 ref[at : at + beyond] = low[LAT_ROWS[field] - beyond :]
-                high = lat_rows(high_ref, field, x, lon)
+                high = high_rows(field, x, lon)
                 ref[at + beyond + TILE : at + TILE + 2 * beyond] = high[:beyond]
             ref[at + beyond : at + beyond + TILE] = state_ref[field, x]
 
@@ -101,33 +136,44 @@
 
 
 def step_kernel(
+    even_ref,
     state_ref,
-    low_ref,
-    high_ref,
+    first_ref,
+    second_ref,
     west_ref,
     east_ref,
     strip_ref,
     turning_ref,
     inside_ref,
-    cell_ref,
-    value_ref,
-    weight_ref,
+    obs_cell_ref,
+    obs_value_ref,
+    obs_weight_ref,
     forecast_ref,
     packed_ref,
     field_ref,
     next_ref,
     last_ref,
     picked_ref,
+    cell_ref,
+    value_ref,
+    weight_ref,
+    sems,
 ):
+    copies = fetch(
+        (obs_cell_ref, obs_value_ref, obs_weight_ref), (cell_ref, value_ref, weight_ref), sems
+    )
     lon = state_ref.shape[1]
+    even = even_ref[0] == 1
+    low_rows = functools.partial(lat_rows, even, first_ref, second_ref)
+    high_rows = functools.partial(lat_rows, even, second_ref, first_ref)
     members = state_ref.shape[3]
     wide = TILE + 2 * REACH
     for field, count in enumerate(LAT_ROWS):
         for x in range(lon):
             field_ref[field, REACH + x, REACH : REACH + TILE] = state_ref[field, x]
-            field_ref[field, REACH + x, REACH - count : REACH] = lat_rows(low_ref, field, x, lon)
-            field_ref[field, REACH + x, REACH + TILE : REACH + TILE + count] = lat_rows(
-                high_ref, field, x, lon
+            field_ref[field, REACH + x, REACH - count : REACH] = low_rows(field, x, lon)
+            field_ref[field, REACH + x, REACH + TILE : REACH + TILE + count] = high_rows(
+                field, x, lon
             )
     for field, distance, beyond, at in lon_layout():
         rows = slice(REACH - beyond, REACH + TILE + beyond)
@@ -178,6 +224,8 @@
             at = (field * lon + x - REACH) * TILE
             forecast_ref[at : at + TILE] = plane[REACH : REACH + TILE]
 
+    for copy in copies:
+        copy.wait()
     count = picked_ref.shape[0]
     for k in range(count):
         picked_ref[k : k + 1] = forecast_ref[pl.ds(cell_ref[0, 0, k], 1)]
@@ -207,12 +255,16 @@
     packed_ref[2 * half + 2 : 2 * half + 3] = projected[:, half:]
 
 
-def on_core(kernel, outs, spaces, scratch):
+def in_hbm(value):
+    return pltpu.with_memory_space_constraint(value, pltpu.HBM)
+
+
+def on_core(kernel, outs, spaces, scratch, out_space=pltpu.VMEM):
     return pl.pallas_call(
         kernel,
         out_shape=tuple(jax.ShapeDtypeStruct(shape, jnp.float32) for shape in outs),
         in_specs=[pl.BlockSpec(memory_space=space) for space in spaces],
-        out_specs=tuple(pl.BlockSpec(memory_space=pltpu.VMEM) for _ in outs),
+        out_specs=tuple(pl.BlockSpec(memory_space=out_space) for _ in outs),
         scratch_shapes=scratch,
         compiler_params=pltpu.CompilerParams(vmem_limit_bytes=VMEM_BYTES),
     )
@@ -230,7 +282,9 @@
     return dot(left_high, right_high) + (dot(left_high, right_low) + dot(left_low, right_high))
 
 
-def finish_kernel(packed_ref, state_ref, analysis_ref, transform_ref):
+def finish_kernel(
+    packed_ref, state_ref, analysis_ref, transform_ref, moved_ref, matrix_ref, sems
+):
     half = packed_ref.shape[1]
     members = 2 * half
     square = packed_ref[:half]
@@ -252,19 +306,22 @@
         jnp.sum(jnp.sum(system * system, axis=0, keepdims=True), axis=1, keepdims=True)
     )
     root = system * (1.0 / scaler)
-    triple = jnp.where(on_diagonal, 1.5, 0.0)
-
-    inverse = triple - 0.5 * root
-    factor = halves(inverse)
-    root = halves(dot3(halves(root), factor))
-    inverse = factor
-    for step in range(1, NS_ITERS):
-        factor = halves(triple - 0.5 * dot3(inverse, root))
-        if step < NS_ITERS - 1:
-            root = halves(dot3(root, factor))
+    level = jnp.where(on_diagonal, 2.25, 0.0)
+
+    product = root
+    for step in range(0, NS_ITERS, 2):
+        split = halves(product)
+        square = dot3(split, split)
+        higher = dot3(halves(square), halves(0.0625 * square - 0.5625 * product))
+        factor = halves(level - 2.4375 * product + 1.6875 * square + higher)
+        if step == 0:
+            inverse = factor
+        elif step < NS_ITERS - 2:
             inverse = halves(dot3(factor, inverse))
         else:
             inverse = dot3(factor, inverse)
+        if step < NS_ITERS - 2:
+            product = dot3(factor, halves(dot3(factor, split)))
     projected = jnp.concatenate(
         [packed_ref[2 * half + 1 : 2 * half + 2], packed_ref[2 * half + 2 : 2 * half + 3]], axis=1
     )
@@ -272,27 +329,34 @@
     once = jnp.sum(jnp.where(on_diagonal, once, 0.0), axis=0, keepdims=True)
     offset = jnp.sum(inverse * once, axis=1, keepdims=True) / scaler
     transform = jnp.sqrt((members - 1.0) / scaler) * inverse + offset
-    transform_ref[...] = transform
+    matrix_ref[...] = transform
+    copies = fetch((matrix_ref,), (transform_ref,), sems)
     transform = halves(transform)
-    block = 256
+    block = 128
     for start in range(0, state_ref.shape[0], block):
-        state = state_ref[start : start + block]
+        rows = pl.ds(start, block)
+        state = state_ref[rows]
         average = jnp.sum(state, axis=1, keepdims=True) * (1.0 / members)
-        analysis_ref[start : start + block] = average + dot3(halves(state - average), transform)
+        moved_ref[rows] = average + dot3(halves(state - average), transform)
+        sem = sems.at[pl.ds(1 + start // block, 1)]
+        copies += fetch((moved_ref.at[rows],), (analysis_ref.at[rows],), sem)
+    for copy in copies:
+        copy.wait()
 
 
 def finish(packed, state):
-    vmem = pl.BlockSpec(memory_space=pltpu.VMEM)
     members = state.shape[1]
-    return pl.pallas_call(
+    square = (members, members)
+    return on_core(
         finish_kernel,
-        out_shape=(
-            jax.ShapeDtypeStruct(state.shape, jnp.float32),
-            jax.ShapeDtypeStruct((members, members), jnp.float32),
-        ),
-        in_specs=[vmem, vmem],
-        out_specs=(vmem, vmem),
-        compiler_params=pltpu.CompilerParams(vmem_limit_bytes=VMEM_BYTES),
+        (state.shape, square),
+        [pltpu.VMEM] * 2,
+        [
+            pltpu.VMEM(state.shape, jnp.float32),
+            pltpu.VMEM(square, jnp.float32),
+            pltpu.SemaphoreType.DMA((1 + state.shape[0] // 128,)),
+        ],
+        pltpu.HBM,
     )(packed, state)
 
 
@@ -318,28 +382,60 @@
     turning = rotation * (2.0 * (rows.astype(jnp.float32) + 0.5) / total_lat - 1.0)
     lat_shape = (ROWS * lon + 8, members)
     lon_shape = (LON_ROWS + wide, members)
-    up, down, depth = on_core(
+    even = (lax.axis_index("lon") % 2 == 0).astype(jnp.int32).reshape(1)
+    first, second, depth = on_core(
         pack_lat_kernel,
         (lat_shape, lat_shape, (lat, 128)),
-        [vmem] * 2,
-        [pltpu.VMEM((128, 128), jnp.float32)],
-    )(ensemble, bathymetry)
-    low = shift_up(up, "lat", False)
-    high = shift_down(down, "lat", False)
+        [pltpu.SMEM] + [pltpu.HBM] * 2,
+        [
+            pltpu.VMEM(ensemble.shape, jnp.float32),
+            pltpu.VMEM(bathymetry.shape, jnp.int32),
+            pltpu.VMEM((128, 128), jnp.float32),
+            pltpu.SemaphoreType.DMA((2,)),
+        ],
+    )(even, in_hbm(ensemble), in_hbm(bathymetry))
+    pairs = [[], []]
+    last = lax.axis_size("lat") - 1
+    for a in range(lax.axis_size("lon")):
+        for b in range(last):
+            lower = a * (last + 1) + b
+            pairs[a % 2].append((lower, lower + 1))
+            pairs[1 - a % 2].append((lower + 1, lower))
+    first = lax.ppermute(first, ("lon", "lat"), pairs[0])
+    second = lax.ppermute(second, ("lon", "lat"), pairs[1])
     up, down, strip = on_core(
-        pack_lon_kernel, (lon_shape, lon_shape, (wide, 128)), [vmem] * 4, []
-    )(ensemble, low, high, depth)
+        pack_lon_kernel,
+        (lon_shape, lon_shape, (wide, 128)),
+        [pltpu.SMEM] + [vmem] * 4,
+        [],
+    )(even, ensemble, first, second, depth)
     west = shift_up(up, "lon", True)
     east = shift_down(down, "lon", True)
     planes = (fields, lon + 2 * REACH, wide, members)
     forecast, packed = on_core(
         step_kernel,
         ((fields * lon * lat, members), (members + 32, members // 2)),
-        [vmem] * 8 + [pltpu.SMEM] + [vmem] * 2,
+        [pltpu.SMEM] + [vmem] * 8 + [pltpu.HBM] * 3,
         [pltpu.VMEM(planes, jnp.float32)] * 2
         + [pltpu.VMEM((1,) + planes[1:], jnp.float32)]
-        + [pltpu.VMEM((obs_cell.shape[2], members), jnp.float32)],
-    )(ensemble, low, high, west, east, strip, turning, inside, obs_cell, obs_value, obs_weight)
+        + [pltpu.VMEM((obs_cell.shape[2], members), jnp.float32)]
+        + [pltpu.SMEM(obs_cell.shape, jnp.int32)]
+        + [pltpu.VMEM(obs_value.shape, jnp.float32)] * 2
+        + [pltpu.SemaphoreType.DMA((3,))],
+    )(
+        even,
+        ensemble,
+        first,
+        second,
+        west,
+        east,
+        strip,
+        turning,
+        inside,
+        in_hbm(obs_cell),
+        in_hbm(obs_value),
+        in_hbm(obs_weight),
+    )
     analysis, transform = finish(reduced(packed), forecast)
     return (analysis.reshape(ensemble.shape), transform)
 

time: 90.8 us -> 88.1 us (0.970)
  waiting for transfers between devices: 9.5 us -> 5.88 us
  local copies, waits for them, and re-layouts: 2.77 us -> 0.26 us
  starting transfers between devices: 14.4 us -> 16.9 us
    ppermute x0 -> x2, starting transfers between devices: none -> 6.29 us  [the longest x1 5 us: local(): second = lax.ppermute(second, ('lon', 'lat'), pairs[1])]
    ppermute x2 -> x1, waiting for transfers between devices: 8.47 us -> 3.56 us  [shift_down(): return lax.ppermute(block, axis, pairs)]
    ppermute x2 -> x1, starting transfers between devices: 10 us -> 7.01 us  [shift_up(): return lax.ppermute(block, axis, pairs)]
    unnamed x12 -> x2, local copies, waits for them, and re-layouts: 2.51 us -> 0.01 us
    ppermute x0 -> x2, waiting for transfers between devices: none -> 2.32 us  [the longest x1 1.48 us: local(): second = lax.ppermute(second, ('lon', 'lat'), pairs[1])]
    ppermute x2 -> x1, waiting for transfers between devices: 1.02 us -> 0.01 us  [shift_up(): return lax.ppermute(block, axis, pairs)]
    ppermute x2 -> x1, starting transfers between devices: 4.32 us -> 3.64 us  [shift_down(): return lax.ppermute(block, axis, pairs)]
where the time goes in v5:
time: 88.1 us; the launch traced here: 87.8 us
  blocking collectives  55.5 us (63%)
  starting transfers between devices  16.9 us (19%)
  Pallas kernels  8.28 us (9%)
  waiting for transfers between devices  5.88 us (7%)
    all_to_all x1, blocking collectives, reduced(): lax.all_to_all(jnp.broadcast_to(piece[None], (lat, 1, width)), 'lat', 0, 0)  23.5 us
    all_to_all x1, blocking collectives, reduced(): pieces = lax.all_to_all(packed.reshape(lon, 1, width), 'lon', 0, 0)  19.1 us
    all_to_all x1, blocking collectives, reduced(): lax.all_to_all(jnp.broadcast_to(piece[None], (lon, 1, width)), 'lon', 0, 0)  12.9 us
    ppermute x1, starting transfers between devices, shift_up(): return lax.ppermute(block, axis, pairs)  7.01 us
    pallas_call x1, Pallas kernels, finish(): on_core(finish_kernel, (state.shape, square), [pltpu.VMEM] * 2, [pltpu.VM...  5.08 us
    ppermute x1, starting transfers between devices, local(): second = lax.ppermute(second, ('lon', 'lat'), pairs[1])  5 us
    ppermute x1, starting transfers between devices, shift_down(): return lax.ppermute(block, axis, pairs)  3.64 us
    ppermute x1, waiting for transfers between devices, shift_down(): return lax.ppermute(block, axis, pairs)  3.56 us
  transfers between devices with their start and end apart: 4, of which 3 were waited for; matrix products, arithmetic and copies ran while one was open for 0% of the time, Pallas kernels for 0%

profile of v5, /device:TPU:1, one launch (start us, length us, event | category | flops | bytes accessed | tf_op | source)
XLA Modules:
  0.0 87.8 jit_solution(9033308734137572181)
XLA Ops:
  0.6 0.0 copy-start
  0.7 1.3 %shard_map.68 = (f32[168,256]{1,0:T(8,128)S(1)}, f32[168,256]{1,0:T(8,128)S(1)}, f32[16,128]{1,0:T(8,128)S(1)}) custom-call(s32[1]{0:T(128)} %bitcast.even_ref, f32[3,16,16,256]{3,2,1,0:T(8,128)} %state_ref.3, s32[16,16]{1,0:T(8,128)} %bathymetry_ref.1), custom_call_target="tpu_custom_call" | custom-call | tf_op jit(solution)/shard_map/pallas_call | solution.py:386
  2.0 1.3 %collective-permute-start = (f32[168,256]{1,0:T(8,128)S(1)}, f32[168,256]{1,0:T(8,128)S(1)}, u32[]{:S(2)}, u32[]{:S(2)}) collective-permute-start(f32[168,256]{1,0:T(8,128)S(1)} %get-tuple-element.12), channel_id=1, source_target_pairs={{0,1},{1,2},{2,3},{3,4},{4,5},{5,6},{6,7},{7,8},{8,9},{9,10},{10,1... | collective-permute-start | bytes 516104 | tf_op jit(solution)/shard_map/ppermute | solution.py:404
  3.3 5.0 %collective-permute-start.1 = (f32[168,256]{1,0:T(8,128)S(1)}, f32[168,256]{1,0:T(8,128)S(1)}, u32[]{:S(2)}, u32[]{:S(2)}) collective-permute-start(f32[168,256]{1,0:T(8,128)S(1)} %get-tuple-element.13), channel_id=1, source_target_pairs={{1,0},{2,1},{3,2},{4,3},{5,4},{6,5},{7,6},{8,7},{9,8},{10,9},{11,1... | collective-permute-start | bytes 516104 | tf_op jit(solution)/shard_map/ppermute | solution.py:405
  8.3 0.8 collective-permute-done.first_ref
  9.1 1.5 %collective-permute-done.1.second_ref = f32[168,256]{1,0:T(8,128)S(1)} collective-permute-done((f32[168,256]{1,0:T(8,128)S(1)}, f32[168,256]{1,0:T(8,128)S(1)}, u32[]{:S(2)}, u32[]{:S(2)}) %collective-permute-start.1) | collective-permute-done | bytes 172064 | tf_op jit(solution)/shard_map/ppermute | solution.py:405
  10.6 0.0 copy-done
  10.6 0.1 shard_map.69
  10.7 7.0 %collective-permute-start.2 = (f32[216,256]{1,0:T(8,128)S(1)}, f32[216,256]{1,0:T(8,128)S(1)}, u32[]{:S(2)}, u32[]{:S(2)}) collective-permute-start(f32[216,256]{1,0:T(8,128)S(1)} %get-tuple-element.15), channel_id=1, source_target_pairs={{0,16},{16,32},{32,48},{48,64},{64,80},{80,96},{96,112},{112,128},... | collective-permute-start | bytes 663560 | tf_op jit(solution)/shard_map/ppermute | solution.py:30
  17.7 3.6 %collective-permute-start.3 = (f32[216,256]{1,0:T(8,128)S(1)}, f32[216,256]{1,0:T(8,128)S(1)}, u32[]{:S(2)}, u32[]{:S(2)}) collective-permute-start(f32[216,256]{1,0:T(8,128)S(1)} %get-tuple-element.16), channel_id=1, source_target_pairs={{16,0},{32,16},{48,32},{64,48},{80,64},{96,80},{112,96},{128,112},... | collective-permute-start | bytes 663560 | tf_op jit(solution)/shard_map/ppermute | solution.py:38
  21.4 0.0 collective-permute-done.2.west_ref
  21.4 3.6 %collective-permute-done.3.east_ref = f32[216,256]{1,0:T(8,128)S(1)} collective-permute-done((f32[216,256]{1,0:T(8,128)S(1)}, f32[216,256]{1,0:T(8,128)S(1)}, u32[]{:S(2)}, u32[]{:S(2)}) %collective-permute-start.3) | collective-permute-done | bytes 221216 | tf_op jit(solution)/shard_map/ppermute | solution.py:38
  24.9 0.1 iota.9.turning_ref
  25.0 0.1 iota.10.inside_ref
  25.1 1.8 %shard_map.70 = (f32[768,256]{1,0:T(8,128)S(1)}, f32[288,128]{1,0:T(8,128)S(1)}) custom-call(s32[1]{0:T(128)} %bitcast.even_ref, f32[3,16,16,256]{3,2,1,0:T(8,128)S(1)} %copy-done, f32[168,256]{1,0:T(8,128)S(1)} %collective-permute-done.first_ref, f32[168,256]{1,0:T(8,128)S(1)} %collective-permute-done.1.second_ref, ...), custom_call_target="tpu_custom_call" | custom-call | tf_op jit(solution)/shard_map/pallas_call | solution.py:415
  26.9 19.1 %all_to_all.15 = f32[32,1,1152]{2,1,0:T(1,128)S(1)} all-to-all(f32[32,1,1152]{2,1,0:T(1,128)S(1)} %bitcast.5), channel_id=1, replica_groups=mesh['lon'=32,'lat'=16] {'lon'}, dimensions={0} | all-to-all | bytes 294912 | tf_op jit(solution)/shard_map/all_to_all | solution.py:367
  46.0 0.1 reduce_sum.18
  46.2 23.5 %all_to_all.16 = f32[16,1,1152]{2,1,0:T(1,128)S(1)} all-to-all(f32[16,1,1152]{2,1,0:T(1,128)S(1)} %broadcast_in_dim.4), channel_id=1, replica_groups=mesh['lon'=32,'lat'=16] {'lat'}, dimensions={0} | all-to-all | bytes 147456 | tf_op jit(solution)/shard_map/all_to_all | solution.py:369
  69.7 0.1 reduce_sum.19
  69.7 0.1 broadcast_in_dim.5
  69.8 12.9 %all_to_all.17 = f32[32,1,1152]{2,1,0:T(1,128)S(1)} all-to-all(f32[32,1,1152]{2,1,0:T(1,128)S(1)} %broadcast_in_dim.5), channel_id=1, replica_groups=mesh['lon'=32,'lat'=16] {'lon'}, dimensions={0} | all-to-all | bytes 294912 | tf_op jit(solution)/shard_map/all_to_all | solution.py:371
  82.7 5.1 %shard_map.71 = (f32[768,256]{1,0:T(8,128)}, f32[256,256]{1,0:T(8,128)}) custom-call(f32[288,128]{1,0:T(8,128)S(1)} %bitcast.4, f32[768,256]{1,0:T(8,128)S(1)} %get-tuple-element.19.state_ref), custom_call_target="tpu_custom_call" | custom-call | tf_op jit(solution)/shard_map/pallas_call | solution.py:350
  (3 shorter events, 0.1 us)
Async XLA Ops:
  0.6 10.0 %copy-start = (f32[3,16,16,256]{3,2,1,0:T(8,128)S(1)}, f32[3,16,16,256]{3,2,1,0:T(8,128)}, u32[]{:S(2)}) copy-start(f32[3,16,16,256]{3,2,1,0:T(8,128)} %state_ref.3) | copy-start | bytes 2359300
  2.0 7.2 %collective-permute-start = (f32[168,256]{1,0:T(8,128)S(1)}, f32[168,256]{1,0:T(8,128)S(1)}, u32[]{:S(2)}, u32[]{:S(2)}) collective-permute-start(f32[168,256]{1,0:T(8,128)S(1)} %get-tuple-element.12), channel_id=1, source_target_pairs={{0,1},{1,2},{2,3},{3,4},{4,5},{5,6},{6,7},{7,8},{8,9},{9,10},{10,1... | collective-permute-start | bytes 516104 | tf_op jit(solution)/shard_map/ppermute | solution.py:404
  3.3 7.3 %collective-permute-start.1 = (f32[168,256]{1,0:T(8,128)S(1)}, f32[168,256]{1,0:T(8,128)S(1)}, u32[]{:S(2)}, u32[]{:S(2)}) collective-permute-start(f32[168,256]{1,0:T(8,128)S(1)} %get-tuple-element.13), channel_id=1, source_target_pairs={{1,0},{2,1},{3,2},{4,3},{5,4},{6,5},{7,6},{8,7},{9,8},{10,9},{11,1... | collective-permute-start | bytes 516104 | tf_op jit(solution)/shard_map/ppermute | solution.py:405
  10.7 10.7 %collective-permute-start.2 = (f32[216,256]{1,0:T(8,128)S(1)}, f32[216,256]{1,0:T(8,128)S(1)}, u32[]{:S(2)}, u32[]{:S(2)}) collective-permute-start(f32[216,256]{1,0:T(8,128)S(1)} %get-tuple-element.15), channel_id=1, source_target_pairs={{0,16},{16,32},{32,48},{48,64},{64,80},{80,96},{96,112},{112,128},... | collective-permute-start | bytes 663560 | tf_op jit(solution)/shard_map/ppermute | solution.py:30
  17.7 7.3 %collective-permute-start.3 = (f32[216,256]{1,0:T(8,128)S(1)}, f32[216,256]{1,0:T(8,128)S(1)}, u32[]{:S(2)}, u32[]{:S(2)}) collective-permute-start(f32[216,256]{1,0:T(8,128)S(1)} %get-tuple-element.16), channel_id=1, source_target_pairs={{16,0},{32,16},{48,32},{64,48},{80,64},{96,80},{112,96},{128,112},... | collective-permute-start | bytes 663560 | tf_op jit(solution)/shard_map/ppermute | solution.py:38

commit v6 on v5

--- a/solution.py
+++ b/solution.py
@@ -22,22 +22,6 @@
 rotation = 0.3
 
 
-def shift_up(block, axis, wrap):
-    count = lax.axis_size(axis)
-    pairs = [(i, i + 1) for i in range(count - 1)]
-    if wrap:
-        pairs.append((count - 1, 0))
-    return lax.ppermute(block, axis, pairs)
-
-
-def shift_down(block, axis, wrap):
-    count = lax.axis_size(axis)
-    pairs = [(i + 1, i) for i in range(count - 1)]
-    if wrap:
-        pairs.append((0, count - 1))
-    return lax.ppermute(block, axis, pairs)
-
-
 def fetch(sources, targets, sems):
     copies = [
         pltpu.make_async_copy(source, target, sems.at[k])
@@ -49,7 +33,7 @@
 
 
 def pack_lat_kernel(
-    even_ref, ensemble_ref, bathymetry_ref, first_ref, second_ref, depth_ref, state_ref, bottom_ref, square_ref, sems
+    parity_ref, ensemble_ref, bathymetry_ref, first_ref, second_ref, depth_ref, state_ref, bottom_ref, square_ref, sems
 ):
     lon, lat = state_ref.shape[1], state_ref.shape[2]
     copies = fetch((bathymetry_ref, ensemble_ref), (bottom_ref, state_ref), sems)
@@ -73,11 +57,11 @@
                 up_ref[at : at + count] = plane[lat - count :]
                 down_ref[at : at + count] = plane[:count]
 
-    @pl.when(even_ref[0] == 1)
+    @pl.when(parity_ref[0] & 1 == 0)
     def _():
         pack(first_ref, second_ref)
 
-    @pl.when(even_ref[0] != 1)
+    @pl.when(parity_ref[0] & 1 == 1)
     def _():
         pack(second_ref, first_ref)
 
@@ -101,30 +85,40 @@
 
 
 def pack_lon_kernel(
-    even_ref, state_ref, first_ref, second_ref, depth_ref, up_ref, down_ref, strip_ref
+    parity_ref, state_ref, first_ref, second_ref, depth_ref, across_ref, within_ref, strip_ref
 ):
     lon = state_ref.shape[1]
-    even = even_ref[0] == 1
-    low_rows = functools.partial(lat_rows, even, first_ref, second_ref)
-    high_rows = functools.partial(lat_rows, even, second_ref, first_ref)
+    even = parity_ref[0] & 1 == 0
+    low_rows = functools.partial(lat_rows, even, second_ref, first_ref)
+    high_rows = functools.partial(lat_rows, even, first_ref, second_ref)
     depth_at = ROWS * lon
     strip_ref[...] = jnp.zeros_like(strip_ref)
     depths = slice(depth_at, depth_at + 3)
-    strip_ref[1:4] = chosen(even, first_ref, second_ref, depths, slice(0, 128))
+    strip_ref[1:4] = chosen(even, second_ref, first_ref, depths, slice(0, 128))
     strip_ref[4:20] = depth_ref[...]
-    strip_ref[20:23] = chosen(even, second_ref, first_ref, depths, slice(0, 128))
-    for ref in (up_ref, down_ref):
+    strip_ref[20:23] = chosen(even, first_ref, second_ref, depths, slice(0, 128))
+    for ref in (across_ref, within_ref):
         ref[LON_ROWS:, 128:] = jnp.zeros((ref.shape[0] - LON_ROWS, 128), jnp.float32)
         ref[LON_ROWS - 2 : LON_ROWS] = jnp.zeros((2, ref.shape[1]), jnp.float32)
         ref[LON_ROWS:, :128] = strip_ref[...]
-    for field, distance, beyond, at in lon_layout():
-        for ref, x in ((up_ref, lon - distance), (down_ref, distance - 1)):
-            if beyond:
-                low = low_rows(field, x, lon)
-                ref[at : at + beyond] = low[LAT_ROWS[field] - beyond :]
-                high = high_rows(field, x, lon)
-                ref[at + beyond + TILE : at + TILE + 2 * beyond] = high[:beyond]
-            ref[at + beyond : at + beyond + TILE] = state_ref[field, x]
+
+    def pack(up_ref, down_ref):
+        for field, distance, beyond, at in lon_layout():
+            for ref, x in ((up_ref, lon - distance), (down_ref, distance - 1)):
+                if beyond:
+                    low = low_rows(field, x, lon)
+                    ref[at : at + beyond] = low[LAT_ROWS[field] - beyond :]
+                    high = high_rows(field, x, lon)
+                    ref[at + beyond + TILE : at + TILE + 2 * beyond] = high[:beyond]
+                ref[at + beyond : at + beyond + TILE] = state_ref[field, x]
+
+    @pl.when(parity_ref[0] < 2)
+    def _():
+        pack(within_ref, across_ref)
+
+    @pl.when(parity_ref[0] >= 2)
+    def _():
+        pack(across_ref, within_ref)
 
 
 def dot3_first(left, right):
@@ -136,12 +130,12 @@
 
 
 def step_kernel(
-    even_ref,
+    parity_ref,
     state_ref,
     first_ref,
     second_ref,
-    west_ref,
-    east_ref,
+    across_ref,
+    within_ref,
     strip_ref,
     turning_ref,
     inside_ref,
@@ -163,9 +157,12 @@
         (obs_cell_ref, obs_value_ref, obs_weight_ref), (cell_ref, value_ref, weight_ref), sems
     )
     lon = state_ref.shape[1]
-    even = even_ref[0] == 1
-    low_rows = functools.partial(lat_rows, even, first_ref, second_ref)
-    high_rows = functools.partial(lat_rows, even, second_ref, first_ref)
+    even = parity_ref[0] & 1 == 0
+    even_lon = parity_ref[0] < 2
+    west = functools.partial(chosen, even_lon, across_ref, within_ref)
+    east = functools.partial(chosen, even_lon, within_ref, across_ref)
+    low_rows = functools.partial(lat_rows, even, second_ref, first_ref)
+    high_rows = functools.partial(lat_rows, even, first_ref, second_ref)
     members = state_ref.shape[3]
     wide = TILE + 2 * REACH
     for field, count in enumerate(LAT_ROWS):
@@ -178,19 +175,23 @@
     for field, distance, beyond, at in lon_layout():
         rows = slice(REACH - beyond, REACH + TILE + beyond)
         taken = slice(at, at + TILE + 2 * beyond)
-        field_ref[field, REACH - distance, rows] = west_ref[taken]
-        field_ref[field, REACH + lon - 1 + distance, rows] = east_ref[taken]
+        field_ref[field, REACH - distance, rows] = west(taken)
+        field_ref[field, REACH + lon - 1 + distance, rows] = east(taken)
     turning = time_step * jnp.broadcast_to(turning_ref[:, :1], (wide, members))
     keeper = jnp.broadcast_to(inside_ref[:, :1], (wide, members))
     pull = 0.5 * time_step * gravity
 
+    west_depth = west(slice(LON_ROWS, None), slice(0, 128))
+    east_depth = east(slice(LON_ROWS, None), slice(0, 128))
+    middle_depth = strip_ref[...]
+
     def column(x):
         if x < REACH:
-            depth = west_ref[LON_ROWS:, lon - REACH + x : lon - REACH + x + 1]
+            depth = west_depth[:, lon - REACH + x : lon - REACH + x + 1]
         elif x < REACH + lon:
-            depth = strip_ref[:, x - REACH : x - REACH + 1]
+            depth = middle_depth[:, x - REACH : x - REACH + 1]
         else:
-            depth = east_ref[LON_ROWS:, x - REACH - lon : x - REACH - lon + 1]
+            depth = east_depth[:, x - REACH - lon : x - REACH - lon + 1]
         return jnp.broadcast_to(0.5 * time_step * depth, (wide, members))
 
     def along(plane):
@@ -382,7 +383,9 @@
     turning = rotation * (2.0 * (rows.astype(jnp.float32) + 0.5) / total_lat - 1.0)
     lat_shape = (ROWS * lon + 8, members)
     lon_shape = (LON_ROWS + wide, members)
-    even = (lax.axis_index("lon") % 2 == 0).astype(jnp.int32).reshape(1)
+    here = lax.axis_index("lon")
+    parity = ((here + lax.axis_index("lat")) & 1) + 2 * (here & 1)
+    parity = parity.reshape(1)
     first, second, depth = on_core(
         pack_lat_kernel,
         (lat_shape, lat_shape, (lat, 128)),
@@ -393,24 +396,27 @@
             pltpu.VMEM((128, 128), jnp.float32),
             pltpu.SemaphoreType.DMA((2,)),
         ],
-    )(even, in_hbm(ensemble), in_hbm(bathymetry))
-    pairs = [[], []]
-    last = lax.axis_size("lat") - 1
-    for a in range(lax.axis_size("lon")):
-        for b in range(last):
-            lower = a * (last + 1) + b
-            pairs[a % 2].append((lower, lower + 1))
-            pairs[1 - a % 2].append((lower + 1, lower))
+    )(parity, in_hbm(ensemble), in_hbm(bathymetry))
+    across, within = [], []
+    columns = lax.axis_size("lon")
+    rows_of = lax.axis_size("lat")
+    pairs = ([], [])
+    for a in range(columns):
+        for b in range(rows_of):
+            ours = a * rows_of + b
+            if b + 1 < rows_of:
+                pairs[(a + b) % 2].extend(((ours, ours + 1), (ours + 1, ours)))
+        (across if a % 2 else within).extend(((a, (a + 1) % columns), ((a + 1) % columns, a)))
     first = lax.ppermute(first, ("lon", "lat"), pairs[0])
     second = lax.ppermute(second, ("lon", "lat"), pairs[1])
-    up, down, strip = on_core(
+    out_across, out_within, strip = on_core(
         pack_lon_kernel,
         (lon_shape, lon_shape, (wide, 128)),
         [pltpu.SMEM] + [vmem] * 4,
         [],
-    )(even, ensemble, first, second, depth)
-    west = shift_up(up, "lon", True)
-    east = shift_down(down, "lon", True)
+    )(parity, ensemble, first, second, depth)
+    across = lax.ppermute(out_across, "lon", across)
+    within = lax.ppermute(out_within, "lon", within)
     planes = (fields, lon + 2 * REACH, wide, members)
     forecast, packed = on_core(
         step_kernel,
@@ -423,12 +429,12 @@
         + [pltpu.VMEM(obs_value.shape, jnp.float32)] * 2
         + [pltpu.SemaphoreType.DMA((3,))],
     )(
-        even,
+        parity,
         ensemble,
         first,
         second,
-        west,
-        east,
+        across,
+        within,
         strip,
         turning,
         inside,

time: 88.1 us -> 84.4 us (0.958)
  blocking collectives: 55.5 us -> 53.2 us
  waiting for transfers between devices: 5.88 us -> 4.18 us
    all_to_all x1, blocking collectives: 19.1 us -> 14.6 us  [reduced(): pieces = lax.all_to_all(packed.reshape(lon, 1, width), 'lon', 0, 0)]
    ppermute x2, waiting for transfers between devices: 3.57 us -> 1.05 us  [the longest x1 1.04 us: local(): within = lax.ppermute(out_within, 'lon', within)]
    ppermute x1, starting transfers between devices: 5 us -> 7.24 us  [local(): second = lax.ppermute(second, ('lon', 'lat'), pairs[1])]
    all_to_all x1, blocking collectives: 23.5 us -> 25.7 us  [reduced(): lax.all_to_all(jnp.broadcast_to(piece[None], (lat, 1, width)), 'lat', 0, 0)]
    ppermute x2, starting transfers between devices: 10.7 us -> 8.78 us  [the longest x1 6.85 us: local(): within = lax.ppermute(out_within, 'lon', within)]
    ppermute x1, waiting for transfers between devices: 1.48 us -> 3.13 us  [local(): second = lax.ppermute(second, ('lon', 'lat'), pairs[1])]
  transfers between devices with their start and end apart: 4 -> 4, of which waited for: 3 -> 2; matrix products, arithmetic and copies ran while one was open for 0% -> 0% of each run, Pallas kernels for 0% -> 0%
where the time goes in v6:
time: 84.4 us; the launch traced here: 84.1 us
  blocking collectives  53.2 us (63%)
  starting transfers between devices  16.7 us (20%)
  Pallas kernels  8.81 us (10%)
  waiting for transfers between devices  4.18 us (5%)
    all_to_all x1, blocking collectives, reduced(): lax.all_to_all(jnp.broadcast_to(piece[None], (lat, 1, width)), 'lat', 0, 0)  25.7 us
    all_to_all x1, blocking collectives, reduced(): pieces = lax.all_to_all(packed.reshape(lon, 1, width), 'lon', 0, 0)  14.6 us
    all_to_all x1, blocking collectives, reduced(): lax.all_to_all(jnp.broadcast_to(piece[None], (lon, 1, width)), 'lon', 0, 0)  12.9 us
    ppermute x1, starting transfers between devices, local(): second = lax.ppermute(second, ('lon', 'lat'), pairs[1])  7.24 us
    ppermute x1, starting transfers between devices, local(): within = lax.ppermute(out_within, 'lon', within)  6.85 us
    pallas_call x1, Pallas kernels, finish(): on_core(finish_kernel, (state.shape, square), [pltpu.VMEM] * 2, [pltpu.VM...  5.08 us
    ppermute x1, waiting for transfers between devices, local(): second = lax.ppermute(second, ('lon', 'lat'), pairs[1])  3.13 us
    pallas_call x1, Pallas kernels, local(): on_core(step_kernel, ((fields * lon * lat, members), (members + 32, membe...  2.34 us
  transfers between devices with their start and end apart: 4, of which 2 were waited for; matrix products, arithmetic and copies ran while one was open for 0% of the time, Pallas kernels for 0%

profile of v6, /device:TPU:1, one launch (start us, length us, event | category | flops | bytes accessed | tf_op | source)
XLA Modules:
  0.0 84.1 jit_solution(10660086133963237010)
XLA Ops:
  0.6 0.0 copy-start
  0.6 1.3 %shard_map.68 = (f32[168,256]{1,0:T(8,128)S(1)}, f32[168,256]{1,0:T(8,128)S(1)}, f32[16,128]{1,0:T(8,128)S(1)}) custom-call(s32[1]{0:T(128)} %bitcast.parity_ref, f32[3,16,16,256]{3,2,1,0:T(8,128)} %state_ref.3, s32[16,16]{1,0:T(8,128)} %bathymetry_ref.1), custom_call_target="tpu_custom_call" | custom-call | tf_op jit(solution)/shard_map/pallas_call | solution.py:389
  2.0 0.7 collective-permute-start
  2.6 7.2 %collective-permute-start.1 = (f32[168,256]{1,0:T(8,128)S(1)}, f32[168,256]{1,0:T(8,128)S(1)}, u32[]{:S(2)}, u32[]{:S(2)}) collective-permute-start(f32[168,256]{1,0:T(8,128)S(1)} %get-tuple-element.13), channel_id=1, source_target_pairs={{1,2},{2,1},{3,4},{4,3},{5,6},{6,5},{7,8},{8,7},{9,10},{10,9},{11,... | collective-permute-start | bytes 516104 | tf_op jit(solution)/shard_map/ppermute | solution.py:411
  9.9 0.0 collective-permute-done.first_ref
  9.9 3.1 %collective-permute-done.1.second_ref = f32[168,256]{1,0:T(8,128)S(1)} collective-permute-done((f32[168,256]{1,0:T(8,128)S(1)}, f32[168,256]{1,0:T(8,128)S(1)}, u32[]{:S(2)}, u32[]{:S(2)}) %collective-permute-start.1) | collective-permute-done | bytes 172064 | tf_op jit(solution)/shard_map/ppermute | solution.py:411
  13.0 0.0 copy-done
  13.0 0.1 shard_map.69
  13.1 1.9 %collective-permute-start.2 = (f32[216,256]{1,0:T(8,128)S(1)}, f32[216,256]{1,0:T(8,128)S(1)}, u32[]{:S(2)}, u32[]{:S(2)}) collective-permute-start(f32[216,256]{1,0:T(8,128)S(1)} %get-tuple-element.15), channel_id=1, source_target_pairs={{16,32},{32,16},{48,64},{64,48},{80,96},{96,80},{112,128},{128,112... | collective-permute-start | bytes 663560 | tf_op jit(solution)/shard_map/ppermute | solution.py:418
  15.0 6.9 %collective-permute-start.3 = (f32[216,256]{1,0:T(8,128)S(1)}, f32[216,256]{1,0:T(8,128)S(1)}, u32[]{:S(2)}, u32[]{:S(2)}) collective-permute-start(f32[216,256]{1,0:T(8,128)S(1)} %get-tuple-element.16), channel_id=1, source_target_pairs={{0,16},{16,0},{32,48},{48,32},{64,80},{80,64},{96,112},{112,96},{1... | collective-permute-start | bytes 663560 | tf_op jit(solution)/shard_map/ppermute | solution.py:419
  21.9 0.0 collective-permute-done.2.across_ref
  21.9 1.0 %collective-permute-done.3.within_ref = f32[216,256]{1,0:T(8,128)S(1)} collective-permute-done((f32[216,256]{1,0:T(8,128)S(1)}, f32[216,256]{1,0:T(8,128)S(1)}, u32[]{:S(2)}, u32[]{:S(2)}) %collective-permute-start.3) | collective-permute-done | bytes 221216 | tf_op jit(solution)/shard_map/ppermute | solution.py:419
  23.0 0.1 iota.9.turning_ref
  23.1 0.1 iota.10.inside_ref
  23.1 2.3 %shard_map.70 = (f32[768,256]{1,0:T(8,128)S(1)}, f32[288,128]{1,0:T(8,128)S(1)}) custom-call(s32[1]{0:T(128)} %bitcast.parity_ref, f32[3,16,16,256]{3,2,1,0:T(8,128)S(1)} %copy-done, f32[168,256]{1,0:T(8,128)S(1)} %collective-permute-done.first_ref, f32[168,256]{1,0:T(8,128)S(1)} %collective-permute-done.1.second_ref, ...), custom_call_target="tpu_custom_call" | custom-call | tf_op jit(solution)/shard_map/pallas_call | solution.py:421
  25.5 14.6 %all_to_all.15 = f32[32,1,1152]{2,1,0:T(1,128)S(1)} all-to-all(f32[32,1,1152]{2,1,0:T(1,128)S(1)} %bitcast.5), channel_id=1, replica_groups=mesh['lon'=32,'lat'=16] {'lon'}, dimensions={0} | all-to-all | bytes 294912 | tf_op jit(solution)/shard_map/all_to_all | solution.py:368
  40.1 0.1 reduce_sum.18
  40.3 25.7 %all_to_all.16 = f32[16,1,1152]{2,1,0:T(1,128)S(1)} all-to-all(f32[16,1,1152]{2,1,0:T(1,128)S(1)} %broadcast_in_dim.4), channel_id=1, replica_groups=mesh['lon'=32,'lat'=16] {'lat'}, dimensions={0} | all-to-all | bytes 147456 | tf_op jit(solution)/shard_map/all_to_all | solution.py:370
  66.0 0.1 reduce_sum.19
  66.0 0.1 broadcast_in_dim.5
  66.1 12.9 %all_to_all.17 = f32[32,1,1152]{2,1,0:T(1,128)S(1)} all-to-all(f32[32,1,1152]{2,1,0:T(1,128)S(1)} %broadcast_in_dim.5), channel_id=1, replica_groups=mesh['lon'=32,'lat'=16] {'lon'}, dimensions={0} | all-to-all | bytes 294912 | tf_op jit(solution)/shard_map/all_to_all | solution.py:372
  79.0 5.1 %shard_map.71 = (f32[768,256]{1,0:T(8,128)}, f32[256,256]{1,0:T(8,128)}) custom-call(f32[288,128]{1,0:T(8,128)S(1)} %bitcast.4, f32[768,256]{1,0:T(8,128)S(1)} %get-tuple-element.19.state_ref), custom_call_target="tpu_custom_call" | custom-call | tf_op jit(solution)/shard_map/pallas_call | solution.py:351
  (3 shorter events, 0.1 us)
Async XLA Ops:
  0.6 12.4 %copy-start = (f32[3,16,16,256]{3,2,1,0:T(8,128)S(1)}, f32[3,16,16,256]{3,2,1,0:T(8,128)}, u32[]{:S(2)}) copy-start(f32[3,16,16,256]{3,2,1,0:T(8,128)} %state_ref.3) | copy-start | bytes 2359300
  2.0 7.9 %collective-permute-start = (f32[168,256]{1,0:T(8,128)S(1)}, f32[168,256]{1,0:T(8,128)S(1)}, u32[]{:S(2)}, u32[]{:S(2)}) collective-permute-start(f32[168,256]{1,0:T(8,128)S(1)} %get-tuple-element.12), channel_id=1, source_target_pairs={{0,1},{1,0},{2,3},{3,2},{4,5},{5,4},{6,7},{7,6},{8,9},{9,8},{10,11... | collective-permute-start | bytes 516104 | tf_op jit(solution)/shard_map/ppermute | solution.py:410
  2.6 10.4 %collective-permute-start.1 = (f32[168,256]{1,0:T(8,128)S(1)}, f32[168,256]{1,0:T(8,128)S(1)}, u32[]{:S(2)}, u32[]{:S(2)}) collective-permute-start(f32[168,256]{1,0:T(8,128)S(1)} %get-tuple-element.13), channel_id=1, source_target_pairs={{1,2},{2,1},{3,4},{4,3},{5,6},{6,5},{7,8},{8,7},{9,10},{10,9},{11,... | collective-permute-start | bytes 516104 | tf_op jit(solution)/shard_map/ppermute | solution.py:411
  13.1 8.8 %collective-permute-start.2 = (f32[216,256]{1,0:T(8,128)S(1)}, f32[216,256]{1,0:T(8,128)S(1)}, u32[]{:S(2)}, u32[]{:S(2)}) collective-permute-start(f32[216,256]{1,0:T(8,128)S(1)} %get-tuple-element.15), channel_id=1, source_target_pairs={{16,32},{32,16},{48,64},{64,48},{80,96},{96,80},{112,128},{128,112... | collective-permute-start | bytes 663560 | tf_op jit(solution)/shard_map/ppermute | solution.py:418
  15.0 7.9 %collective-permute-start.3 = (f32[216,256]{1,0:T(8,128)S(1)}, f32[216,256]{1,0:T(8,128)S(1)}, u32[]{:S(2)}, u32[]{:S(2)}) collective-permute-start(f32[216,256]{1,0:T(8,128)S(1)} %get-tuple-element.16), channel_id=1, source_target_pairs={{0,16},{16,0},{32,48},{48,32},{64,80},{80,64},{96,112},{112,96},{1... | collective-permute-start | bytes 663560 | tf_op jit(solution)/shard_map/ppermute | solution.py:419

commit v7 on v6

--- a/solution.py
+++ b/solution.py
@@ -123,22 +123,123 @@
 
 def dot3_first(left, right):
     dims = (((0,), (0,)), ((), ()))
-    dot = functools.partial(lax.dot_general, dimension_numbers=dims, preferred_element_type=jnp.float32)
     left_high, left_low = left
     right_high, right_low = right
-    return dot(left_high, right_high) + (dot(left_high, right_low) + dot(left_low, right_high))
-
-
-def step_kernel(
+    return lax.dot_general(
+        jnp.concatenate([left_high, left_high, left_low]),
+        jnp.concatenate([right_high, right_low, right_high]),
+        dims,
+        preferred_element_type=jnp.float32,
+    )
+
+
+def along(plane):
+    return pltpu.roll(plane, plane.shape[0] - 1, 0) - pltpu.roll(plane, 1, 0)
+
+
+def advance_height(source, depth, x):
+    spread = source(1, x + 1) - source(1, x - 1) + along(source(2, x))
+    return source(0, x) - depth(x) * spread
+
+
+def advance_flow(source, height, turning, x):
+    pull = 0.5 * time_step * gravity
+    east = source(1, x)
+    north = source(2, x)
+    slope_east = height(x + 1) - height(x - 1)
+    slope_north = along(height(x))
+    return (
+        east + (turning * north - pull * slope_east),
+        north - (turning * east + pull * slope_north),
+    )
+
+
+def spread_out(column, shape):
+    return jnp.broadcast_to(column, shape)
+
+
+HANDED = ((4, 5, 18, 19),) * 3 + ((5, 6, 17, 18),) + ((6, 7, 16, 17),) * 2 + ((7, 8, 15, 16),)
+
+
+def inner_kernel(
     parity_ref,
     state_ref,
     first_ref,
     second_ref,
+    strip_ref,
+    turning_ref,
+    inside_ref,
+    inner_ref,
+    handed_ref,
+    field_ref,
+    next_ref,
+    last_ref,
+):
+    lon = state_ref.shape[1]
+    shape = field_ref.shape[2:]
+    even = parity_ref[0] & 1 == 0
+    low_rows = functools.partial(lat_rows, even, second_ref, first_ref)
+    high_rows = functools.partial(lat_rows, even, first_ref, second_ref)
+    for field, count in enumerate(LAT_ROWS):
+        for x in range(lon):
+            field_ref[field, x, REACH : REACH + TILE] = state_ref[field, x]
+            field_ref[field, x, REACH - count : REACH] = low_rows(field, x, lon)
+            field_ref[field, x, REACH + TILE : REACH + TILE + count] = high_rows(field, x, lon)
+    turning = time_step * spread_out(turning_ref[:, :1], shape)
+    keeper = spread_out(inside_ref[:, :1], shape)
+    strip = 0.5 * time_step * strip_ref[...]
+    end = lon + 2 * REACH
+
+    def depth(x):
+        return spread_out(strip[:, x - REACH : x - REACH + 1], shape)
+
+    def source(field, x):
+        return field_ref[field, x - REACH]
+
+    def after(field, x):
+        return next_ref[field, x - REACH]
+
+    def height(x):
+        return next_ref[0, x - REACH]
+
+    def last_height(x):
+        return last_ref[0, x - REACH]
+
+    for x in range(REACH + 1, end - REACH - 1):
+        next_ref[0, x - REACH] = advance_height(source, depth, x)
+    for x in range(REACH + 2, end - REACH - 2):
+        east, north = advance_flow(source, height, turning, x)
+        next_ref[1, x - REACH] = east
+        next_ref[2, x - REACH] = north * keeper
+    for x in range(REACH + 3, end - REACH - 3):
+        last_ref[0, x - REACH] = advance_height(after, depth, x)
+    for x in range(2 * REACH, end - 2 * REACH):
+        east, north = advance_flow(after, last_height, turning, x)
+        for field, plane in enumerate((last_height(x), east, north)):
+            inner_ref[field, x - 2 * REACH] = plane[REACH : REACH + TILE]
+    kinds = (
+        functools.partial(source, 0),
+        functools.partial(source, 1),
+        functools.partial(source, 2),
+        height,
+        functools.partial(after, 1),
+        functools.partial(after, 2),
+        last_height,
+    )
+    for kind, (columns, plane) in enumerate(zip(HANDED, kinds)):
+        for k, x in enumerate(columns):
+            handed_ref[kind, k] = plane(x)
+
+
+def step_kernel(
+    parity_ref,
     across_ref,
     within_ref,
     strip_ref,
     turning_ref,
     inside_ref,
+    inner_ref,
+    handed_ref,
     obs_cell_ref,
     obs_value_ref,
     obs_weight_ref,
@@ -156,74 +257,78 @@
     copies = fetch(
         (obs_cell_ref, obs_value_ref, obs_weight_ref), (cell_ref, value_ref, weight_ref), sems
     )
-    lon = state_ref.shape[1]
-    even = parity_ref[0] & 1 == 0
+    shape = field_ref.shape[2:]
+    members = shape[1]
+    end = next_ref.shape[1]
+    lon = end - 2 * REACH
     even_lon = parity_ref[0] < 2
     west = functools.partial(chosen, even_lon, across_ref, within_ref)
     east = functools.partial(chosen, even_lon, within_ref, across_ref)
-    low_rows = functools.partial(lat_rows, even, second_ref, first_ref)
-    high_rows = functools.partial(lat_rows, even, first_ref, second_ref)
-    members = state_ref.shape[3]
-    wide = TILE + 2 * REACH
-    for field, count in enumerate(LAT_ROWS):
-        for x in range(lon):
-            field_ref[field, REACH + x, REACH : REACH + TILE] = state_ref[field, x]
-            field_ref[field, REACH + x, REACH - count : REACH] = low_rows(field, x, lon)
-            field_ref[field, REACH + x, REACH + TILE : REACH + TILE + count] = high_rows(
-                field, x, lon
-            )
     for field, distance, beyond, at in lon_layout():
         rows = slice(REACH - beyond, REACH + TILE + beyond)
         taken = slice(at, at + TILE + 2 * beyond)
         field_ref[field, REACH - distance, rows] = west(taken)
-        field_ref[field, REACH + lon - 1 + distance, rows] = east(taken)
-    turning = time_step * jnp.broadcast_to(turning_ref[:, :1], (wide, members))
-    keeper = jnp.broadcast_to(inside_ref[:, :1], (wide, members))
-    pull = 0.5 * time_step * gravity
-
-    west_depth = west(slice(LON_ROWS, None), slice(0, 128))
-    east_depth = east(slice(LON_ROWS, None), slice(0, 128))
-    middle_depth = strip_ref[...]
-
-    def column(x):
+        field_ref[field, REACH - 1 + distance, rows] = east(taken)
+    turning = time_step * spread_out(turning_ref[:, :1], shape)
+    keeper = spread_out(inside_ref[:, :1], shape)
+    strips = [
+        0.5 * time_step * strip
+        for strip in (
+            west(slice(LON_ROWS, None), slice(0, 128)),
+            strip_ref[...],
+            east(slice(LON_ROWS, None), slice(0, 128)),
+        )
+    ]
+
+    def depth(x):
         if x < REACH:
-            depth = west_depth[:, lon - REACH + x : lon - REACH + x + 1]
+            column = strips[0][:, lon - REACH + x : lon - REACH + x + 1]
         elif x < REACH + lon:
-            depth = middle_depth[:, x - REACH : x - REACH + 1]
+            column = strips[1][:, x - REACH : x - REACH + 1]
         else:
-            depth = east_depth[:, x - REACH - lon : x - REACH - lon + 1]
-        return jnp.broadcast_to(0.5 * time_step * depth, (wide, members))
-
-    def along(plane):
-        return pltpu.roll(plane, wide - 1, 0) - pltpu.roll(plane, 1, 0)
-
-    def advance_height(source, target, x):
-        spread = source[1, x + 1] - source[1, x - 1] + along(source[2, x])
-        target[0, x] = source[0, x] - column(x) * spread
-
-    def advance_flow(source, heights, x):
-        east = source[1, x]
-        north = source[2, x]
-        slope_east = heights[0, x + 1] - heights[0, x - 1]
-        slope_north = along(heights[0, x])
-        return (
-            east + (turning * north - pull * slope_east),
-            north - (turning * east + pull * slope_north),
-        )
-
-    for x in range(1, wide - 1):
-        advance_height(field_ref, next_ref, x)
-    for x in range(2, wide - 2):
-        east, north = advance_flow(field_ref, next_ref, x)
-        next_ref[1, x] = east
-        next_ref[2, x] = north * keeper
-    for x in range(3, wide - 3):
-        advance_height(next_ref, last_ref, x)
-    for x in range(REACH, REACH + lon):
-        east, north = advance_flow(next_ref, last_ref, x)
-        for field, plane in enumerate((last_ref[0, x], east, north)):
+            column = strips[2][:, x - REACH - lon : x - REACH - lon + 1]
+        return spread_out(column, shape)
+
+    def source(field, x):
+        if x < REACH:
+            return field_ref[field, x]
+        if x >= REACH + lon:
+            return field_ref[field, x - lon]
+        return handed_ref[field, HANDED[field].index(x)]
+
+    def after(field, x):
+        if x in HANDED[3 + field]:
+            return handed_ref[3 + field, HANDED[3 + field].index(x)]
+        return next_ref[field, x]
+
+    def height(x):
+        return after(0, x)
+
+    def last_height(x):
+        if x in HANDED[6]:
+            return handed_ref[6, HANDED[6].index(x)]
+        return last_ref[0, x]
+
+    def edges(margin):
+        return (*range(margin, margin + REACH), *range(end - margin - REACH, end - margin))
+
+    for x in edges(1):
+        next_ref[0, x] = advance_height(source, depth, x)
+    for x in edges(2):
+        east_flow, north_flow = advance_flow(source, height, turning, x)
+        next_ref[1, x] = east_flow
+        next_ref[2, x] = north_flow * keeper
+    for x in edges(3):
+        last_ref[0, x] = advance_height(after, depth, x)
+    for x in edges(REACH):
+        east_flow, north_flow = advance_flow(after, last_height, turning, x)
+        for field, plane in enumerate((last_height(x), east_flow, north_flow)):
             at = (field * lon + x - REACH) * TILE
             forecast_ref[at : at + TILE] = plane[REACH : REACH + TILE]
+    for field in range(len(LAT_ROWS)):
+        for x in range(REACH, lon - REACH):
+            at = (field * lon + x) * TILE
+            forecast_ref[at : at + TILE] = inner_ref[field, x - REACH]
 
     for copy in copies:
         copy.wait()
@@ -279,8 +384,11 @@
 def dot3(left, right):
     left_high, left_low = left
     right_high, right_low = right
-    dot = functools.partial(jnp.dot, preferred_element_type=jnp.float32)
-    return dot(left_high, right_high) + (dot(left_high, right_low) + dot(left_low, right_high))
+    return jnp.dot(
+        jnp.concatenate([left_high, left_high, left_low], axis=1),
+        jnp.concatenate([right_high, right_low, right_high], axis=0),
+        preferred_element_type=jnp.float32,
+    )
 
 
 def finish_kernel(
@@ -415,29 +523,39 @@
         [pltpu.SMEM] + [vmem] * 4,
         [],
     )(parity, ensemble, first, second, depth)
+    planes = (fields, lon, wide, members)
     across = lax.ppermute(out_across, "lon", across)
     within = lax.ppermute(out_within, "lon", within)
-    planes = (fields, lon + 2 * REACH, wide, members)
+    inner, handed = on_core(
+        inner_kernel,
+        ((fields, lon - 2 * REACH, lat, members), (len(HANDED), REACH) + planes[2:]),
+        [pltpu.SMEM] + [vmem] * 6,
+        [pltpu.VMEM(planes, jnp.float32)] * 2
+        + [pltpu.VMEM((1,) + planes[1:], jnp.float32)],
+    )(parity, ensemble, first, second, strip, turning, inside)
+    planes = (fields, wide, wide, members)
     forecast, packed = on_core(
         step_kernel,
         ((fields * lon * lat, members), (members + 32, members // 2)),
-        [pltpu.SMEM] + [vmem] * 8 + [pltpu.HBM] * 3,
-        [pltpu.VMEM(planes, jnp.float32)] * 2
-        + [pltpu.VMEM((1,) + planes[1:], jnp.float32)]
-        + [pltpu.VMEM((obs_cell.shape[2], members), jnp.float32)]
-        + [pltpu.SMEM(obs_cell.shape, jnp.int32)]
+        [pltpu.SMEM] + [vmem] * 7 + [pltpu.HBM] * 3,
+        [
+            pltpu.VMEM((fields, 2 * REACH) + planes[2:], jnp.float32),
+            pltpu.VMEM(planes, jnp.float32),
+            pltpu.VMEM((1,) + planes[1:], jnp.float32),
+            pltpu.VMEM((obs_cell.shape[2], members), jnp.float32),
+            pltpu.SMEM(obs_cell.shape, jnp.int32),
+        ]
         + [pltpu.VMEM(obs_value.shape, jnp.float32)] * 2
         + [pltpu.SemaphoreType.DMA((3,))],
     )(
         parity,
-        ensemble,
-        first,
-        second,
         across,
         within,
         strip,
         turning,
         inside,
+        inner,
+        handed,
         in_hbm(obs_cell),
         in_hbm(obs_value),
         in_hbm(obs_weight),

time: 84.4 us -> 83.2 us (0.986)
  waiting for transfers between devices: 4.18 us -> 3.27 us
    pallas_call x1, Pallas kernels: 2.34 us -> 1.3 us  [local(): on_core(step_kernel, ((fields * lon * lat, members), (members + 32, membe...]
    ppermute x1, waiting for transfers between devices: 1.04 us -> 0.14 us  [local(): within = lax.ppermute(out_within, 'lon', within)]
  transfers between devices with their start and end apart: 4 -> 4, of which waited for: 2 -> 2; matrix products, arithmetic and copies ran while one was open for 0% -> 0% of each run, Pallas kernels for 0% -> 1%
where the time goes in v7:
time: 83.2 us; the launch traced here: 82.9 us
  blocking collectives  53.2 us (64%)
  starting transfers between devices  16.7 us (20%)
  Pallas kernels  8.51 us (10%)
  waiting for transfers between devices  3.27 us (4%)
    all_to_all x1, blocking collectives, reduced(): lax.all_to_all(jnp.broadcast_to(piece[None], (lat, 1, width)), 'lat', 0, 0)  25.7 us
    all_to_all x1, blocking collectives, reduced(): pieces = lax.all_to_all(packed.reshape(lon, 1, width), 'lon', 0, 0)  14.7 us
    all_to_all x1, blocking collectives, reduced(): lax.all_to_all(jnp.broadcast_to(piece[None], (lon, 1, width)), 'lon', 0, 0)  12.9 us
    ppermute x1, starting transfers between devices, local(): second = lax.ppermute(second, ('lon', 'lat'), pairs[1])  7.24 us
    ppermute x1, starting transfers between devices, local(): within = lax.ppermute(out_within, 'lon', within)  6.85 us
    pallas_call x1, Pallas kernels, finish(): on_core(finish_kernel, (state.shape, square), [pltpu.VMEM] * 2, [pltpu.VM...  5.07 us
    ppermute x1, waiting for transfers between devices, local(): second = lax.ppermute(second, ('lon', 'lat'), pairs[1])  3.13 us
    ppermute x1, starting transfers between devices, local(): across = lax.ppermute(out_across, 'lon', across)  1.92 us
  transfers between devices with their start and end apart: 4, of which 2 were waited for; matrix products, arithmetic and copies ran while one was open for 0% of the time, Pallas kernels for 1%

profile of v7, /device:TPU:1, one launch (start us, length us, event | category | flops | bytes accessed | tf_op | source)
XLA Modules:
  0.0 82.9 jit_solution(16580229204164864859)
XLA Ops:
  0.6 0.0 copy-start
  0.6 1.3 %shard_map.68 = (f32[168,256]{1,0:T(8,128)S(1)}, f32[168,256]{1,0:T(8,128)S(1)}, f32[16,128]{1,0:T(8,128)S(1)}) custom-call(s32[1]{0:T(128)} %bitcast.parity_ref, f32[3,16,16,256]{3,2,1,0:T(8,128)} %state_ref.3, s32[16,16]{1,0:T(8,128)} %bathymetry_ref.1), custom_call_target="tpu_custom_call" | custom-call | tf_op jit(solution)/shard_map/pallas_call | solution.py:497
  2.0 0.7 collective-permute-start
  2.6 7.2 %collective-permute-start.1 = (f32[168,256]{1,0:T(8,128)S(1)}, f32[168,256]{1,0:T(8,128)S(1)}, u32[]{:S(2)}, u32[]{:S(2)}) collective-permute-start(f32[168,256]{1,0:T(8,128)S(1)} %get-tuple-element.15), channel_id=1, source_target_pairs={{1,2},{2,1},{3,4},{4,3},{5,6},{6,5},{7,8},{8,7},{9,10},{10,9},{11,... | collective-permute-start | bytes 516104 | tf_op jit(solution)/shard_map/ppermute | solution.py:519
  9.9 0.0 collective-permute-done.first_ref
  9.9 3.1 %collective-permute-done.1.second_ref = f32[168,256]{1,0:T(8,128)S(1)} collective-permute-done((f32[168,256]{1,0:T(8,128)S(1)}, f32[168,256]{1,0:T(8,128)S(1)}, u32[]{:S(2)}, u32[]{:S(2)}) %collective-permute-start.1) | collective-permute-done | bytes 172064 | tf_op jit(solution)/shard_map/ppermute | solution.py:519
  13.0 0.0 copy-done
  13.0 0.1 shard_map.69
  13.1 1.9 %collective-permute-start.2 = (f32[216,256]{1,0:T(8,128)S(1)}, f32[216,256]{1,0:T(8,128)S(1)}, u32[]{:S(2)}, u32[]{:S(2)}) collective-permute-start(f32[216,256]{1,0:T(8,128)S(1)} %get-tuple-element.17), channel_id=1, source_target_pairs={{16,32},{32,16},{48,64},{64,48},{80,96},{96,80},{112,128},{128,112... | collective-permute-start | bytes 663560 | tf_op jit(solution)/shard_map/ppermute | solution.py:527
  15.0 6.9 %collective-permute-start.3 = (f32[216,256]{1,0:T(8,128)S(1)}, f32[216,256]{1,0:T(8,128)S(1)}, u32[]{:S(2)}, u32[]{:S(2)}) collective-permute-start(f32[216,256]{1,0:T(8,128)S(1)} %get-tuple-element.18), channel_id=1, source_target_pairs={{0,16},{16,0},{32,48},{48,32},{64,80},{80,64},{96,112},{112,96},{1... | collective-permute-start | bytes 663560 | tf_op jit(solution)/shard_map/ppermute | solution.py:528
  21.9 0.1 iota.9.turning_ref
  22.0 0.1 iota.10.inside_ref
  22.1 0.8 shard_map.70
  22.8 0.0 collective-permute-done.2.across_ref
  22.9 0.1 collective-permute-done.3.within_ref
  23.0 1.3 %shard_map.71 = (f32[768,256]{1,0:T(8,128)S(1)}, f32[288,128]{1,0:T(8,128)S(1)}) custom-call(s32[1]{0:T(128)} %bitcast.parity_ref, f32[216,256]{1,0:T(8,128)S(1)} %collective-permute-done.2.across_ref, f32[216,256]{1,0:T(8,128)S(1)} %collective-permute-done.3.within_ref, f32[24,128]{1,0:T(8,128)S(1)} %get-tuple-element.19.strip_ref, ...), custom_call_target="tpu_custom_call" | custom-call | tf_op jit(solution)/shard_map/pallas_call | solution.py:537
  24.3 14.7 %all_to_all.15 = f32[32,1,1152]{2,1,0:T(1,128)S(1)} all-to-all(f32[32,1,1152]{2,1,0:T(1,128)S(1)} %bitcast.5), channel_id=1, replica_groups=mesh['lon'=32,'lat'=16] {'lon'}, dimensions={0} | all-to-all | bytes 294912 | tf_op jit(solution)/shard_map/all_to_all | solution.py:476
  39.0 0.1 reduce_sum.18
  39.1 25.7 %all_to_all.16 = f32[16,1,1152]{2,1,0:T(1,128)S(1)} all-to-all(f32[16,1,1152]{2,1,0:T(1,128)S(1)} %broadcast_in_dim.4), channel_id=1, replica_groups=mesh['lon'=32,'lat'=16] {'lat'}, dimensions={0} | all-to-all | bytes 147456 | tf_op jit(solution)/shard_map/all_to_all | solution.py:478
  64.8 0.1 reduce_sum.19
  64.8 0.1 broadcast_in_dim.5
  64.9 12.9 %all_to_all.17 = f32[32,1,1152]{2,1,0:T(1,128)S(1)} all-to-all(f32[32,1,1152]{2,1,0:T(1,128)S(1)} %broadcast_in_dim.5), channel_id=1, replica_groups=mesh['lon'=32,'lat'=16] {'lon'}, dimensions={0} | all-to-all | bytes 294912 | tf_op jit(solution)/shard_map/all_to_all | solution.py:480
  77.8 5.1 %shard_map.72 = (f32[768,256]{1,0:T(8,128)}, f32[256,256]{1,0:T(8,128)}) custom-call(f32[288,128]{1,0:T(8,128)S(1)} %bitcast.4, f32[768,256]{1,0:T(8,128)S(1)} %get-tuple-element.23.state_ref), custom_call_target="tpu_custom_call" | custom-call | tf_op jit(solution)/shard_map/pallas_call | solution.py:459
  (3 shorter events, 0.1 us)
Async XLA Ops:
  0.6 12.4 %copy-start = (f32[3,16,16,256]{3,2,1,0:T(8,128)S(1)}, f32[3,16,16,256]{3,2,1,0:T(8,128)}, u32[]{:S(2)}) copy-start(f32[3,16,16,256]{3,2,1,0:T(8,128)} %state_ref.3) | copy-start | bytes 2359300
  2.0 7.9 %collective-permute-start = (f32[168,256]{1,0:T(8,128)S(1)}, f32[168,256]{1,0:T(8,128)S(1)}, u32[]{:S(2)}, u32[]{:S(2)}) collective-permute-start(f32[168,256]{1,0:T(8,128)S(1)} %get-tuple-element.14), channel_id=1, source_target_pairs={{0,1},{1,0},{2,3},{3,2},{4,5},{5,4},{6,7},{7,6},{8,9},{9,8},{10,11... | collective-permute-start | bytes 516104 | tf_op jit(solution)/shard_map/ppermute | solution.py:518
  2.6 10.4 %collective-permute-start.1 = (f32[168,256]{1,0:T(8,128)S(1)}, f32[168,256]{1,0:T(8,128)S(1)}, u32[]{:S(2)}, u32[]{:S(2)}) collective-permute-start(f32[168,256]{1,0:T(8,128)S(1)} %get-tuple-element.15), channel_id=1, source_target_pairs={{1,2},{2,1},{3,4},{4,3},{5,6},{6,5},{7,8},{8,7},{9,10},{10,9},{11,... | collective-permute-start | bytes 516104 | tf_op jit(solution)/shard_map/ppermute | solution.py:519
  13.1 9.7 %collective-permute-start.2 = (f32[216,256]{1,0:T(8,128)S(1)}, f32[216,256]{1,0:T(8,128)S(1)}, u32[]{:S(2)}, u32[]{:S(2)}) collective-permute-start(f32[216,256]{1,0:T(8,128)S(1)} %get-tuple-element.17), channel_id=1, source_target_pairs={{16,32},{32,16},{48,64},{64,48},{80,96},{96,80},{112,128},{128,112... | collective-permute-start | bytes 663560 | tf_op jit(solution)/shard_map/ppermute | solution.py:527
  15.0 7.9 %collective-permute-start.3 = (f32[216,256]{1,0:T(8,128)S(1)}, f32[216,256]{1,0:T(8,128)S(1)}, u32[]{:S(2)}, u32[]{:S(2)}) collective-permute-start(f32[216,256]{1,0:T(8,128)S(1)} %get-tuple-element.18), channel_id=1, source_target_pairs={{0,16},{16,0},{32,48},{48,32},{64,80},{80,64},{96,112},{112,96},{1... | collective-permute-start | bytes 663560 | tf_op jit(solution)/shard_map/ppermute | solution.py:528

commit v8 on v7

--- a/solution.py
+++ b/solution.py
@@ -57,11 +57,11 @@
                 up_ref[at : at + count] = plane[lat - count :]
                 down_ref[at : at + count] = plane[:count]
 
-    @pl.when(parity_ref[0] & 1 == 0)
+    @pl.when(parity_ref[0] == 0)
     def _():
         pack(first_ref, second_ref)
 
-    @pl.when(parity_ref[0] & 1 == 1)
+    @pl.when(parity_ref[0] == 1)
     def _():
         pack(second_ref, first_ref)
 
@@ -88,15 +88,15 @@
     parity_ref, state_ref, first_ref, second_ref, depth_ref, across_ref, within_ref, strip_ref
 ):
     lon = state_ref.shape[1]
-    even = parity_ref[0] & 1 == 0
-    low_rows = functools.partial(lat_rows, even, second_ref, first_ref)
-    high_rows = functools.partial(lat_rows, even, first_ref, second_ref)
+    even = parity_ref[0] == 0
+    low_rows = functools.partial(lat_rows, even, first_ref, second_ref)
+    high_rows = functools.partial(lat_rows, even, second_ref, first_ref)
     depth_at = ROWS * lon
     strip_ref[...] = jnp.zeros_like(strip_ref)
     depths = slice(depth_at, depth_at + 3)
-    strip_ref[1:4] = chosen(even, second_ref, first_ref, depths, slice(0, 128))
+    strip_ref[1:4] = chosen(even, first_ref, second_ref, depths, slice(0, 128))
     strip_ref[4:20] = depth_ref[...]
-    strip_ref[20:23] = chosen(even, first_ref, second_ref, depths, slice(0, 128))
+    strip_ref[20:23] = chosen(even, second_ref, first_ref, depths, slice(0, 128))
     for ref in (across_ref, within_ref):
         ref[LON_ROWS:, 128:] = jnp.zeros((ref.shape[0] - LON_ROWS, 128), jnp.float32)
         ref[LON_ROWS - 2 : LON_ROWS] = jnp.zeros((2, ref.shape[1]), jnp.float32)
@@ -112,11 +112,11 @@
                     ref[at + beyond + TILE : at + TILE + 2 * beyond] = high[:beyond]
                 ref[at + beyond : at + beyond + TILE] = state_ref[field, x]
 
-    @pl.when(parity_ref[0] < 2)
+    @pl.when(parity_ref[0] == 0)
     def _():
         pack(within_ref, across_ref)
 
-    @pl.when(parity_ref[0] >= 2)
+    @pl.when(parity_ref[0] == 1)
     def _():
         pack(across_ref, within_ref)
 
@@ -177,9 +177,9 @@
 ):
     lon = state_ref.shape[1]
     shape = field_ref.shape[2:]
-    even = parity_ref[0] & 1 == 0
-    low_rows = functools.partial(lat_rows, even, second_ref, first_ref)
-    high_rows = functools.partial(lat_rows, even, first_ref, second_ref)
+    even = parity_ref[0] == 0
+    low_rows = functools.partial(lat_rows, even, first_ref, second_ref)
+    high_rows = functools.partial(lat_rows, even, second_ref, first_ref)
     for field, count in enumerate(LAT_ROWS):
         for x in range(lon):
             field_ref[field, x, REACH : REACH + TILE] = state_ref[field, x]
@@ -261,7 +261,7 @@
     members = shape[1]
     end = next_ref.shape[1]
     lon = end - 2 * REACH
-    even_lon = parity_ref[0] < 2
+    even_lon = parity_ref[0] == 0
     west = functools.partial(chosen, even_lon, across_ref, within_ref)
     east = functools.partial(chosen, even_lon, within_ref, across_ref)
     for field, distance, beyond, at in lon_layout():
@@ -492,8 +492,7 @@
     lat_shape = (ROWS * lon + 8, members)
     lon_shape = (LON_ROWS + wide, members)
     here = lax.axis_index("lon")
-    parity = ((here + lax.axis_index("lat")) & 1) + 2 * (here & 1)
-    parity = parity.reshape(1)
+    parity = (here & 1).reshape(1)
     first, second, depth = on_core(
         pack_lat_kernel,
         (lat_shape, lat_shape, (lat, 128)),
@@ -513,7 +512,8 @@
         for b in range(rows_of):
             ours = a * rows_of + b
             if b + 1 < rows_of:
-                pairs[(a + b) % 2].extend(((ours, ours + 1), (ours + 1, ours)))
+                pairs[a % 2].append((ours, ours + 1))
+                pairs[1 - a % 2].append((ours + 1, ours))
         (across if a % 2 else within).extend(((a, (a + 1) % columns), ((a + 1) % columns, a)))
     first = lax.ppermute(first, ("lon", "lat"), pairs[0])
     second = lax.ppermute(second, ("lon", "lat"), pairs[1])

time: 83.2 us -> 84.4 us (1.014)
  blocking collectives: 53.2 us -> 55 us
    ppermute x1, starting transfers between devices: 1.92 us -> 7.01 us  [local(): across = lax.ppermute(out_across, 'lon', across)]
    ppermute x1, starting transfers between devices: 6.85 us -> 3.64 us  [local(): within = lax.ppermute(out_within, 'lon', within)]
    ppermute x1, starting transfers between devices: 7.24 us -> 5 us  [local(): second = lax.ppermute(second, ('lon', 'lat'), pairs[1])]
    ppermute x1, waiting for transfers between devices: 3.13 us -> 1.48 us  [local(): second = lax.ppermute(second, ('lon', 'lat'), pairs[1])]
    all_to_all x1, blocking collectives: 14.7 us -> 16.1 us  [reduced(): pieces = lax.all_to_all(packed.reshape(lon, 1, width), 'lon', 0, 0)]
  transfers between devices with their start and end apart: 4 -> 4, of which waited for: 2 -> 3; matrix products, arithmetic and copies ran while one was open for 0% -> 0% of each run, Pallas kernels for 1% -> 1%
where the time goes in v8:
time: 84.4 us; the launch traced here: 84.1 us
  blocking collectives  55 us (65%)
  starting transfers between devices  16.9 us (20%)
  Pallas kernels  8.51 us (10%)
  waiting for transfers between devices  2.46 us (3%)
    all_to_all x1, blocking collectives, reduced(): lax.all_to_all(jnp.broadcast_to(piece[None], (lat, 1, width)), 'lat', 0, 0)  26 us
    all_to_all x1, blocking collectives, reduced(): pieces = lax.all_to_all(packed.reshape(lon, 1, width), 'lon', 0, 0)  16.1 us
    all_to_all x1, blocking collectives, reduced(): lax.all_to_all(jnp.broadcast_to(piece[None], (lon, 1, width)), 'lon', 0, 0)  12.9 us
    ppermute x1, starting transfers between devices, local(): across = lax.ppermute(out_across, 'lon', across)  7.01 us
    pallas_call x1, Pallas kernels, finish(): on_core(finish_kernel, (state.shape, square), [pltpu.VMEM] * 2, [pltpu.VM...  5.07 us
    ppermute x1, starting transfers between devices, local(): second = lax.ppermute(second, ('lon', 'lat'), pairs[1])  5 us
    ppermute x1, starting transfers between devices, local(): within = lax.ppermute(out_within, 'lon', within)  3.64 us
  transfers between devices with their start and end apart: 4, of which 3 were waited for; matrix products, arithmetic and copies ran while one was open for 0% of the time, Pallas kernels for 1%

profile of v8, /device:TPU:1, one launch (start us, length us, event | category | flops | bytes accessed | tf_op | source)
XLA Modules:
  0.0 84.1 jit_solution(2699043499493732160)
XLA Ops:
  0.6 0.0 copy-start
  0.6 1.3 %shard_map.68 = (f32[168,256]{1,0:T(8,128)S(1)}, f32[168,256]{1,0:T(8,128)S(1)}, f32[16,128]{1,0:T(8,128)S(1)}) custom-call(s32[1]{0:T(128)} %bitcast.parity_ref, f32[3,16,16,256]{3,2,1,0:T(8,128)} %state_ref.3, s32[16,16]{1,0:T(8,128)} %bathymetry_ref.1), custom_call_target="tpu_custom_call" | custom-call | tf_op jit(solution)/shard_map/pallas_call | solution.py:496
  2.0 1.3 %collective-permute-start = (f32[168,256]{1,0:T(8,128)S(1)}, f32[168,256]{1,0:T(8,128)S(1)}, u32[]{:S(2)}, u32[]{:S(2)}) collective-permute-start(f32[168,256]{1,0:T(8,128)S(1)} %get-tuple-element.14), channel_id=1, source_target_pairs={{0,1},{1,2},{2,3},{3,4},{4,5},{5,6},{6,7},{7,8},{8,9},{9,10},{10,1... | collective-permute-start | bytes 516104 | tf_op jit(solution)/shard_map/ppermute | solution.py:518
  3.3 5.0 %collective-permute-start.1 = (f32[168,256]{1,0:T(8,128)S(1)}, f32[168,256]{1,0:T(8,128)S(1)}, u32[]{:S(2)}, u32[]{:S(2)}) collective-permute-start(f32[168,256]{1,0:T(8,128)S(1)} %get-tuple-element.15), channel_id=1, source_target_pairs={{1,0},{2,1},{3,2},{4,3},{5,4},{6,5},{7,6},{8,7},{9,8},{10,9},{11,1... | collective-permute-start | bytes 516104 | tf_op jit(solution)/shard_map/ppermute | solution.py:519
  8.3 0.8 %collective-permute-done.first_ref = f32[168,256]{1,0:T(8,128)S(1)} collective-permute-done((f32[168,256]{1,0:T(8,128)S(1)}, f32[168,256]{1,0:T(8,128)S(1)}, u32[]{:S(2)}, u32[]{:S(2)}) %collective-permute-start) | collective-permute-done | bytes 172064 | tf_op jit(solution)/shard_map/ppermute | solution.py:518
  9.1 1.5 %collective-permute-done.1.second_ref = f32[168,256]{1,0:T(8,128)S(1)} collective-permute-done((f32[168,256]{1,0:T(8,128)S(1)}, f32[168,256]{1,0:T(8,128)S(1)}, u32[]{:S(2)}, u32[]{:S(2)}) %collective-permute-start.1) | collective-permute-done | bytes 172064 | tf_op jit(solution)/shard_map/ppermute | solution.py:519
  10.6 0.0 copy-done
  10.6 0.1 shard_map.69
  10.7 7.0 %collective-permute-start.2 = (f32[216,256]{1,0:T(8,128)S(1)}, f32[216,256]{1,0:T(8,128)S(1)}, u32[]{:S(2)}, u32[]{:S(2)}) collective-permute-start(f32[216,256]{1,0:T(8,128)S(1)} %get-tuple-element.17), channel_id=1, source_target_pairs={{16,32},{32,16},{48,64},{64,48},{80,96},{96,80},{112,128},{128,112... | collective-permute-start | bytes 663560 | tf_op jit(solution)/shard_map/ppermute | solution.py:527
  17.7 3.6 %collective-permute-start.3 = (f32[216,256]{1,0:T(8,128)S(1)}, f32[216,256]{1,0:T(8,128)S(1)}, u32[]{:S(2)}, u32[]{:S(2)}) collective-permute-start(f32[216,256]{1,0:T(8,128)S(1)} %get-tuple-element.18), channel_id=1, source_target_pairs={{0,16},{16,0},{32,48},{48,32},{64,80},{80,64},{96,112},{112,96},{1... | collective-permute-start | bytes 663560 | tf_op jit(solution)/shard_map/ppermute | solution.py:528
  21.4 0.1 iota.9.turning_ref
  21.4 0.1 iota.10.inside_ref
  21.5 0.8 shard_map.70
  22.3 0.0 collective-permute-done.2.across_ref
  22.3 0.1 collective-permute-done.3.within_ref
  22.4 1.3 %shard_map.71 = (f32[768,256]{1,0:T(8,128)S(1)}, f32[288,128]{1,0:T(8,128)S(1)}) custom-call(s32[1]{0:T(128)} %bitcast.parity_ref, f32[216,256]{1,0:T(8,128)S(1)} %collective-permute-done.2.across_ref, f32[216,256]{1,0:T(8,128)S(1)} %collective-permute-done.3.within_ref, f32[24,128]{1,0:T(8,128)S(1)} %get-tuple-element.19.strip_ref, ...), custom_call_target="tpu_custom_call" | custom-call | tf_op jit(solution)/shard_map/pallas_call | solution.py:537
  23.7 16.1 %all_to_all.15 = f32[32,1,1152]{2,1,0:T(1,128)S(1)} all-to-all(f32[32,1,1152]{2,1,0:T(1,128)S(1)} %bitcast.5), channel_id=1, replica_groups=mesh['lon'=32,'lat'=16] {'lon'}, dimensions={0} | all-to-all | bytes 294912 | tf_op jit(solution)/shard_map/all_to_all | solution.py:476
  39.9 0.1 reduce_sum.18
  40.0 26.0 %all_to_all.16 = f32[16,1,1152]{2,1,0:T(1,128)S(1)} all-to-all(f32[16,1,1152]{2,1,0:T(1,128)S(1)} %broadcast_in_dim.4), channel_id=1, replica_groups=mesh['lon'=32,'lat'=16] {'lat'}, dimensions={0} | all-to-all | bytes 147456 | tf_op jit(solution)/shard_map/all_to_all | solution.py:478
  66.0 0.1 reduce_sum.19
  66.1 0.1 broadcast_in_dim.5
  66.1 12.9 %all_to_all.17 = f32[32,1,1152]{2,1,0:T(1,128)S(1)} all-to-all(f32[32,1,1152]{2,1,0:T(1,128)S(1)} %broadcast_in_dim.5), channel_id=1, replica_groups=mesh['lon'=32,'lat'=16] {'lon'}, dimensions={0} | all-to-all | bytes 294912 | tf_op jit(solution)/shard_map/all_to_all | solution.py:480
  79.0 5.1 %shard_map.72 = (f32[768,256]{1,0:T(8,128)}, f32[256,256]{1,0:T(8,128)}) custom-call(f32[288,128]{1,0:T(8,128)S(1)} %bitcast.4, f32[768,256]{1,0:T(8,128)S(1)} %get-tuple-element.23.state_ref), custom_call_target="tpu_custom_call" | custom-call | tf_op jit(solution)/shard_map/pallas_call | solution.py:459
  (3 shorter events, 0.1 us)
Async XLA Ops:
  0.6 10.0 %copy-start = (f32[3,16,16,256]{3,2,1,0:T(8,128)S(1)}, f32[3,16,16,256]{3,2,1,0:T(8,128)}, u32[]{:S(2)}) copy-start(f32[3,16,16,256]{3,2,1,0:T(8,128)} %state_ref.3) | copy-start | bytes 2359300
  2.0 7.2 %collective-permute-start = (f32[168,256]{1,0:T(8,128)S(1)}, f32[168,256]{1,0:T(8,128)S(1)}, u32[]{:S(2)}, u32[]{:S(2)}) collective-permute-start(f32[168,256]{1,0:T(8,128)S(1)} %get-tuple-element.14), channel_id=1, source_target_pairs={{0,1},{1,2},{2,3},{3,4},{4,5},{5,6},{6,7},{7,8},{8,9},{9,10},{10,1... | collective-permute-start | bytes 516104 | tf_op jit(solution)/shard_map/ppermute | solution.py:518
  3.3 7.3 %collective-permute-start.1 = (f32[168,256]{1,0:T(8,128)S(1)}, f32[168,256]{1,0:T(8,128)S(1)}, u32[]{:S(2)}, u32[]{:S(2)}) collective-permute-start(f32[168,256]{1,0:T(8,128)S(1)} %get-tuple-element.15), channel_id=1, source_target_pairs={{1,0},{2,1},{3,2},{4,3},{5,4},{6,5},{7,6},{8,7},{9,8},{10,9},{11,1... | collective-permute-start | bytes 516104 | tf_op jit(solution)/shard_map/ppermute | solution.py:519
  10.7 11.6 %collective-permute-start.2 = (f32[216,256]{1,0:T(8,128)S(1)}, f32[216,256]{1,0:T(8,128)S(1)}, u32[]{:S(2)}, u32[]{:S(2)}) collective-permute-start(f32[216,256]{1,0:T(8,128)S(1)} %get-tuple-element.17), channel_id=1, source_target_pairs={{16,32},{32,16},{48,64},{64,48},{80,96},{96,80},{112,128},{128,112... | collective-permute-start | bytes 663560 | tf_op jit(solution)/shard_map/ppermute | solution.py:527
  17.7 4.7 %collective-permute-start.3 = (f32[216,256]{1,0:T(8,128)S(1)}, f32[216,256]{1,0:T(8,128)S(1)}, u32[]{:S(2)}, u32[]{:S(2)}) collective-permute-start(f32[216,256]{1,0:T(8,128)S(1)} %get-tuple-element.18), channel_id=1, source_target_pairs={{0,16},{16,0},{32,48},{48,32},{64,80},{80,64},{96,112},{112,96},{1... | collective-permute-start | bytes 663560 | tf_op jit(solution)/shard_map/ppermute | solution.py:528

commit v9 on v7

--- a/solution.py
+++ b/solution.py
@@ -15,6 +15,7 @@
 TILE = 16
 LAT_ROWS = (3, 3, 4)
 ROWS = sum(LAT_ROWS)
+MAIN_ROWS = 160
 LON_ROWS = 192
 
 time_step = 0.6
@@ -33,7 +34,7 @@
 
 
 def pack_lat_kernel(
-    parity_ref, ensemble_ref, bathymetry_ref, first_ref, second_ref, depth_ref, state_ref, bottom_ref, square_ref, sems
+    parity_ref, ensemble_ref, bathymetry_ref, first_ref, second_ref, ahead_ref, depth_ref, state_ref, bottom_ref, square_ref, sems
 ):
     lon, lat = state_ref.shape[1], state_ref.shape[2]
     copies = fetch((bathymetry_ref, ensemble_ref), (bottom_ref, state_ref), sems)
@@ -65,6 +66,11 @@
     def _():
         pack(second_ref, first_ref)
 
+    even_lon = parity_ref[0] < 2
+    for field, distance, _, main, _ in lon_layout():
+        down, up = state_ref[field, distance - 1], state_ref[field, lon - distance]
+        ahead_ref[main : main + TILE] = jnp.where(even_lon, down, up)
+
 
 def chosen(even, first_ref, second_ref, rows, lanes=slice(None)):
     return jnp.where(even, first_ref[rows, lanes], second_ref[rows, lanes])
@@ -76,12 +82,13 @@
 
 
 def lon_layout():
-    at = 0
+    main, corner = 0, MAIN_ROWS
     for field, width, reach in ((0, 3, 3), (1, 4, 4), (2, 3, 4)):
         for distance in range(1, width + 1):
             beyond = reach - distance
-            yield field, distance, beyond, at
-            at += TILE + 2 * beyond
+            yield field, distance, beyond, main, corner
+            main += TILE
+            corner += 2 * beyond
 
 
 def pack_lon_kernel(
@@ -97,28 +104,35 @@
     strip_ref[1:4] = chosen(even, second_ref, first_ref, depths, slice(0, 128))
     strip_ref[4:20] = depth_ref[...]
     strip_ref[20:23] = chosen(even, first_ref, second_ref, depths, slice(0, 128))
-    for ref in (across_ref, within_ref):
-        ref[LON_ROWS:, 128:] = jnp.zeros((ref.shape[0] - LON_ROWS, 128), jnp.float32)
-        ref[LON_ROWS - 2 : LON_ROWS] = jnp.zeros((2, ref.shape[1]), jnp.float32)
-        ref[LON_ROWS:, :128] = strip_ref[...]
-
-    def pack(up_ref, down_ref):
-        for field, distance, beyond, at in lon_layout():
-            for ref, x in ((up_ref, lon - distance), (down_ref, distance - 1)):
+    for ref, skipped in ((across_ref, MAIN_ROWS), (within_ref, 0)):
+        depths = slice(LON_ROWS - skipped, None)
+        ref[depths, 128:] = jnp.zeros((strip_ref.shape[0], 128), jnp.float32)
+        ref[LON_ROWS - 2 - skipped : LON_ROWS - skipped] = jnp.zeros((2, ref.shape[1]), jnp.float32)
+        ref[depths, :128] = strip_ref[...]
+
+    def pack(upward):
+        for field, distance, beyond, main, corner in lon_layout():
+            up, down = lon - distance, distance - 1
+            for ref, x, skipped in (
+                (across_ref, up if upward else down, MAIN_ROWS),
+                (within_ref, down if upward else up, 0),
+            ):
                 if beyond:
+                    at = corner - skipped
                     low = low_rows(field, x, lon)
                     ref[at : at + beyond] = low[LAT_ROWS[field] - beyond :]
                     high = high_rows(field, x, lon)
-                    ref[at + beyond + TILE : at + TILE + 2 * beyond] = high[:beyond]
-                ref[at + beyond : at + beyond + TILE] = state_ref[field, x]
+                    ref[at + beyond : at + 2 * beyond] = high[:beyond]
+                if not skipped:
+                    ref[main : main + TILE] = state_ref[field, x]
 
     @pl.when(parity_ref[0] < 2)
     def _():
-        pack(within_ref, across_ref)
+        pack(False)
 
     @pl.when(parity_ref[0] >= 2)
     def _():
-        pack(across_ref, within_ref)
+        pack(True)
 
 
 def dot3_first(left, right):
@@ -233,6 +247,7 @@
 
 def step_kernel(
     parity_ref,
+    ahead_ref,
     across_ref,
     within_ref,
     strip_ref,
@@ -262,23 +277,29 @@
     end = next_ref.shape[1]
     lon = end - 2 * REACH
     even_lon = parity_ref[0] < 2
-    west = functools.partial(chosen, even_lon, across_ref, within_ref)
-    east = functools.partial(chosen, even_lon, within_ref, across_ref)
-    for field, distance, beyond, at in lon_layout():
-        rows = slice(REACH - beyond, REACH + TILE + beyond)
-        taken = slice(at, at + TILE + 2 * beyond)
-        field_ref[field, REACH - distance, rows] = west(taken)
-        field_ref[field, REACH - 1 + distance, rows] = east(taken)
+
+    def taken(rows, lanes=slice(None)):
+        start, stop = rows
+        if stop <= MAIN_ROWS:
+            across = ahead_ref[start:stop, lanes]
+        else:
+            across = across_ref[start - MAIN_ROWS : stop - MAIN_ROWS, lanes]
+        within = within_ref[start:stop, lanes]
+        return jnp.where(even_lon, across, within), jnp.where(even_lon, within, across)
+
+    for field, distance, beyond, main, corner in lon_layout():
+        parts = [((main, main + TILE), REACH, TILE)]
+        if beyond:
+            parts.append(((corner, corner + beyond), REACH - beyond, beyond))
+            parts.append(((corner + beyond, corner + 2 * beyond), REACH + TILE, beyond))
+        for rows, at, count in parts:
+            west, east = taken(rows)
+            field_ref[field, REACH - distance, at : at + count] = west
+            field_ref[field, REACH - 1 + distance, at : at + count] = east
+    west_strip, east_strip = taken((LON_ROWS, within_ref.shape[0]), slice(0, 128))
     turning = time_step * spread_out(turning_ref[:, :1], shape)
     keeper = spread_out(inside_ref[:, :1], shape)
-    strips = [
-        0.5 * time_step * strip
-        for strip in (
-            west(slice(LON_ROWS, None), slice(0, 128)),
-            strip_ref[...],
-            east(slice(LON_ROWS, None), slice(0, 128)),
-        )
-    ]
+    strips = [0.5 * time_step * strip for strip in (west_strip, strip_ref[...], east_strip)]
 
     def depth(x):
         if x < REACH:
@@ -494,9 +515,9 @@
     here = lax.axis_index("lon")
     parity = ((here + lax.axis_index("lat")) & 1) + 2 * (here & 1)
     parity = parity.reshape(1)
-    first, second, depth = on_core(
+    first, second, ahead, depth = on_core(
         pack_lat_kernel,
-        (lat_shape, lat_shape, (lat, 128)),
+        (lat_shape, lat_shape, (MAIN_ROWS, members), (lat, 128)),
         [pltpu.SMEM] + [pltpu.HBM] * 2,
         [
             pltpu.VMEM(ensemble.shape, jnp.float32),
@@ -517,9 +538,10 @@
         (across if a % 2 else within).extend(((a, (a + 1) % columns), ((a + 1) % columns, a)))
     first = lax.ppermute(first, ("lon", "lat"), pairs[0])
     second = lax.ppermute(second, ("lon", "lat"), pairs[1])
+    ahead = lax.ppermute(ahead, "lon", across)
     out_across, out_within, strip = on_core(
         pack_lon_kernel,
-        (lon_shape, lon_shape, (wide, 128)),
+        ((LON_ROWS + wide - MAIN_ROWS, members), lon_shape, (wide, 128)),
         [pltpu.SMEM] + [vmem] * 4,
         [],
     )(parity, ensemble, first, second, depth)
@@ -537,7 +559,7 @@
     forecast, packed = on_core(
         step_kernel,
         ((fields * lon * lat, members), (members + 32, members // 2)),
-        [pltpu.SMEM] + [vmem] * 7 + [pltpu.HBM] * 3,
+        [pltpu.SMEM] + [vmem] * 8 + [pltpu.HBM] * 3,
         [
             pltpu.VMEM((fields, 2 * REACH) + planes[2:], jnp.float32),
             pltpu.VMEM(planes, jnp.float32),
@@ -549,6 +571,7 @@
         + [pltpu.SemaphoreType.DMA((3,))],
     )(
         parity,
+        ahead,
         across,
         within,
         strip,

time: 83.2 us -> 86.7 us (1.042)
  blocking collectives: 53.2 us -> 54.7 us
  starting transfers between devices: 16.7 us -> 17.8 us
    ppermute x1, waiting for transfers between devices: 0.01 us -> 2.64 us  [local(): across = lax.ppermute(out_across, 'lon', across)]
    all_to_all x1, blocking collectives: 25.7 us -> 28 us  [reduced(): lax.all_to_all(jnp.broadcast_to(piece[None], (lat, 1, width)), 'lat', 0, 0)]
    ppermute x1, waiting for transfers between devices: 3.13 us -> 1.2 us  [local(): second = lax.ppermute(second, ('lon', 'lat'), pairs[1])]
    ppermute x0 -> x1, starting transfers between devices: none -> 1.92 us  [local(): ahead = lax.ppermute(ahead, 'lon', across)]
  transfers between devices with their start and end apart: 4 -> 5, of which waited for: 2 -> 2; matrix products, arithmetic and copies ran while one was open for 0% -> 0% of each run, Pallas kernels for 1% -> 1%
where the time goes in v9:
time: 86.7 us; the launch traced here: 86.4 us
  blocking collectives  54.7 us (63%)
  starting transfers between devices  17.8 us (21%)
  Pallas kernels  8.8 us (10%)
  waiting for transfers between devices  3.85 us (4%)
    all_to_all x1, blocking collectives, reduced(): lax.all_to_all(jnp.broadcast_to(piece[None], (lat, 1, width)), 'lat', 0, 0)  28 us
    all_to_all x1, blocking collectives, reduced(): pieces = lax.all_to_all(packed.reshape(lon, 1, width), 'lon', 0, 0)  13.8 us
    all_to_all x1, blocking collectives, reduced(): lax.all_to_all(jnp.broadcast_to(piece[None], (lon, 1, width)), 'lon', 0, 0)  12.9 us
    ppermute x1, starting transfers between devices, local(): second = lax.ppermute(second, ('lon', 'lat'), pairs[1])  7.24 us
    ppermute x1, starting transfers between devices, local(): within = lax.ppermute(out_within, 'lon', within)  6.04 us
    pallas_call x1, Pallas kernels, finish(): on_core(finish_kernel, (state.shape, square), [pltpu.VMEM] * 2, [pltpu.VM...  5.07 us
    ppermute x1, waiting for transfers between devices, local(): across = lax.ppermute(out_across, 'lon', across)  2.64 us
    ppermute x1, starting transfers between devices, local(): ahead = lax.ppermute(ahead, 'lon', across)  1.92 us
  transfers between devices with their start and end apart: 5, of which 2 were waited for; matrix products, arithmetic and copies ran while one was open for 0% of the time, Pallas kernels for 1%

profile of v9, /device:TPU:1, one launch (start us, length us, event | category | flops | bytes accessed | tf_op | source)
XLA Modules:
  0.0 86.4 jit_solution(5054126759041382417)
XLA Ops:
  0.6 0.0 copy-start
  0.6 1.3 %shard_map.68 = (f32[168,256]{1,0:T(8,128)S(1)}, f32[168,256]{1,0:T(8,128)S(1)}, f32[160,256]{1,0:T(8,128)S(1)}, f32[16,128]{1,0:T(8,128)S(1)}) custom-call(s32[1]{0:T(128)} %bitcast.parity_ref, f32[3,16,16,256]{3,2,1,0:T(8,128)} %state_ref.3, s32[16,16]{1,0:T(8,128)} %bathymetry_ref.1), custom_call_target="tpu_custom_call" | custom-call | tf_op jit(solution)/shard_map/pallas_call | solution.py:518
  2.0 0.7 collective-permute-start.1
  2.7 7.2 %collective-permute-start.2 = (f32[168,256]{1,0:T(8,128)S(1)}, f32[168,256]{1,0:T(8,128)S(1)}, u32[]{:S(2)}, u32[]{:S(2)}) collective-permute-start(f32[168,256]{1,0:T(8,128)S(1)} %get-tuple-element.17), channel_id=1, source_target_pairs={{1,2},{2,1},{3,4},{4,3},{5,6},{6,5},{7,8},{8,7},{9,10},{10,9},{11,... | collective-permute-start | bytes 516104 | tf_op jit(solution)/shard_map/ppermute | solution.py:540
  9.9 1.9 %collective-permute-start = (f32[160,256]{1,0:T(8,128)S(1)}, f32[160,256]{1,0:T(8,128)S(1)}, u32[]{:S(2)}, u32[]{:S(2)}) collective-permute-start(f32[160,256]{1,0:T(8,128)S(1)} %get-tuple-element.15), channel_id=1, source_target_pairs={{16,32},{32,16},{48,64},{64,48},{80,96},{96,80},{112,128},{128,112... | collective-permute-start | bytes 491528 | tf_op jit(solution)/shard_map/ppermute | solution.py:541
  11.8 0.0 collective-permute-done.1.first_ref
  11.8 1.2 %collective-permute-done.2.second_ref = f32[168,256]{1,0:T(8,128)S(1)} collective-permute-done((f32[168,256]{1,0:T(8,128)S(1)}, f32[168,256]{1,0:T(8,128)S(1)}, u32[]{:S(2)}, u32[]{:S(2)}) %collective-permute-start.2) | collective-permute-done | bytes 172064 | tf_op jit(solution)/shard_map/ppermute | solution.py:540
  13.1 0.0 copy-done
  13.1 0.1 shard_map.69
  13.1 6.0 %collective-permute-start.4 = (f32[216,256]{1,0:T(8,128)S(1)}, f32[216,256]{1,0:T(8,128)S(1)}, u32[]{:S(2)}, u32[]{:S(2)}) collective-permute-start(f32[216,256]{1,0:T(8,128)S(1)} %get-tuple-element.20), channel_id=1, source_target_pairs={{0,16},{16,0},{32,48},{48,32},{64,80},{80,64},{96,112},{112,96},{1... | collective-permute-start | bytes 663560 | tf_op jit(solution)/shard_map/ppermute | solution.py:550
  19.2 1.9 %collective-permute-start.3 = (f32[56,256]{1,0:T(8,128)S(1)}, f32[56,256]{1,0:T(8,128)S(1)}, u32[]{:S(2)}, u32[]{:S(2)}) collective-permute-start(f32[56,256]{1,0:T(8,128)S(1)} %get-tuple-element.19), channel_id=1, source_target_pairs={{16,32},{32,16},{48,64},{64,48},{80,96},{96,80},{112,128},{128,112... | collective-permute-start | bytes 172040 | tf_op jit(solution)/shard_map/ppermute | solution.py:549
  21.1 0.1 iota.9.turning_ref
  21.2 0.1 iota.10.inside_ref
  21.3 0.8 shard_map.70
  22.0 0.0 collective-permute-done.ahead_ref
  22.0 2.6 %collective-permute-done.3.across_ref = f32[56,256]{1,0:T(8,128)S(1)} collective-permute-done((f32[56,256]{1,0:T(8,128)S(1)}, f32[56,256]{1,0:T(8,128)S(1)}, u32[]{:S(2)}, u32[]{:S(2)}) %collective-permute-start.3) | collective-permute-done | bytes 57376 | tf_op jit(solution)/shard_map/ppermute | solution.py:549
  24.7 0.0 collective-permute-done.4.within_ref
  24.7 1.6 %shard_map.71 = (f32[768,256]{1,0:T(8,128)S(1)}, f32[288,128]{1,0:T(8,128)S(1)}) custom-call(s32[1]{0:T(128)} %bitcast.parity_ref, f32[160,256]{1,0:T(8,128)S(1)} %collective-permute-done.ahead_ref, f32[56,256]{1,0:T(8,128)S(1)} %collective-permute-done.3.across_ref, f32[216,256]{1,0:T(8,128)S(1)} %collective-permute-done.4.within_ref, ...), custom_call_target="tpu_custom_call" | custom-call | tf_op jit(solution)/shard_map/pallas_call | solution.py:559
  26.3 13.8 %all_to_all.15 = f32[32,1,1152]{2,1,0:T(1,128)S(1)} all-to-all(f32[32,1,1152]{2,1,0:T(1,128)S(1)} %bitcast.5), channel_id=1, replica_groups=mesh['lon'=32,'lat'=16] {'lon'}, dimensions={0} | all-to-all | bytes 294912 | tf_op jit(solution)/shard_map/all_to_all | solution.py:497
  40.1 0.1 reduce_sum.18
  40.3 28.0 %all_to_all.16 = f32[16,1,1152]{2,1,0:T(1,128)S(1)} all-to-all(f32[16,1,1152]{2,1,0:T(1,128)S(1)} %broadcast_in_dim.4), channel_id=1, replica_groups=mesh['lon'=32,'lat'=16] {'lat'}, dimensions={0} | all-to-all | bytes 147456 | tf_op jit(solution)/shard_map/all_to_all | solution.py:499
  68.2 0.1 reduce_sum.19
  68.3 0.1 broadcast_in_dim.5
  68.4 12.9 %all_to_all.17 = f32[32,1,1152]{2,1,0:T(1,128)S(1)} all-to-all(f32[32,1,1152]{2,1,0:T(1,128)S(1)} %broadcast_in_dim.5), channel_id=1, replica_groups=mesh['lon'=32,'lat'=16] {'lon'}, dimensions={0} | all-to-all | bytes 294912 | tf_op jit(solution)/shard_map/all_to_all | solution.py:501
  81.3 5.1 %shard_map.72 = (f32[768,256]{1,0:T(8,128)}, f32[256,256]{1,0:T(8,128)}) custom-call(f32[288,128]{1,0:T(8,128)S(1)} %bitcast.4, f32[768,256]{1,0:T(8,128)S(1)} %get-tuple-element.25.state_ref), custom_call_target="tpu_custom_call" | custom-call | tf_op jit(solution)/shard_map/pallas_call | solution.py:480
  (3 shorter events, 0.1 us)
Async XLA Ops:
  0.6 12.4 %copy-start = (f32[3,16,16,256]{3,2,1,0:T(8,128)S(1)}, f32[3,16,16,256]{3,2,1,0:T(8,128)}, u32[]{:S(2)}) copy-start(f32[3,16,16,256]{3,2,1,0:T(8,128)} %state_ref.3) | copy-start | bytes 2359300
  2.0 9.9 %collective-permute-start.1 = (f32[168,256]{1,0:T(8,128)S(1)}, f32[168,256]{1,0:T(8,128)S(1)}, u32[]{:S(2)}, u32[]{:S(2)}) collective-permute-start(f32[168,256]{1,0:T(8,128)S(1)} %get-tuple-element.16), channel_id=1, source_target_pairs={{0,1},{1,0},{2,3},{3,2},{4,5},{5,4},{6,7},{7,6},{8,9},{9,8},{10,11... | collective-permute-start | bytes 516104 | tf_op jit(solution)/shard_map/ppermute | solution.py:539
  2.7 10.4 %collective-permute-start.2 = (f32[168,256]{1,0:T(8,128)S(1)}, f32[168,256]{1,0:T(8,128)S(1)}, u32[]{:S(2)}, u32[]{:S(2)}) collective-permute-start(f32[168,256]{1,0:T(8,128)S(1)} %get-tuple-element.17), channel_id=1, source_target_pairs={{1,2},{2,1},{3,4},{4,3},{5,6},{6,5},{7,8},{8,7},{9,10},{10,9},{11,... | collective-permute-start | bytes 516104 | tf_op jit(solution)/shard_map/ppermute | solution.py:540
  9.9 12.1 %collective-permute-start = (f32[160,256]{1,0:T(8,128)S(1)}, f32[160,256]{1,0:T(8,128)S(1)}, u32[]{:S(2)}, u32[]{:S(2)}) collective-permute-start(f32[160,256]{1,0:T(8,128)S(1)} %get-tuple-element.15), channel_id=1, source_target_pairs={{16,32},{32,16},{48,64},{64,48},{80,96},{96,80},{112,128},{128,112... | collective-permute-start | bytes 491528 | tf_op jit(solution)/shard_map/ppermute | solution.py:541
  13.1 11.6 %collective-permute-start.4 = (f32[216,256]{1,0:T(8,128)S(1)}, f32[216,256]{1,0:T(8,128)S(1)}, u32[]{:S(2)}, u32[]{:S(2)}) collective-permute-start(f32[216,256]{1,0:T(8,128)S(1)} %get-tuple-element.20), channel_id=1, source_target_pairs={{0,16},{16,0},{32,48},{48,32},{64,80},{80,64},{96,112},{112,96},{1... | collective-permute-start | bytes 663560 | tf_op jit(solution)/shard_map/ppermute | solution.py:550
  19.2 5.5 %collective-permute-start.3 = (f32[56,256]{1,0:T(8,128)S(1)}, f32[56,256]{1,0:T(8,128)S(1)}, u32[]{:S(2)}, u32[]{:S(2)}) collective-permute-start(f32[56,256]{1,0:T(8,128)S(1)} %get-tuple-element.19), channel_id=1, source_target_pairs={{16,32},{32,16},{48,64},{64,48},{80,96},{96,80},{112,128},{128,112... | collective-permute-start | bytes 172040 | tf_op jit(solution)/shard_map/ppermute | solution.py:549

commit v10 on v9

--- a/solution.py
+++ b/solution.py
@@ -16,6 +16,7 @@
 LAT_ROWS = (3, 3, 4)
 ROWS = sum(LAT_ROWS)
 MAIN_ROWS = 160
+BLOCKS = 2
 LON_ROWS = 192
 
 time_step = 0.6
@@ -413,7 +414,17 @@
 
 
 def finish_kernel(
-    packed_ref, state_ref, analysis_ref, transform_ref, moved_ref, matrix_ref, sems
+    packed_ref,
+    state_ref,
+    analysis_ref,
+    transform_ref,
+    moved_ref,
+    matrix_ref,
+    split_ref,
+    product_ref,
+    square_ref,
+    level_ref,
+    sems,
 ):
     half = packed_ref.shape[1]
     members = 2 * half
@@ -436,22 +447,59 @@
         jnp.sum(jnp.sum(system * system, axis=0, keepdims=True), axis=1, keepdims=True)
     )
     root = system * (1.0 / scaler)
+    block = members // BLOCKS
+    spans = [slice(k * block, (k + 1) * block) for k in range(BLOCKS)]
+
+    def store(target, rows, value):
+        high, low = halves(value)
+        split_ref[target, 0, rows] = high
+        split_ref[target, 1, rows] = low
+
+    def multiply(left, right, use):
+        high, low = split_ref[right, 0], split_ref[right, 1]
+        deep = jnp.concatenate([high, low, high], axis=0)
+        for rows in spans:
+            high, low = split_ref[left, 0, rows], split_ref[left, 1, rows]
+            wide = jnp.concatenate([high, high, low], axis=1)
+            use(rows, jnp.dot(wide, deep, preferred_element_type=jnp.float32))
+
     level = jnp.where(on_diagonal, 2.25, 0.0)
-
-    product = root
+    level_ref[...] = level
+    product_ref[...] = root
+    product, square, mixed, factor, turned_product = range(5)
+    inverse, inverse_next = 5, 6
+    for rows in spans:
+        store(product, rows, root[rows])
+
+    def use_square(rows, value):
+        square_ref[rows] = value
+        store(square, rows, value)
+        store(mixed, rows, 0.0625 * value - 0.5625 * product_ref[rows])
+
+    def use_higher(target, rows, value):
+        value = value + (level_ref[rows] - 2.4375 * product_ref[rows] + 1.6875 * square_ref[rows])
+        store(target, rows, value)
+
+    def use_product(rows, value):
+        product_ref[rows] = value
+        store(product, rows, value)
+
+    def use_last(rows, value):
+        matrix_ref[rows] = value
+
     for step in range(0, NS_ITERS, 2):
-        split = halves(product)
-        square = dot3(split, split)
-        higher = dot3(halves(square), halves(0.0625 * square - 0.5625 * product))
-        factor = halves(level - 2.4375 * product + 1.6875 * square + higher)
-        if step == 0:
-            inverse = factor
-        elif step < NS_ITERS - 2:
-            inverse = halves(dot3(factor, inverse))
+        multiply(product, product, use_square)
+        target = inverse if step == 0 else factor
+        multiply(square, mixed, functools.partial(use_higher, target))
+        if step < NS_ITERS - 2:
+            multiply(target, product, functools.partial(store, turned_product))
+            if step > 0:
+                multiply(factor, inverse, functools.partial(store, inverse_next))
+                inverse, inverse_next = inverse_next, inverse
+            multiply(target, turned_product, use_product)
         else:
-            inverse = dot3(factor, inverse)
-        if step < NS_ITERS - 2:
-            product = dot3(factor, halves(dot3(factor, split)))
+            multiply(factor, inverse, use_last)
+    inverse = matrix_ref[...]
     projected = jnp.concatenate(
         [packed_ref[2 * half + 1 : 2 * half + 2], packed_ref[2 * half + 2 : 2 * half + 3]], axis=1
     )
@@ -483,6 +531,10 @@
         [pltpu.VMEM] * 2,
         [
             pltpu.VMEM(state.shape, jnp.float32),
+            pltpu.VMEM(square, jnp.float32),
+            pltpu.VMEM((7, 2) + square, jnp.bfloat16),
+            pltpu.VMEM(square, jnp.float32),
+            pltpu.VMEM(square, jnp.float32),
             pltpu.VMEM(square, jnp.float32),
             pltpu.SemaphoreType.DMA((1 + state.shape[0] // 128,)),
         ],

time: 86.7 us -> 86.1 us (level)
  no operation moved by 1% of the time
where the time goes in v10:
time: 86.1 us; the launch traced here: 85.7 us
  blocking collectives  54.7 us (64%)
  starting transfers between devices  17.8 us (21%)
  Pallas kernels  8.17 us (9%)
  waiting for transfers between devices  3.85 us (4%)
    all_to_all x1, blocking collectives, reduced(): lax.all_to_all(jnp.broadcast_to(piece[None], (lat, 1, width)), 'lat', 0, 0)  28 us
    all_to_all x1, blocking collectives, reduced(): pieces = lax.all_to_all(packed.reshape(lon, 1, width), 'lon', 0, 0)  13.8 us
    all_to_all x1, blocking collectives, reduced(): lax.all_to_all(jnp.broadcast_to(piece[None], (lon, 1, width)), 'lon', 0, 0)  12.9 us
    ppermute x1, starting transfers between devices, local(): second = lax.ppermute(second, ('lon', 'lat'), pairs[1])  7.24 us
    ppermute x1, starting transfers between devices, local(): within = lax.ppermute(out_within, 'lon', within)  6.04 us
    pallas_call x1, Pallas kernels, finish(): on_core(finish_kernel, (state.shape, square), [pltpu.VMEM] * 2, [pltpu.VM...  4.44 us
    ppermute x1, waiting for transfers between devices, local(): across = lax.ppermute(out_across, 'lon', across)  2.64 us
    ppermute x1, starting transfers between devices, local(): ahead = lax.ppermute(ahead, 'lon', across)  1.92 us
  transfers between devices with their start and end apart: 5, of which 2 were waited for; matrix products, arithmetic and copies ran while one was open for 0% of the time, Pallas kernels for 1%

profile of v10, /device:TPU:1, one launch (start us, length us, event | category | flops | bytes accessed | tf_op | source)
XLA Modules:
  0.0 85.7 jit_solution(2542192058721017236)
XLA Ops:
  0.6 0.0 copy-start
  0.6 1.3 %shard_map.68 = (f32[168,256]{1,0:T(8,128)S(1)}, f32[168,256]{1,0:T(8,128)S(1)}, f32[160,256]{1,0:T(8,128)S(1)}, f32[16,128]{1,0:T(8,128)S(1)}) custom-call(s32[1]{0:T(128)} %bitcast.parity_ref, f32[3,16,16,256]{3,2,1,0:T(8,128)} %state_ref.3, s32[16,16]{1,0:T(8,128)} %bathymetry_ref.1), custom_call_target="tpu_custom_call" | custom-call | tf_op jit(solution)/shard_map/pallas_call | solution.py:570
  2.0 0.7 collective-permute-start.1
  2.7 7.2 %collective-permute-start.2 = (f32[168,256]{1,0:T(8,128)S(1)}, f32[168,256]{1,0:T(8,128)S(1)}, u32[]{:S(2)}, u32[]{:S(2)}) collective-permute-start(f32[168,256]{1,0:T(8,128)S(1)} %get-tuple-element.17), channel_id=1, source_target_pairs={{1,2},{2,1},{3,4},{4,3},{5,6},{6,5},{7,8},{8,7},{9,10},{10,9},{11,... | collective-permute-start | bytes 516104 | tf_op jit(solution)/shard_map/ppermute | solution.py:592
  9.9 1.9 %collective-permute-start = (f32[160,256]{1,0:T(8,128)S(1)}, f32[160,256]{1,0:T(8,128)S(1)}, u32[]{:S(2)}, u32[]{:S(2)}) collective-permute-start(f32[160,256]{1,0:T(8,128)S(1)} %get-tuple-element.15), channel_id=1, source_target_pairs={{16,32},{32,16},{48,64},{64,48},{80,96},{96,80},{112,128},{128,112... | collective-permute-start | bytes 491528 | tf_op jit(solution)/shard_map/ppermute | solution.py:593
  11.8 0.0 collective-permute-done.1.first_ref
  11.8 1.2 %collective-permute-done.2.second_ref = f32[168,256]{1,0:T(8,128)S(1)} collective-permute-done((f32[168,256]{1,0:T(8,128)S(1)}, f32[168,256]{1,0:T(8,128)S(1)}, u32[]{:S(2)}, u32[]{:S(2)}) %collective-permute-start.2) | collective-permute-done | bytes 172064 | tf_op jit(solution)/shard_map/ppermute | solution.py:592
  13.1 0.0 copy-done
  13.1 0.1 shard_map.69
  13.1 6.0 %collective-permute-start.4 = (f32[216,256]{1,0:T(8,128)S(1)}, f32[216,256]{1,0:T(8,128)S(1)}, u32[]{:S(2)}, u32[]{:S(2)}) collective-permute-start(f32[216,256]{1,0:T(8,128)S(1)} %get-tuple-element.20), channel_id=1, source_target_pairs={{0,16},{16,0},{32,48},{48,32},{64,80},{80,64},{96,112},{112,96},{1... | collective-permute-start | bytes 663560 | tf_op jit(solution)/shard_map/ppermute | solution.py:602
  19.2 1.9 %collective-permute-start.3 = (f32[56,256]{1,0:T(8,128)S(1)}, f32[56,256]{1,0:T(8,128)S(1)}, u32[]{:S(2)}, u32[]{:S(2)}) collective-permute-start(f32[56,256]{1,0:T(8,128)S(1)} %get-tuple-element.19), channel_id=1, source_target_pairs={{16,32},{32,16},{48,64},{64,48},{80,96},{96,80},{112,128},{128,112... | collective-permute-start | bytes 172040 | tf_op jit(solution)/shard_map/ppermute | solution.py:601
  21.1 0.1 iota.9.turning_ref
  21.2 0.1 iota.10.inside_ref
  21.3 0.8 shard_map.70
  22.0 0.0 collective-permute-done.ahead_ref
  22.0 2.6 %collective-permute-done.3.across_ref = f32[56,256]{1,0:T(8,128)S(1)} collective-permute-done((f32[56,256]{1,0:T(8,128)S(1)}, f32[56,256]{1,0:T(8,128)S(1)}, u32[]{:S(2)}, u32[]{:S(2)}) %collective-permute-start.3) | collective-permute-done | bytes 57376 | tf_op jit(solution)/shard_map/ppermute | solution.py:601
  24.7 0.0 collective-permute-done.4.within_ref
  24.7 1.6 %shard_map.71 = (f32[768,256]{1,0:T(8,128)S(1)}, f32[288,128]{1,0:T(8,128)S(1)}) custom-call(s32[1]{0:T(128)} %bitcast.parity_ref, f32[160,256]{1,0:T(8,128)S(1)} %collective-permute-done.ahead_ref, f32[56,256]{1,0:T(8,128)S(1)} %collective-permute-done.3.across_ref, f32[216,256]{1,0:T(8,128)S(1)} %collective-permute-done.4.within_ref, ...), custom_call_target="tpu_custom_call" | custom-call | tf_op jit(solution)/shard_map/pallas_call | solution.py:611
  26.3 13.8 %all_to_all.15 = f32[32,1,1152]{2,1,0:T(1,128)S(1)} all-to-all(f32[32,1,1152]{2,1,0:T(1,128)S(1)} %bitcast.5), channel_id=1, replica_groups=mesh['lon'=32,'lat'=16] {'lon'}, dimensions={0} | all-to-all | bytes 294912 | tf_op jit(solution)/shard_map/all_to_all | solution.py:549
  40.1 0.1 reduce_sum.18
  40.3 28.0 %all_to_all.16 = f32[16,1,1152]{2,1,0:T(1,128)S(1)} all-to-all(f32[16,1,1152]{2,1,0:T(1,128)S(1)} %broadcast_in_dim.4), channel_id=1, replica_groups=mesh['lon'=32,'lat'=16] {'lat'}, dimensions={0} | all-to-all | bytes 147456 | tf_op jit(solution)/shard_map/all_to_all | solution.py:551
  68.2 0.1 reduce_sum.19
  68.3 0.1 broadcast_in_dim.5
  68.4 12.9 %all_to_all.17 = f32[32,1,1152]{2,1,0:T(1,128)S(1)} all-to-all(f32[32,1,1152]{2,1,0:T(1,128)S(1)} %broadcast_in_dim.5), channel_id=1, replica_groups=mesh['lon'=32,'lat'=16] {'lon'}, dimensions={0} | all-to-all | bytes 294912 | tf_op jit(solution)/shard_map/all_to_all | solution.py:553
  81.3 4.4 %shard_map.72 = (f32[768,256]{1,0:T(8,128)}, f32[256,256]{1,0:T(8,128)}) custom-call(f32[288,128]{1,0:T(8,128)S(1)} %bitcast.4, f32[768,256]{1,0:T(8,128)S(1)} %get-tuple-element.25.state_ref), custom_call_target="tpu_custom_call" | custom-call | tf_op jit(solution)/shard_map/pallas_call | solution.py:528
  (3 shorter events, 0.1 us)
Async XLA Ops:
  0.6 12.4 %copy-start = (f32[3,16,16,256]{3,2,1,0:T(8,128)S(1)}, f32[3,16,16,256]{3,2,1,0:T(8,128)}, u32[]{:S(2)}) copy-start(f32[3,16,16,256]{3,2,1,0:T(8,128)} %state_ref.3) | copy-start | bytes 2359300
  2.0 9.9 %collective-permute-start.1 = (f32[168,256]{1,0:T(8,128)S(1)}, f32[168,256]{1,0:T(8,128)S(1)}, u32[]{:S(2)}, u32[]{:S(2)}) collective-permute-start(f32[168,256]{1,0:T(8,128)S(1)} %get-tuple-element.16), channel_id=1, source_target_pairs={{0,1},{1,0},{2,3},{3,2},{4,5},{5,4},{6,7},{7,6},{8,9},{9,8},{10,11... | collective-permute-start | bytes 516104 | tf_op jit(solution)/shard_map/ppermute | solution.py:591
  2.7 10.4 %collective-permute-start.2 = (f32[168,256]{1,0:T(8,128)S(1)}, f32[168,256]{1,0:T(8,128)S(1)}, u32[]{:S(2)}, u32[]{:S(2)}) collective-permute-start(f32[168,256]{1,0:T(8,128)S(1)} %get-tuple-element.17), channel_id=1, source_target_pairs={{1,2},{2,1},{3,4},{4,3},{5,6},{6,5},{7,8},{8,7},{9,10},{10,9},{11,... | collective-permute-start | bytes 516104 | tf_op jit(solution)/shard_map/ppermute | solution.py:592
  9.9 12.1 %collective-permute-start = (f32[160,256]{1,0:T(8,128)S(1)}, f32[160,256]{1,0:T(8,128)S(1)}, u32[]{:S(2)}, u32[]{:S(2)}) collective-permute-start(f32[160,256]{1,0:T(8,128)S(1)} %get-tuple-element.15), channel_id=1, source_target_pairs={{16,32},{32,16},{48,64},{64,48},{80,96},{96,80},{112,128},{128,112... | collective-permute-start | bytes 491528 | tf_op jit(solution)/shard_map/ppermute | solution.py:593
  13.1 11.6 %collective-permute-start.4 = (f32[216,256]{1,0:T(8,128)S(1)}, f32[216,256]{1,0:T(8,128)S(1)}, u32[]{:S(2)}, u32[]{:S(2)}) collective-permute-start(f32[216,256]{1,0:T(8,128)S(1)} %get-tuple-element.20), channel_id=1, source_target_pairs={{0,16},{16,0},{32,48},{48,32},{64,80},{80,64},{96,112},{112,96},{1... | collective-permute-start | bytes 663560 | tf_op jit(solution)/shard_map/ppermute | solution.py:602
  19.2 5.5 %collective-permute-start.3 = (f32[56,256]{1,0:T(8,128)S(1)}, f32[56,256]{1,0:T(8,128)S(1)}, u32[]{:S(2)}, u32[]{:S(2)}) collective-permute-start(f32[56,256]{1,0:T(8,128)S(1)} %get-tuple-element.19), channel_id=1, source_target_pairs={{16,32},{32,16},{48,64},{64,48},{80,96},{96,80},{112,128},{128,112... | collective-permute-start | bytes 172040 | tf_op jit(solution)/shard_map/ppermute | solution.py:601

commit v11 on v10

--- a/solution.py
+++ b/solution.py
@@ -59,15 +59,15 @@
                 up_ref[at : at + count] = plane[lat - count :]
                 down_ref[at : at + count] = plane[:count]
 
-    @pl.when(parity_ref[0] & 1 == 0)
+    @pl.when(parity_ref[0] == 0)
     def _():
         pack(first_ref, second_ref)
 
-    @pl.when(parity_ref[0] & 1 == 1)
+    @pl.when(parity_ref[0] == 1)
     def _():
         pack(second_ref, first_ref)
 
-    even_lon = parity_ref[0] < 2
+    even_lon = parity_ref[0] == 0
     for field, distance, _, main, _ in lon_layout():
         down, up = state_ref[field, distance - 1], state_ref[field, lon - distance]
         ahead_ref[main : main + TILE] = jnp.where(even_lon, down, up)
@@ -96,15 +96,15 @@
     parity_ref, state_ref, first_ref, second_ref, depth_ref, across_ref, within_ref, strip_ref
 ):
     lon = state_ref.shape[1]
-    even = parity_ref[0] & 1 == 0
-    low_rows = functools.partial(lat_rows, even, second_ref, first_ref)
-    high_rows = functools.partial(lat_rows, even, first_ref, second_ref)
+    even = parity_ref[0] == 0
+    low_rows = functools.partial(lat_rows, even, first_ref, second_ref)
+    high_rows = functools.partial(lat_rows, even, second_ref, first_ref)
     depth_at = ROWS * lon
     strip_ref[...] = jnp.zeros_like(strip_ref)
     depths = slice(depth_at, depth_at + 3)
-    strip_ref[1:4] = chosen(even, second_ref, first_ref, depths, slice(0, 128))
+    strip_ref[1:4] = chosen(even, first_ref, second_ref, depths, slice(0, 128))
     strip_ref[4:20] = depth_ref[...]
-    strip_ref[20:23] = chosen(even, first_ref, second_ref, depths, slice(0, 128))
+    strip_ref[20:23] = chosen(even, second_ref, first_ref, depths, slice(0, 128))
     for ref, skipped in ((across_ref, MAIN_ROWS), (within_ref, 0)):
         depths = slice(LON_ROWS - skipped, None)
         ref[depths, 128:] = jnp.zeros((strip_ref.shape[0], 128), jnp.float32)
@@ -127,11 +127,11 @@
                 if not skipped:
                     ref[main : main + TILE] = state_ref[field, x]
 
-    @pl.when(parity_ref[0] < 2)
+    @pl.when(parity_ref[0] == 0)
     def _():
         pack(False)
 
-    @pl.when(parity_ref[0] >= 2)
+    @pl.when(parity_ref[0] == 1)
     def _():
         pack(True)
 
@@ -192,9 +192,9 @@
 ):
     lon = state_ref.shape[1]
     shape = field_ref.shape[2:]
-    even = parity_ref[0] & 1 == 0
-    low_rows = functools.partial(lat_rows, even, second_ref, first_ref)
-    high_rows = functools.partial(lat_rows, even, first_ref, second_ref)
+    even = parity_ref[0] == 0
+    low_rows = functools.partial(lat_rows, even, first_ref, second_ref)
+    high_rows = functools.partial(lat_rows, even, second_ref, first_ref)
     for field, count in enumerate(LAT_ROWS):
         for x in range(lon):
             field_ref[field, x, REACH : REACH + TILE] = state_ref[field, x]
@@ -277,7 +277,7 @@
     members = shape[1]
     end = next_ref.shape[1]
     lon = end - 2 * REACH
-    even_lon = parity_ref[0] < 2
+    even_lon = parity_ref[0] == 0
 
     def taken(rows, lanes=slice(None)):
         start, stop = rows
@@ -565,8 +565,7 @@
     lat_shape = (ROWS * lon + 8, members)
     lon_shape = (LON_ROWS + wide, members)
     here = lax.axis_index("lon")
-    parity = ((here + lax.axis_index("lat")) & 1) + 2 * (here & 1)
-    parity = parity.reshape(1)
+    parity = (here & 1).reshape(1)
     first, second, ahead, depth = on_core(
         pack_lat_kernel,
         (lat_shape, lat_shape, (MAIN_ROWS, members), (lat, 128)),
@@ -586,7 +585,8 @@
         for b in range(rows_of):
             ours = a * rows_of + b
             if b + 1 < rows_of:
-                pairs[(a + b) % 2].extend(((ours, ours + 1), (ours + 1, ours)))
+                pairs[a % 2].append((ours, ours + 1))
+                pairs[1 - a % 2].append((ours + 1, ours))
         (across if a % 2 else within).extend(((a, (a + 1) % columns), ((a + 1) % columns, a)))
     first = lax.ppermute(first, ("lon", "lat"), pairs[0])
     second = lax.ppermute(second, ("lon", "lat"), pairs[1])

time: 86.1 us -> 85.6 us (level)
  starting transfers between devices: 17.8 us -> 19.2 us
  waiting for transfers between devices: 3.85 us -> 2.65 us
    ppermute x1, starting transfers between devices: 7.24 us -> 5 us  [local(): second = lax.ppermute(second, ('lon', 'lat'), pairs[1])]
    all_to_all x1, blocking collectives: 28 us -> 26.3 us  [reduced(): lax.all_to_all(jnp.broadcast_to(piece[None], (lat, 1, width)), 'lat', 0, 0)]
    ppermute x1, starting transfers between devices: 6.04 us -> 7.67 us  [local(): within = lax.ppermute(out_within, 'lon', within)]
    ppermute x1, starting transfers between devices: 1.92 us -> 3.34 us  [local(): ahead = lax.ppermute(ahead, 'lon', across)]
    ppermute x1, waiting for transfers between devices: 1.2 us -> 0.01 us  [local(): second = lax.ppermute(second, ('lon', 'lat'), pairs[1])]
    all_to_all x1, blocking collectives: 13.8 us -> 14.8 us  [reduced(): pieces = lax.all_to_all(packed.reshape(lon, 1, width), 'lon', 0, 0)]
  transfers between devices with their start and end apart: 5 -> 5, of which waited for: 2 -> 1; matrix products, arithmetic and copies ran while one was open for 0% -> 0% of each run, Pallas kernels for 1% -> 1%
where the time goes in v11:
time: 85.6 us; the launch traced here: 85.3 us
  blocking collectives  54 us (63%)
  starting transfers between devices  19.2 us (22%)
  Pallas kernels  8.18 us (10%)
  waiting for transfers between devices  2.65 us (3%)
    all_to_all x1, blocking collectives, reduced(): lax.all_to_all(jnp.broadcast_to(piece[None], (lat, 1, width)), 'lat', 0, 0)  26.3 us
    all_to_all x1, blocking collectives, reduced(): pieces = lax.all_to_all(packed.reshape(lon, 1, width), 'lon', 0, 0)  14.8 us
    all_to_all x1, blocking collectives, reduced(): lax.all_to_all(jnp.broadcast_to(piece[None], (lon, 1, width)), 'lon', 0, 0)  12.9 us
    ppermute x1, starting transfers between devices, local(): within = lax.ppermute(out_within, 'lon', within)  7.67 us
    ppermute x1, starting transfers between devices, local(): second = lax.ppermute(second, ('lon', 'lat'), pairs[1])  5 us
    pallas_call x1, Pallas kernels, finish(): on_core(finish_kernel, (state.shape, square), [pltpu.VMEM] * 2, [pltpu.VM...  4.45 us
    ppermute x1, starting transfers between devices, local(): ahead = lax.ppermute(ahead, 'lon', across)  3.34 us
    ppermute x1, waiting for transfers between devices, local(): across = lax.ppermute(out_across, 'lon', across)  2.64 us
  transfers between devices with their start and end apart: 5, of which 1 were waited for; matrix products, arithmetic and copies ran while one was open for 0% of the time, Pallas kernels for 1%

profile of v11, /device:TPU:1, one launch (start us, length us, event | category | flops | bytes accessed | tf_op | source)
XLA Modules:
  0.0 85.3 jit_solution(9115920197413270240)
XLA Ops:
  0.6 0.0 copy-start
  0.6 1.3 %shard_map.68 = (f32[168,256]{1,0:T(8,128)S(1)}, f32[168,256]{1,0:T(8,128)S(1)}, f32[160,256]{1,0:T(8,128)S(1)}, f32[16,128]{1,0:T(8,128)S(1)}) custom-call(s32[1]{0:T(128)} %bitcast.parity_ref, f32[3,16,16,256]{3,2,1,0:T(8,128)} %state_ref.3, s32[16,16]{1,0:T(8,128)} %bathymetry_ref.1), custom_call_target="tpu_custom_call" | custom-call | tf_op jit(solution)/shard_map/pallas_call | solution.py:569
  2.0 1.3 %collective-permute-start.1 = (f32[168,256]{1,0:T(8,128)S(1)}, f32[168,256]{1,0:T(8,128)S(1)}, u32[]{:S(2)}, u32[]{:S(2)}) collective-permute-start(f32[168,256]{1,0:T(8,128)S(1)} %get-tuple-element.16), channel_id=1, source_target_pairs={{0,1},{1,2},{2,3},{3,4},{4,5},{5,6},{6,7},{7,8},{8,9},{9,10},{10,1... | collective-permute-start | bytes 516104 | tf_op jit(solution)/shard_map/ppermute | solution.py:591
  3.3 5.0 %collective-permute-start.2 = (f32[168,256]{1,0:T(8,128)S(1)}, f32[168,256]{1,0:T(8,128)S(1)}, u32[]{:S(2)}, u32[]{:S(2)}) collective-permute-start(f32[168,256]{1,0:T(8,128)S(1)} %get-tuple-element.17), channel_id=1, source_target_pairs={{1,0},{2,1},{3,2},{4,3},{5,4},{6,5},{7,6},{8,7},{9,8},{10,9},{11,1... | collective-permute-start | bytes 516104 | tf_op jit(solution)/shard_map/ppermute | solution.py:592
  8.3 3.3 %collective-permute-start = (f32[160,256]{1,0:T(8,128)S(1)}, f32[160,256]{1,0:T(8,128)S(1)}, u32[]{:S(2)}, u32[]{:S(2)}) collective-permute-start(f32[160,256]{1,0:T(8,128)S(1)} %get-tuple-element.15), channel_id=1, source_target_pairs={{16,32},{32,16},{48,64},{64,48},{80,96},{96,80},{112,128},{128,112... | collective-permute-start | bytes 491528 | tf_op jit(solution)/shard_map/ppermute | solution.py:593
  11.6 0.0 collective-permute-done.1.first_ref
  11.6 0.0 collective-permute-done.2.second_ref
  11.7 0.0 copy-done
  11.7 0.1 shard_map.69
  11.7 7.7 %collective-permute-start.4 = (f32[216,256]{1,0:T(8,128)S(1)}, f32[216,256]{1,0:T(8,128)S(1)}, u32[]{:S(2)}, u32[]{:S(2)}) collective-permute-start(f32[216,256]{1,0:T(8,128)S(1)} %get-tuple-element.20), channel_id=1, source_target_pairs={{0,16},{16,0},{32,48},{48,32},{64,80},{80,64},{96,112},{112,96},{1... | collective-permute-start | bytes 663560 | tf_op jit(solution)/shard_map/ppermute | solution.py:602
  19.4 1.9 %collective-permute-start.3 = (f32[56,256]{1,0:T(8,128)S(1)}, f32[56,256]{1,0:T(8,128)S(1)}, u32[]{:S(2)}, u32[]{:S(2)}) collective-permute-start(f32[56,256]{1,0:T(8,128)S(1)} %get-tuple-element.19), channel_id=1, source_target_pairs={{16,32},{32,16},{48,64},{64,48},{80,96},{96,80},{112,128},{128,112... | collective-permute-start | bytes 172040 | tf_op jit(solution)/shard_map/ppermute | solution.py:601
  21.4 0.1 iota.9.turning_ref
  21.4 0.1 iota.10.inside_ref
  21.5 0.8 shard_map.70
  22.3 0.0 collective-permute-done.ahead_ref
  22.3 2.6 %collective-permute-done.3.across_ref = f32[56,256]{1,0:T(8,128)S(1)} collective-permute-done((f32[56,256]{1,0:T(8,128)S(1)}, f32[56,256]{1,0:T(8,128)S(1)}, u32[]{:S(2)}, u32[]{:S(2)}) %collective-permute-start.3) | collective-permute-done | bytes 57376 | tf_op jit(solution)/shard_map/ppermute | solution.py:601
  24.9 0.0 collective-permute-done.4.within_ref
  24.9 1.6 %shard_map.71 = (f32[768,256]{1,0:T(8,128)S(1)}, f32[288,128]{1,0:T(8,128)S(1)}) custom-call(s32[1]{0:T(128)} %bitcast.parity_ref, f32[160,256]{1,0:T(8,128)S(1)} %collective-permute-done.ahead_ref, f32[56,256]{1,0:T(8,128)S(1)} %collective-permute-done.3.across_ref, f32[216,256]{1,0:T(8,128)S(1)} %collective-permute-done.4.within_ref, ...), custom_call_target="tpu_custom_call" | custom-call | tf_op jit(solution)/shard_map/pallas_call | solution.py:611
  26.5 14.8 %all_to_all.15 = f32[32,1,1152]{2,1,0:T(1,128)S(1)} all-to-all(f32[32,1,1152]{2,1,0:T(1,128)S(1)} %bitcast.5), channel_id=1, replica_groups=mesh['lon'=32,'lat'=16] {'lon'}, dimensions={0} | all-to-all | bytes 294912 | tf_op jit(solution)/shard_map/all_to_all | solution.py:549
  41.3 0.1 reduce_sum.18
  41.5 26.3 %all_to_all.16 = f32[16,1,1152]{2,1,0:T(1,128)S(1)} all-to-all(f32[16,1,1152]{2,1,0:T(1,128)S(1)} %broadcast_in_dim.4), channel_id=1, replica_groups=mesh['lon'=32,'lat'=16] {'lat'}, dimensions={0} | all-to-all | bytes 147456 | tf_op jit(solution)/shard_map/all_to_all | solution.py:551
  67.8 0.1 reduce_sum.19
  67.8 0.1 broadcast_in_dim.5
  67.9 12.9 %all_to_all.17 = f32[32,1,1152]{2,1,0:T(1,128)S(1)} all-to-all(f32[32,1,1152]{2,1,0:T(1,128)S(1)} %broadcast_in_dim.5), channel_id=1, replica_groups=mesh['lon'=32,'lat'=16] {'lon'}, dimensions={0} | all-to-all | bytes 294912 | tf_op jit(solution)/shard_map/all_to_all | solution.py:553
  80.8 4.4 %shard_map.72 = (f32[768,256]{1,0:T(8,128)}, f32[256,256]{1,0:T(8,128)}) custom-call(f32[288,128]{1,0:T(8,128)S(1)} %bitcast.4, f32[768,256]{1,0:T(8,128)S(1)} %get-tuple-element.25.state_ref), custom_call_target="tpu_custom_call" | custom-call | tf_op jit(solution)/shard_map/pallas_call | solution.py:528
  (3 shorter events, 0.1 us)
Async XLA Ops:
  0.6 11.0 %copy-start = (f32[3,16,16,256]{3,2,1,0:T(8,128)S(1)}, f32[3,16,16,256]{3,2,1,0:T(8,128)}, u32[]{:S(2)}) copy-start(f32[3,16,16,256]{3,2,1,0:T(8,128)} %state_ref.3) | copy-start | bytes 2359300
  2.0 9.7 %collective-permute-start.1 = (f32[168,256]{1,0:T(8,128)S(1)}, f32[168,256]{1,0:T(8,128)S(1)}, u32[]{:S(2)}, u32[]{:S(2)}) collective-permute-start(f32[168,256]{1,0:T(8,128)S(1)} %get-tuple-element.16), channel_id=1, source_target_pairs={{0,1},{1,2},{2,3},{3,4},{4,5},{5,6},{6,7},{7,8},{8,9},{9,10},{10,1... | collective-permute-start | bytes 516104 | tf_op jit(solution)/shard_map/ppermute | solution.py:591
  3.3 8.4 %collective-permute-start.2 = (f32[168,256]{1,0:T(8,128)S(1)}, f32[168,256]{1,0:T(8,128)S(1)}, u32[]{:S(2)}, u32[]{:S(2)}) collective-permute-start(f32[168,256]{1,0:T(8,128)S(1)} %get-tuple-element.17), channel_id=1, source_target_pairs={{1,0},{2,1},{3,2},{4,3},{5,4},{6,5},{7,6},{8,7},{9,8},{10,9},{11,1... | collective-permute-start | bytes 516104 | tf_op jit(solution)/shard_map/ppermute | solution.py:592
  8.3 14.0 %collective-permute-start = (f32[160,256]{1,0:T(8,128)S(1)}, f32[160,256]{1,0:T(8,128)S(1)}, u32[]{:S(2)}, u32[]{:S(2)}) collective-permute-start(f32[160,256]{1,0:T(8,128)S(1)} %get-tuple-element.15), channel_id=1, source_target_pairs={{16,32},{32,16},{48,64},{64,48},{80,96},{96,80},{112,128},{128,112... | collective-permute-start | bytes 491528 | tf_op jit(solution)/shard_map/ppermute | solution.py:593
  11.7 13.2 %collective-permute-start.4 = (f32[216,256]{1,0:T(8,128)S(1)}, f32[216,256]{1,0:T(8,128)S(1)}, u32[]{:S(2)}, u32[]{:S(2)}) collective-permute-start(f32[216,256]{1,0:T(8,128)S(1)} %get-tuple-element.20), channel_id=1, source_target_pairs={{0,16},{16,0},{32,48},{48,32},{64,80},{80,64},{96,112},{112,96},{1... | collective-permute-start | bytes 663560 | tf_op jit(solution)/shard_map/ppermute | solution.py:602
  19.4 5.5 %collective-permute-start.3 = (f32[56,256]{1,0:T(8,128)S(1)}, f32[56,256]{1,0:T(8,128)S(1)}, u32[]{:S(2)}, u32[]{:S(2)}) collective-permute-start(f32[56,256]{1,0:T(8,128)S(1)} %get-tuple-element.19), channel_id=1, source_target_pairs={{16,32},{32,16},{48,64},{64,48},{80,96},{96,80},{112,128},{128,112... | collective-permute-start | bytes 172040 | tf_op jit(solution)/shard_map/ppermute | solution.py:601

commit v12 on v10

--- a/solution.py
+++ b/solution.py
@@ -35,7 +35,7 @@
 
 
 def pack_lat_kernel(
-    parity_ref, ensemble_ref, bathymetry_ref, first_ref, second_ref, ahead_ref, depth_ref, state_ref, bottom_ref, square_ref, sems
+    parity_ref, ensemble_ref, bathymetry_ref, first_ref, second_ref, ahead_ref, beside_ref, depth_ref, state_ref, bottom_ref, square_ref, sems
 ):
     lon, lat = state_ref.shape[1], state_ref.shape[2]
     copies = fetch((bathymetry_ref, ensemble_ref), (bottom_ref, state_ref), sems)
@@ -71,6 +71,7 @@
     for field, distance, _, main, _ in lon_layout():
         down, up = state_ref[field, distance - 1], state_ref[field, lon - distance]
         ahead_ref[main : main + TILE] = jnp.where(even_lon, down, up)
+        beside_ref[main : main + TILE] = jnp.where(even_lon, up, down)
 
 
 def chosen(even, first_ref, second_ref, rows, lanes=slice(None)):
@@ -105,27 +106,25 @@
     strip_ref[1:4] = chosen(even, second_ref, first_ref, depths, slice(0, 128))
     strip_ref[4:20] = depth_ref[...]
     strip_ref[20:23] = chosen(even, first_ref, second_ref, depths, slice(0, 128))
-    for ref, skipped in ((across_ref, MAIN_ROWS), (within_ref, 0)):
-        depths = slice(LON_ROWS - skipped, None)
-        ref[depths, 128:] = jnp.zeros((strip_ref.shape[0], 128), jnp.float32)
-        ref[LON_ROWS - 2 - skipped : LON_ROWS - skipped] = jnp.zeros((2, ref.shape[1]), jnp.float32)
-        ref[depths, :128] = strip_ref[...]
+    for ref in (across_ref, within_ref):
+        corners = LON_ROWS - MAIN_ROWS
+        ref[corners:, 128:] = jnp.zeros((strip_ref.shape[0], 128), jnp.float32)
+        ref[corners - 2 : corners] = jnp.zeros((2, ref.shape[1]), jnp.float32)
+        ref[corners:, :128] = strip_ref[...]
 
     def pack(upward):
-        for field, distance, beyond, main, corner in lon_layout():
+        for field, distance, beyond, _, corner in lon_layout():
             up, down = lon - distance, distance - 1
-            for ref, x, skipped in (
-                (across_ref, up if upward else down, MAIN_ROWS),
-                (within_ref, down if upward else up, 0),
+            for ref, x in (
+                (across_ref, up if upward else down),
+                (within_ref, down if upward else up),
             ):
                 if beyond:
-                    at = corner - skipped
+                    at = corner - MAIN_ROWS
                     low = low_rows(field, x, lon)
                     ref[at : at + beyond] = low[LAT_ROWS[field] - beyond :]
                     high = high_rows(field, x, lon)
                     ref[at + beyond : at + 2 * beyond] = high[:beyond]
-                if not skipped:
-                    ref[main : main + TILE] = state_ref[field, x]
 
     @pl.when(parity_ref[0] < 2)
     def _():
@@ -249,6 +248,7 @@
 def step_kernel(
     parity_ref,
     ahead_ref,
+    beside_ref,
     across_ref,
     within_ref,
     strip_ref,
@@ -282,10 +282,10 @@
     def taken(rows, lanes=slice(None)):
         start, stop = rows
         if stop <= MAIN_ROWS:
-            across = ahead_ref[start:stop, lanes]
+            across, within = ahead_ref[start:stop, lanes], beside_ref[start:stop, lanes]
         else:
-            across = across_ref[start - MAIN_ROWS : stop - MAIN_ROWS, lanes]
-        within = within_ref[start:stop, lanes]
+            rows = slice(start - MAIN_ROWS, stop - MAIN_ROWS)
+            across, within = across_ref[rows, lanes], within_ref[rows, lanes]
         return jnp.where(even_lon, across, within), jnp.where(even_lon, within, across)
 
     for field, distance, beyond, main, corner in lon_layout():
@@ -297,7 +297,7 @@
             west, east = taken(rows)
             field_ref[field, REACH - distance, at : at + count] = west
             field_ref[field, REACH - 1 + distance, at : at + count] = east
-    west_strip, east_strip = taken((LON_ROWS, within_ref.shape[0]), slice(0, 128))
+    west_strip, east_strip = taken((LON_ROWS, MAIN_ROWS + within_ref.shape[0]), slice(0, 128))
     turning = time_step * spread_out(turning_ref[:, :1], shape)
     keeper = spread_out(inside_ref[:, :1], shape)
     strips = [0.5 * time_step * strip for strip in (west_strip, strip_ref[...], east_strip)]
@@ -563,13 +563,14 @@
     inside = ((rows >= 0) & (rows < total_lat)).astype(jnp.float32)
     turning = rotation * (2.0 * (rows.astype(jnp.float32) + 0.5) / total_lat - 1.0)
     lat_shape = (ROWS * lon + 8, members)
-    lon_shape = (LON_ROWS + wide, members)
+    main_shape = (MAIN_ROWS, members)
+    lon_shape = (LON_ROWS - MAIN_ROWS + wide, members)
     here = lax.axis_index("lon")
     parity = ((here + lax.axis_index("lat")) & 1) + 2 * (here & 1)
     parity = parity.reshape(1)
-    first, second, ahead, depth = on_core(
+    first, second, ahead, beside, depth = on_core(
         pack_lat_kernel,
-        (lat_shape, lat_shape, (MAIN_ROWS, members), (lat, 128)),
+        (lat_shape, lat_shape, main_shape, main_shape, (lat, 128)),
         [pltpu.SMEM] + [pltpu.HBM] * 2,
         [
             pltpu.VMEM(ensemble.shape, jnp.float32),
@@ -591,9 +592,10 @@
     first = lax.ppermute(first, ("lon", "lat"), pairs[0])
     second = lax.ppermute(second, ("lon", "lat"), pairs[1])
     ahead = lax.ppermute(ahead, "lon", across)
+    beside = lax.ppermute(beside, "lon", within)
     out_across, out_within, strip = on_core(
         pack_lon_kernel,
-        ((LON_ROWS + wide - MAIN_ROWS, members), lon_shape, (wide, 128)),
+        (lon_shape, lon_shape, (wide, 128)),
         [pltpu.SMEM] + [vmem] * 4,
         [],
     )(parity, ensemble, first, second, depth)
@@ -611,7 +613,7 @@
     forecast, packed = on_core(
         step_kernel,
         ((fields * lon * lat, members), (members + 32, members // 2)),
-        [pltpu.SMEM] + [vmem] * 8 + [pltpu.HBM] * 3,
+        [pltpu.SMEM] + [vmem] * 9 + [pltpu.HBM] * 3,
         [
             pltpu.VMEM((fields, 2 * REACH) + planes[2:], jnp.float32),
             pltpu.VMEM(planes, jnp.float32),
@@ -624,6 +626,7 @@
     )(
         parity,
         ahead,
+        beside,
         across,
         within,
         strip,

time: 86.1 us -> 82.8 us (0.962)
  starting transfers between devices: 17.8 us -> 22.1 us
  blocking collectives: 54.7 us -> 50.8 us
  waiting for transfers between devices: 3.85 us -> 0.02 us
    ppermute x0 -> x1, starting transfers between devices: none -> 7.22 us  [local(): beside = lax.ppermute(beside, 'lon', within)]
    all_to_all x1, blocking collectives: 28 us -> 24.6 us  [reduced(): lax.all_to_all(jnp.broadcast_to(piece[None], (lat, 1, width)), 'lat', 0, 0)]
    ppermute x1, starting transfers between devices: 6.04 us -> 3.18 us  [local(): within = lax.ppermute(out_within, 'lon', within)]
    ppermute x1, waiting for transfers between devices: 2.64 us -> 0.01 us  [local(): across = lax.ppermute(out_across, 'lon', across)]
    ppermute x1, waiting for transfers between devices: 1.2 us -> 0.01 us  [local(): second = lax.ppermute(second, ('lon', 'lat'), pairs[1])]
  transfers between devices with their start and end apart: 5 -> 6, of which waited for: 2 -> 0; matrix products, arithmetic and copies ran while one was open for 0% -> 0% of each run, Pallas kernels for 1% -> 1%
where the time goes in v12:
time: 82.8 us; the launch traced here: 82.4 us
  blocking collectives  50.8 us (61%)
  starting transfers between devices  22.1 us (27%)
  Pallas kernels  8.19 us (10%)
    all_to_all x1, blocking collectives, reduced(): lax.all_to_all(jnp.broadcast_to(piece[None], (lat, 1, width)), 'lat', 0, 0)  24.6 us
    all_to_all x1, blocking collectives, reduced(): pieces = lax.all_to_all(packed.reshape(lon, 1, width), 'lon', 0, 0)  13.3 us
    all_to_all x1, blocking collectives, reduced(): lax.all_to_all(jnp.broadcast_to(piece[None], (lon, 1, width)), 'lon', 0, 0)  12.9 us
    ppermute x1, starting transfers between devices, local(): second = lax.ppermute(second, ('lon', 'lat'), pairs[1])  7.24 us
    ppermute x1, starting transfers between devices, local(): beside = lax.ppermute(beside, 'lon', within)  7.22 us
    pallas_call x1, Pallas kernels, finish(): on_core(finish_kernel, (state.shape, square), [pltpu.VMEM] * 2, [pltpu.VM...  4.45 us
    ppermute x1, starting transfers between devices, local(): within = lax.ppermute(out_within, 'lon', within)  3.18 us
    ppermute x1, starting transfers between devices, local(): ahead = lax.ppermute(ahead, 'lon', across)  1.92 us
  transfers between devices with their start and end apart: 6, of which 0 were waited for; matrix products, arithmetic and copies ran while one was open for 0% of the time, Pallas kernels for 1%

profile of v12, /device:TPU:1, one launch (start us, length us, event | category | flops | bytes accessed | tf_op | source)
XLA Modules:
  0.0 82.4 jit_solution(17358674961635495128)
XLA Ops:
  0.6 0.0 copy-start
  0.6 1.3 %shard_map.68 = (f32[168,256]{1,0:T(8,128)S(1)}, f32[168,256]{1,0:T(8,128)S(1)}, f32[160,256]{1,0:T(8,128)S(1)}, f32[160,256]{1,0:T(8,128)S(1)}, f32[16,128]{1,0:T(8,128)S(1)}) custom-call(s32[1]{0:T(128)} %bitcast.parity_ref, f32[3,16,16,256]{3,2,1,0:T(8,128)} %state_ref.3, s32[16,16]{1,0:T(8,128)} %bathymetry_ref.1), custom_call_target="tpu_custom_call" | custom-call | tf_op jit(solution)/shard_map/pallas_call | solution.py:571
  2.0 0.7 collective-permute-start.2
  2.7 7.2 %collective-permute-start.3 = (f32[168,256]{1,0:T(8,128)S(1)}, f32[168,256]{1,0:T(8,128)S(1)}, u32[]{:S(2)}, u32[]{:S(2)}) collective-permute-start(f32[168,256]{1,0:T(8,128)S(1)} %get-tuple-element.19), channel_id=1, source_target_pairs={{1,2},{2,1},{3,4},{4,3},{5,6},{6,5},{7,8},{8,7},{9,10},{10,9},{11,... | collective-permute-start | bytes 516104 | tf_op jit(solution)/shard_map/ppermute | solution.py:593
  9.9 1.9 %collective-permute-start = (f32[160,256]{1,0:T(8,128)S(1)}, f32[160,256]{1,0:T(8,128)S(1)}, u32[]{:S(2)}, u32[]{:S(2)}) collective-permute-start(f32[160,256]{1,0:T(8,128)S(1)} %get-tuple-element.16), channel_id=1, source_target_pairs={{16,32},{32,16},{48,64},{64,48},{80,96},{96,80},{112,128},{128,112... | collective-permute-start | bytes 491528 | tf_op jit(solution)/shard_map/ppermute | solution.py:594
  11.8 7.2 %collective-permute-start.1 = (f32[160,256]{1,0:T(8,128)S(1)}, f32[160,256]{1,0:T(8,128)S(1)}, u32[]{:S(2)}, u32[]{:S(2)}) collective-permute-start(f32[160,256]{1,0:T(8,128)S(1)} %get-tuple-element.17), channel_id=1, source_target_pairs={{0,16},{16,0},{32,48},{48,32},{64,80},{80,64},{96,112},{112,96},{1... | collective-permute-start | bytes 491528 | tf_op jit(solution)/shard_map/ppermute | solution.py:595
  19.1 0.0 collective-permute-done.2.first_ref
  19.1 0.0 collective-permute-done.3.second_ref
  19.1 0.0 copy-done
  19.1 0.1 shard_map.69
  19.2 1.9 %collective-permute-start.4 = (f32[56,256]{1,0:T(8,128)S(1)}, f32[56,256]{1,0:T(8,128)S(1)}, u32[]{:S(2)}, u32[]{:S(2)}) collective-permute-start(f32[56,256]{1,0:T(8,128)S(1)} %get-tuple-element.21), channel_id=1, source_target_pairs={{16,32},{32,16},{48,64},{64,48},{80,96},{96,80},{112,128},{128,112... | collective-permute-start | bytes 172040 | tf_op jit(solution)/shard_map/ppermute | solution.py:603
  21.1 3.2 %collective-permute-start.5 = (f32[56,256]{1,0:T(8,128)S(1)}, f32[56,256]{1,0:T(8,128)S(1)}, u32[]{:S(2)}, u32[]{:S(2)}) collective-permute-start(f32[56,256]{1,0:T(8,128)S(1)} %get-tuple-element.22), channel_id=1, source_target_pairs={{0,16},{16,0},{32,48},{48,32},{64,80},{80,64},{96,112},{112,96},{1... | collective-permute-start | bytes 172040 | tf_op jit(solution)/shard_map/ppermute | solution.py:604
  24.3 0.1 iota.9.turning_ref
  24.4 0.1 iota.10.inside_ref
  24.4 0.8 shard_map.70
  25.2 0.0 collective-permute-done.ahead_ref
  25.2 0.0 collective-permute-done.1.beside_ref
  25.2 0.0 collective-permute-done.4.across_ref
  25.2 0.0 collective-permute-done.5.within_ref
  25.3 1.6 %shard_map.71 = (f32[768,256]{1,0:T(8,128)S(1)}, f32[288,128]{1,0:T(8,128)S(1)}) custom-call(s32[1]{0:T(128)} %bitcast.parity_ref, f32[160,256]{1,0:T(8,128)S(1)} %collective-permute-done.ahead_ref, f32[160,256]{1,0:T(8,128)S(1)} %collective-permute-done.1.beside_ref, f32[56,256]{1,0:T(8,128)S(1)} %collective-permute-done.4.across_ref, ...), custom_call_target="tpu_custom_call" | custom-call | tf_op jit(solution)/shard_map/pallas_call | solution.py:613
  26.8 13.3 %all_to_all.15 = f32[32,1,1152]{2,1,0:T(1,128)S(1)} all-to-all(f32[32,1,1152]{2,1,0:T(1,128)S(1)} %bitcast.5), channel_id=1, replica_groups=mesh['lon'=32,'lat'=16] {'lon'}, dimensions={0} | all-to-all | bytes 294912 | tf_op jit(solution)/shard_map/all_to_all | solution.py:549
  40.1 0.1 reduce_sum.18
  40.3 24.6 %all_to_all.16 = f32[16,1,1152]{2,1,0:T(1,128)S(1)} all-to-all(f32[16,1,1152]{2,1,0:T(1,128)S(1)} %broadcast_in_dim.4), channel_id=1, replica_groups=mesh['lon'=32,'lat'=16] {'lat'}, dimensions={0} | all-to-all | bytes 147456 | tf_op jit(solution)/shard_map/all_to_all | solution.py:551
  64.9 0.1 reduce_sum.19
  65.0 0.1 broadcast_in_dim.5
  65.0 12.9 %all_to_all.17 = f32[32,1,1152]{2,1,0:T(1,128)S(1)} all-to-all(f32[32,1,1152]{2,1,0:T(1,128)S(1)} %broadcast_in_dim.5), channel_id=1, replica_groups=mesh['lon'=32,'lat'=16] {'lon'}, dimensions={0} | all-to-all | bytes 294912 | tf_op jit(solution)/shard_map/all_to_all | solution.py:553
  77.9 4.4 %shard_map.72 = (f32[768,256]{1,0:T(8,128)}, f32[256,256]{1,0:T(8,128)}) custom-call(f32[288,128]{1,0:T(8,128)S(1)} %bitcast.4, f32[768,256]{1,0:T(8,128)S(1)} %get-tuple-element.27.state_ref), custom_call_target="tpu_custom_call" | custom-call | tf_op jit(solution)/shard_map/pallas_call | solution.py:528
  (3 shorter events, 0.1 us)
Async XLA Ops:
  0.6 18.5 %copy-start = (f32[3,16,16,256]{3,2,1,0:T(8,128)S(1)}, f32[3,16,16,256]{3,2,1,0:T(8,128)}, u32[]{:S(2)}) copy-start(f32[3,16,16,256]{3,2,1,0:T(8,128)} %state_ref.3) | copy-start | bytes 2359300
  2.0 17.1 %collective-permute-start.2 = (f32[168,256]{1,0:T(8,128)S(1)}, f32[168,256]{1,0:T(8,128)S(1)}, u32[]{:S(2)}, u32[]{:S(2)}) collective-permute-start(f32[168,256]{1,0:T(8,128)S(1)} %get-tuple-element.18), channel_id=1, source_target_pairs={{0,1},{1,0},{2,3},{3,2},{4,5},{5,4},{6,7},{7,6},{8,9},{9,8},{10,11... | collective-permute-start | bytes 516104 | tf_op jit(solution)/shard_map/ppermute | solution.py:592
  2.7 16.4 %collective-permute-start.3 = (f32[168,256]{1,0:T(8,128)S(1)}, f32[168,256]{1,0:T(8,128)S(1)}, u32[]{:S(2)}, u32[]{:S(2)}) collective-permute-start(f32[168,256]{1,0:T(8,128)S(1)} %get-tuple-element.19), channel_id=1, source_target_pairs={{1,2},{2,1},{3,4},{4,3},{5,6},{6,5},{7,8},{8,7},{9,10},{10,9},{11,... | collective-permute-start | bytes 516104 | tf_op jit(solution)/shard_map/ppermute | solution.py:593
  9.9 15.3 %collective-permute-start = (f32[160,256]{1,0:T(8,128)S(1)}, f32[160,256]{1,0:T(8,128)S(1)}, u32[]{:S(2)}, u32[]{:S(2)}) collective-permute-start(f32[160,256]{1,0:T(8,128)S(1)} %get-tuple-element.16), channel_id=1, source_target_pairs={{16,32},{32,16},{48,64},{64,48},{80,96},{96,80},{112,128},{128,112... | collective-permute-start | bytes 491528 | tf_op jit(solution)/shard_map/ppermute | solution.py:594
  11.8 13.4 %collective-permute-start.1 = (f32[160,256]{1,0:T(8,128)S(1)}, f32[160,256]{1,0:T(8,128)S(1)}, u32[]{:S(2)}, u32[]{:S(2)}) collective-permute-start(f32[160,256]{1,0:T(8,128)S(1)} %get-tuple-element.17), channel_id=1, source_target_pairs={{0,16},{16,0},{32,48},{48,32},{64,80},{80,64},{96,112},{112,96},{1... | collective-permute-start | bytes 491528 | tf_op jit(solution)/shard_map/ppermute | solution.py:595
  19.2 6.1 %collective-permute-start.4 = (f32[56,256]{1,0:T(8,128)S(1)}, f32[56,256]{1,0:T(8,128)S(1)}, u32[]{:S(2)}, u32[]{:S(2)}) collective-permute-start(f32[56,256]{1,0:T(8,128)S(1)} %get-tuple-element.21), channel_id=1, source_target_pairs={{16,32},{32,16},{48,64},{64,48},{80,96},{96,80},{112,128},{128,112... | collective-permute-start | bytes 172040 | tf_op jit(solution)/shard_map/ppermute | solution.py:603
  21.1 4.1 %collective-permute-start.5 = (f32[56,256]{1,0:T(8,128)S(1)}, f32[56,256]{1,0:T(8,128)S(1)}, u32[]{:S(2)}, u32[]{:S(2)}) collective-permute-start(f32[56,256]{1,0:T(8,128)S(1)} %get-tuple-element.22), channel_id=1, source_target_pairs={{0,16},{16,0},{32,48},{48,32},{64,80},{80,64},{96,112},{112,96},{1... | collective-permute-start | bytes 172040 | tf_op jit(solution)/shard_map/ppermute | solution.py:604

commit v13 on v10

--- a/solution.py
+++ b/solution.py
@@ -265,6 +265,8 @@
     next_ref,
     last_ref,
     picked_ref,
+    left_ref,
+    right_ref,
     cell_ref,
     value_ref,
     weight_ref,
@@ -346,17 +348,23 @@
         east_flow, north_flow = advance_flow(after, last_height, turning, x)
         for field, plane in enumerate((last_height(x), east_flow, north_flow)):
             at = (field * lon + x - REACH) * TILE
-            forecast_ref[at : at + TILE] = plane[REACH : REACH + TILE]
+            tile = plane[REACH : REACH + TILE]
+            forecast_ref[at : at + TILE] = tile
+            left_ref[at : at + TILE], right_ref[at : at + TILE] = tile[:, :128], tile[:, 128:]
     for field in range(len(LAT_ROWS)):
         for x in range(REACH, lon - REACH):
             at = (field * lon + x) * TILE
-            forecast_ref[at : at + TILE] = inner_ref[field, x - REACH]
+            tile = inner_ref[field, x - REACH]
+            forecast_ref[at : at + TILE] = tile
+            left_ref[at : at + TILE], right_ref[at : at + TILE] = tile[:, :128], tile[:, 128:]
 
     for copy in copies:
         copy.wait()
     count = picked_ref.shape[0]
     for k in range(count):
-        picked_ref[k : k + 1] = forecast_ref[pl.ds(cell_ref[0, 0, k], 1)]
+        cell = cell_ref[0, 0, k]
+        picked_ref[k : k + 1, :128] = left_ref[pl.ds(cell, 1)]
+        picked_ref[k : k + 1, 128:] = right_ref[pl.ds(cell, 1)]
     picked = picked_ref[...]
     ymean = jnp.sum(picked, axis=1, keepdims=True) * (1.0 / members)
     half = members // 2
@@ -617,6 +625,8 @@
             pltpu.VMEM(planes, jnp.float32),
             pltpu.VMEM((1,) + planes[1:], jnp.float32),
             pltpu.VMEM((obs_cell.shape[2], members), jnp.float32),
+            pltpu.VMEM((fields * lon * lat, members // 2), jnp.float32),
+            pltpu.VMEM((fields * lon * lat, members // 2), jnp.float32),
             pltpu.SMEM(obs_cell.shape, jnp.int32),
         ]
         + [pltpu.VMEM(obs_value.shape, jnp.float32)] * 2

time: 86.1 us -> 86 us (level)
  no operation moved by 1% of the time
where the time goes in v13:
time: 86 us; the launch traced here: 85.7 us
  blocking collectives  54.7 us (64%)
  starting transfers between devices  17.8 us (21%)
  Pallas kernels  8.12 us (9%)
  waiting for transfers between devices  3.85 us (4%)
    all_to_all x1, blocking collectives, reduced(): lax.all_to_all(jnp.broadcast_to(piece[None], (lat, 1, width)), 'lat', 0, 0)  28 us
    all_to_all x1, blocking collectives, reduced(): pieces = lax.all_to_all(packed.reshape(lon, 1, width), 'lon', 0, 0)  13.8 us
    all_to_all x1, blocking collectives, reduced(): lax.all_to_all(jnp.broadcast_to(piece[None], (lon, 1, width)), 'lon', 0, 0)  12.9 us
    ppermute x1, starting transfers between devices, local(): second = lax.ppermute(second, ('lon', 'lat'), pairs[1])  7.24 us
    ppermute x1, starting transfers between devices, local(): within = lax.ppermute(out_within, 'lon', within)  6.04 us
    pallas_call x1, Pallas kernels, finish(): on_core(finish_kernel, (state.shape, square), [pltpu.VMEM] * 2, [pltpu.VM...  4.44 us
    ppermute x1, waiting for transfers between devices, local(): across = lax.ppermute(out_across, 'lon', across)  2.64 us
    ppermute x1, starting transfers between devices, local(): ahead = lax.ppermute(ahead, 'lon', across)  1.92 us
  transfers between devices with their start and end apart: 5, of which 2 were waited for; matrix products, arithmetic and copies ran while one was open for 0% of the time, Pallas kernels for 1%

profile of v13, /device:TPU:1, one launch (start us, length us, event | category | flops | bytes accessed | tf_op | source)
XLA Modules:
  0.0 85.7 jit_solution(13669619347489819225)
XLA Ops:
  0.6 0.0 copy-start
  0.6 1.3 %shard_map.68 = (f32[168,256]{1,0:T(8,128)S(1)}, f32[168,256]{1,0:T(8,128)S(1)}, f32[160,256]{1,0:T(8,128)S(1)}, f32[16,128]{1,0:T(8,128)S(1)}) custom-call(s32[1]{0:T(128)} %bitcast.parity_ref, f32[3,16,16,256]{3,2,1,0:T(8,128)} %state_ref.3, s32[16,16]{1,0:T(8,128)} %bathymetry_ref.1), custom_call_target="tpu_custom_call" | custom-call | tf_op jit(solution)/shard_map/pallas_call | solution.py:578
  2.0 0.7 collective-permute-start.1
  2.7 7.2 %collective-permute-start.2 = (f32[168,256]{1,0:T(8,128)S(1)}, f32[168,256]{1,0:T(8,128)S(1)}, u32[]{:S(2)}, u32[]{:S(2)}) collective-permute-start(f32[168,256]{1,0:T(8,128)S(1)} %get-tuple-element.17), channel_id=1, source_target_pairs={{1,2},{2,1},{3,4},{4,3},{5,6},{6,5},{7,8},{8,7},{9,10},{10,9},{11,... | collective-permute-start | bytes 516104 | tf_op jit(solution)/shard_map/ppermute | solution.py:600
  9.9 1.9 %collective-permute-start = (f32[160,256]{1,0:T(8,128)S(1)}, f32[160,256]{1,0:T(8,128)S(1)}, u32[]{:S(2)}, u32[]{:S(2)}) collective-permute-start(f32[160,256]{1,0:T(8,128)S(1)} %get-tuple-element.15), channel_id=1, source_target_pairs={{16,32},{32,16},{48,64},{64,48},{80,96},{96,80},{112,128},{128,112... | collective-permute-start | bytes 491528 | tf_op jit(solution)/shard_map/ppermute | solution.py:601
  11.8 0.0 collective-permute-done.1.first_ref
  11.8 1.2 %collective-permute-done.2.second_ref = f32[168,256]{1,0:T(8,128)S(1)} collective-permute-done((f32[168,256]{1,0:T(8,128)S(1)}, f32[168,256]{1,0:T(8,128)S(1)}, u32[]{:S(2)}, u32[]{:S(2)}) %collective-permute-start.2) | collective-permute-done | bytes 172064 | tf_op jit(solution)/shard_map/ppermute | solution.py:600
  13.1 0.0 copy-done
  13.1 0.1 shard_map.69
  13.1 6.0 %collective-permute-start.4 = (f32[216,256]{1,0:T(8,128)S(1)}, f32[216,256]{1,0:T(8,128)S(1)}, u32[]{:S(2)}, u32[]{:S(2)}) collective-permute-start(f32[216,256]{1,0:T(8,128)S(1)} %get-tuple-element.20), channel_id=1, source_target_pairs={{0,16},{16,0},{32,48},{48,32},{64,80},{80,64},{96,112},{112,96},{1... | collective-permute-start | bytes 663560 | tf_op jit(solution)/shard_map/ppermute | solution.py:610
  19.2 1.9 %collective-permute-start.3 = (f32[56,256]{1,0:T(8,128)S(1)}, f32[56,256]{1,0:T(8,128)S(1)}, u32[]{:S(2)}, u32[]{:S(2)}) collective-permute-start(f32[56,256]{1,0:T(8,128)S(1)} %get-tuple-element.19), channel_id=1, source_target_pairs={{16,32},{32,16},{48,64},{64,48},{80,96},{96,80},{112,128},{128,112... | collective-permute-start | bytes 172040 | tf_op jit(solution)/shard_map/ppermute | solution.py:609
  21.1 0.1 iota.9.turning_ref
  21.2 0.1 iota.10.inside_ref
  21.3 0.8 shard_map.70
  22.0 0.0 collective-permute-done.ahead_ref
  22.0 2.6 %collective-permute-done.3.across_ref = f32[56,256]{1,0:T(8,128)S(1)} collective-permute-done((f32[56,256]{1,0:T(8,128)S(1)}, f32[56,256]{1,0:T(8,128)S(1)}, u32[]{:S(2)}, u32[]{:S(2)}) %collective-permute-start.3) | collective-permute-done | bytes 57376 | tf_op jit(solution)/shard_map/ppermute | solution.py:609
  24.7 0.0 collective-permute-done.4.within_ref
  24.7 1.5 %shard_map.71 = (f32[768,256]{1,0:T(8,128)S(1)}, f32[288,128]{1,0:T(8,128)S(1)}) custom-call(s32[1]{0:T(128)} %bitcast.parity_ref, f32[160,256]{1,0:T(8,128)S(1)} %collective-permute-done.ahead_ref, f32[56,256]{1,0:T(8,128)S(1)} %collective-permute-done.3.across_ref, f32[216,256]{1,0:T(8,128)S(1)} %collective-permute-done.4.within_ref, ...), custom_call_target="tpu_custom_call" | custom-call | tf_op jit(solution)/shard_map/pallas_call | solution.py:619
  26.2 13.8 %all_to_all.15 = f32[32,1,1152]{2,1,0:T(1,128)S(1)} all-to-all(f32[32,1,1152]{2,1,0:T(1,128)S(1)} %bitcast.5), channel_id=1, replica_groups=mesh['lon'=32,'lat'=16] {'lon'}, dimensions={0} | all-to-all | bytes 294912 | tf_op jit(solution)/shard_map/all_to_all | solution.py:557
  40.1 0.1 reduce_sum.18
  40.2 28.0 %all_to_all.16 = f32[16,1,1152]{2,1,0:T(1,128)S(1)} all-to-all(f32[16,1,1152]{2,1,0:T(1,128)S(1)} %broadcast_in_dim.4), channel_id=1, replica_groups=mesh['lon'=32,'lat'=16] {'lat'}, dimensions={0} | all-to-all | bytes 147456 | tf_op jit(solution)/shard_map/all_to_all | solution.py:559
  68.2 0.1 reduce_sum.19
  68.2 0.1 broadcast_in_dim.5
  68.3 12.9 %all_to_all.17 = f32[32,1,1152]{2,1,0:T(1,128)S(1)} all-to-all(f32[32,1,1152]{2,1,0:T(1,128)S(1)} %broadcast_in_dim.5), channel_id=1, replica_groups=mesh['lon'=32,'lat'=16] {'lon'}, dimensions={0} | all-to-all | bytes 294912 | tf_op jit(solution)/shard_map/all_to_all | solution.py:561
  81.2 4.4 %shard_map.72 = (f32[768,256]{1,0:T(8,128)}, f32[256,256]{1,0:T(8,128)}) custom-call(f32[288,128]{1,0:T(8,128)S(1)} %bitcast.4, f32[768,256]{1,0:T(8,128)S(1)} %get-tuple-element.25.state_ref), custom_call_target="tpu_custom_call" | custom-call | tf_op jit(solution)/shard_map/pallas_call | solution.py:536
  (3 shorter events, 0.1 us)
Async XLA Ops:
  0.6 12.4 %copy-start = (f32[3,16,16,256]{3,2,1,0:T(8,128)S(1)}, f32[3,16,16,256]{3,2,1,0:T(8,128)}, u32[]{:S(2)}) copy-start(f32[3,16,16,256]{3,2,1,0:T(8,128)} %state_ref.3) | copy-start | bytes 2359300
  2.0 9.9 %collective-permute-start.1 = (f32[168,256]{1,0:T(8,128)S(1)}, f32[168,256]{1,0:T(8,128)S(1)}, u32[]{:S(2)}, u32[]{:S(2)}) collective-permute-start(f32[168,256]{1,0:T(8,128)S(1)} %get-tuple-element.16), channel_id=1, source_target_pairs={{0,1},{1,0},{2,3},{3,2},{4,5},{5,4},{6,7},{7,6},{8,9},{9,8},{10,11... | collective-permute-start | bytes 516104 | tf_op jit(solution)/shard_map/ppermute | solution.py:599
  2.7 10.4 %collective-permute-start.2 = (f32[168,256]{1,0:T(8,128)S(1)}, f32[168,256]{1,0:T(8,128)S(1)}, u32[]{:S(2)}, u32[]{:S(2)}) collective-permute-start(f32[168,256]{1,0:T(8,128)S(1)} %get-tuple-element.17), channel_id=1, source_target_pairs={{1,2},{2,1},{3,4},{4,3},{5,6},{6,5},{7,8},{8,7},{9,10},{10,9},{11,... | collective-permute-start | bytes 516104 | tf_op jit(solution)/shard_map/ppermute | solution.py:600
  9.9 12.1 %collective-permute-start = (f32[160,256]{1,0:T(8,128)S(1)}, f32[160,256]{1,0:T(8,128)S(1)}, u32[]{:S(2)}, u32[]{:S(2)}) collective-permute-start(f32[160,256]{1,0:T(8,128)S(1)} %get-tuple-element.15), channel_id=1, source_target_pairs={{16,32},{32,16},{48,64},{64,48},{80,96},{96,80},{112,128},{128,112... | collective-permute-start | bytes 491528 | tf_op jit(solution)/shard_map/ppermute | solution.py:601
  13.1 11.6 %collective-permute-start.4 = (f32[216,256]{1,0:T(8,128)S(1)}, f32[216,256]{1,0:T(8,128)S(1)}, u32[]{:S(2)}, u32[]{:S(2)}) collective-permute-start(f32[216,256]{1,0:T(8,128)S(1)} %get-tuple-element.20), channel_id=1, source_target_pairs={{0,16},{16,0},{32,48},{48,32},{64,80},{80,64},{96,112},{112,96},{1... | collective-permute-start | bytes 663560 | tf_op jit(solution)/shard_map/ppermute | solution.py:610
  19.2 5.5 %collective-permute-start.3 = (f32[56,256]{1,0:T(8,128)S(1)}, f32[56,256]{1,0:T(8,128)S(1)}, u32[]{:S(2)}, u32[]{:S(2)}) collective-permute-start(f32[56,256]{1,0:T(8,128)S(1)} %get-tuple-element.19), channel_id=1, source_target_pairs={{16,32},{32,16},{48,64},{64,48},{80,96},{96,80},{112,128},{128,112... | collective-permute-start | bytes 172040 | tf_op jit(solution)/shard_map/ppermute | solution.py:609
